TPU v7x, 32 devices: a whole 2x2x4 slice. The times are simulated.
32 devices in a mesh: rep: 2 (over core), fsdp: 2 (over y), seq: 8 (over z, x).
Axes of the slice: x: 2, y: 2, z: 4, core: 2. Of those that a mesh axis runs over, the one named last changes fastest.
Arguments:
- hidden_states: bfloat16 [4, 2048, 1024], P(('rep', 'fsdp'), 'seq'), may hold values from -6 to 6
- unit_order: int32 [4, 16], P(('rep', 'fsdp')), may hold values from 0 to 15, each once within a row
- piece_starts: int32 [4, 2], P(('rep', 'fsdp')), may hold values from 0 to 1792, as said below
- first_gain: bfloat16 [1024], P('fsdp'), may hold values from 0.5 to 1.5
- first_shift: bfloat16 [1024], P('fsdp'), may hold values from -1 to 1
- second_gain: bfloat16 [1024], P('fsdp'), may hold values from 0.5 to 1.5
- second_shift: bfloat16 [1024], P('fsdp'), may hold values from -1 to 1
- merged_weight: bfloat16 [1024, 3072], P('fsdp'), may hold values from -0.1875 to 0.1875
- merged_bias: bfloat16 [3072], P('fsdp'), may hold values from -1 to 1
- output_weight: bfloat16 [1024, 1024], P('fsdp'), may hold values from -0.5 to 0.5
- output_bias: bfloat16 [1024], P('fsdp'), may hold values from -1 to 1
- expand_weight: bfloat16 [1024, 4096], P('fsdp'), may hold values from -0.1875 to 0.1875
- expand_bias: bfloat16 [4096], P('fsdp'), may hold values from -1 to 1
- contract_weight: bfloat16 [4096, 1024], P('fsdp'), may hold values from -0.09375 to 0.09375
- contract_bias: bfloat16 [1024], P('fsdp'), may hold values from -1 to 1
- out_cotangent: bfloat16 [4, 2048, 1024], P(('rep', 'fsdp'), 'seq'), may hold values from -6 to 6
Outputs:
- hidden_output: bfloat16 [4, 2048, 1024], P(('rep', 'fsdp'), 'seq')
- input_gradient: float32 [4, 2048, 1024], P(('rep', 'fsdp'), 'seq')
- first_gain_gradient: float32 [1024], P('fsdp')
- first_shift_gradient: float32 [1024], P('fsdp')
- second_gain_gradient: float32 [1024], P('fsdp')
- second_shift_gradient: float32 [1024], P('fsdp')
- merged_weight_gradient: float32 [1024, 3072], P('fsdp')
- merged_bias_gradient: float32 [3072], P('fsdp')
- output_weight_gradient: float32 [1024, 1024], P('fsdp')
- output_bias_gradient: float32 [1024], P('fsdp')
- expand_weight_gradient: float32 [1024, 4096], P('fsdp')
- expand_bias_gradient: float32 [4096], P('fsdp')
- contract_weight_gradient: float32 [4096, 1024], P('fsdp')
- contract_bias_gradient: float32 [1024], P('fsdp')
Inputs may be any that keep to these rules, and one draw needn't show every extreme that they name: `piece_starts`: piece p of a sequence starts at (8 p + k) * 128 for some k from 0 to 6, so pieces lie in order and never intersection (two may be adjacent); some sequence's first piece starts at 0 and some sequence's last piece ends at the sequence's end. Each sequence's row of unit_order names every unit of positions once.
All inputs are finite; a program needn't handle non-finite values.
Results may differ from a plain program's by a relative error of at most 0.012.
Values may be sent and summed in bfloat16 or wider, within the bound.
A program may use at most 384 MiB of HBM per device.

v0:
```python
import math

import jax
import jax.numpy as jnp
from jax import lax
from jax.sharding import PartitionSpec as P

HEAD = 64
ROT = 16
UNIT = 128
PIECE = 256


EPS = 1e-05
NEGATIVE = -1e30


def norm_rows(values, gain, shift):
    mean = jnp.mean(values, axis=-1, keepdims=True)
    centred = values - mean
    spread = jnp.mean(centred * centred, axis=-1, keepdims=True)
    return centred * lax.rsqrt(spread + EPS) * gain + shift


def gelu_exact(values):
    return jax.nn.gelu(values, approximate=False)


def rotary_tables(positions):
    index = jnp.arange(ROT // 2, dtype=jnp.float32)
    inverse = jnp.exp(index * (-2.0 * math.log(10000.0) / ROT))
    angles = positions.astype(jnp.float32)[:, None] * inverse[None, :]
    angles = jnp.concatenate([angles, angles], axis=1)
    return (jnp.cos(angles), jnp.sin(angles))


def rotate(values, cosine, sine):
    part = values[..., :ROT]
    turned = jnp.concatenate([-part[..., ROT // 2 :], part[..., : ROT // 2]], axis=-1)
    moved = part * cosine[:, None, :] + turned * sine[:, None, :]
    return jnp.concatenate([moved, values[..., ROT:]], axis=-1)


def unit_positions(order):
    offsets = jnp.arange(UNIT, dtype=jnp.int32)
    return (order[:, None] * UNIT + offsets[None, :]).reshape(-1)


def piece_labels(positions, starts):
    inside = (positions[:, None] >= starts[None, :]) & (
        positions[:, None] < starts[None, :] + PIECE
    )
    labels = jnp.arange(1, starts.shape[0] + 1, dtype=jnp.int32)
    return jnp.sum(jnp.where(inside, labels[None, :], 0), axis=1) - 1


def visible(row_pos, row_lab, col_pos, col_lab):
    earlier = col_pos[None, :] <= row_pos[:, None]
    same = (row_lab[:, None] == col_lab[None, :]) & (row_lab[:, None] >= 0)
    return earlier | same


def merged_parts(first, merged_weight, merged_bias, cosine, sine):
    tokens = first.shape[0]
    width = first.shape[1]
    heads = width // HEAD
    merged = jnp.dot(first, merged_weight, preferred_element_type=jnp.float32) + merged_bias.astype(
        jnp.float32
    )
    queries = rotate(merged[:, :width].reshape(tokens, heads, HEAD), cosine, sine).astype(
        jnp.bfloat16
    )
    keys = rotate(merged[:, width : 2 * width].reshape(tokens, heads, HEAD), cosine, sine)
    keys = keys.reshape(tokens, width).astype(jnp.bfloat16)
    values = merged[:, 2 * width :].astype(jnp.bfloat16)
    return (queries, keys, values)


def block_view(queries, keys_all, values_all, row_pos, row_lab, col_pos, col_lab, span):
    heads = queries.shape[1]
    scale = 1.0 / math.sqrt(HEAD)

    def view(index):
        start = index * span
        key_rows = lax.dynamic_slice_in_dim(keys_all, start, span, 0).reshape(span, heads, HEAD)
        value_rows = lax.dynamic_slice_in_dim(values_all, start, span, 0).reshape(span, heads, HEAD)
        scores = (
            jnp.einsum("thd,khd->htk", queries, key_rows, preferred_element_type=jnp.float32)
            * scale
        )
        allowed = visible(
            row_pos,
            row_lab,
            lax.dynamic_slice_in_dim(col_pos, start, span, 0),
            lax.dynamic_slice_in_dim(col_lab, start, span, 0),
        )[None]
        return (scores, allowed, key_rows, value_rows)

    return view


def log_sums(view, count, heads, tokens):

    def log_step(carry, index):
        top, total = carry
        scores, allowed, key_rows, value_rows = view(index)
        masked = jnp.where(allowed, scores, NEGATIVE)
        newer = jnp.maximum(top, jnp.max(masked, axis=-1))
        terms = jnp.where(allowed, jnp.exp(masked - newer[..., None]), 0.0)
        total = total * jnp.exp(top - newer) + jnp.sum(terms, axis=-1)
        return ((newer, total), None)

    begin = (
        jnp.full((heads, tokens), NEGATIVE, jnp.float32),
        jnp.zeros((heads, tokens), jnp.float32),
    )
    (top, total), unused = lax.scan(log_step, begin, jnp.arange(count, dtype=jnp.int32))
    return top + jnp.log(total)


def mix_values(view, count, logsum, heads, tokens, grad_rows):

    def mix_step(carry, index):
        mixed, delta = carry
        scores, allowed, key_rows, value_rows = view(index)
        weights = jnp.where(allowed, jnp.exp(scores - logsum[..., None]), 0.0)
        mixed = mixed + jnp.einsum(
            "htk,khd->thd",
            weights.astype(jnp.bfloat16),
            value_rows,
            preferred_element_type=jnp.float32,
        )
        if grad_rows is not None:
            slopes = jnp.einsum(
                "thd,khd->htk", grad_rows, value_rows, preferred_element_type=jnp.float32
            )
            delta = delta + jnp.sum(weights * slopes, axis=-1)
        return ((mixed, delta), None)

    begin = (jnp.zeros((tokens, heads, HEAD), jnp.float32), jnp.zeros((heads, tokens), jnp.float32))
    (mixed, delta), unused = lax.scan(mix_step, begin, jnp.arange(count, dtype=jnp.int32))
    return (mixed, delta)


def attend_back(view, count, logsum, delta, grad_rows, queries):
    scale = 1.0 / math.sqrt(HEAD)

    def attend_step(carry, index):
        scores, allowed, key_rows, value_rows = view(index)
        weights = jnp.where(allowed, jnp.exp(scores - logsum[..., None]), 0.0)
        slopes = jnp.einsum(
            "thd,khd->htk", grad_rows, value_rows, preferred_element_type=jnp.float32
        )
        grad_scores = (weights * (slopes - delta[..., None])).astype(jnp.bfloat16)
        carry = carry + jnp.einsum(
            "htk,khd->thd", grad_scores, key_rows, preferred_element_type=jnp.float32
        )
        key_grad = jnp.einsum(
            "htk,thd->khd", grad_scores, queries, preferred_element_type=jnp.float32
        )
        value_grad = jnp.einsum(
            "htk,thd->khd",
            weights.astype(jnp.bfloat16),
            grad_rows,
            preferred_element_type=jnp.float32,
        )
        span = key_rows.shape[0]
        joined = jnp.concatenate(
            [key_grad.reshape(span, -1) * scale, value_grad.reshape(span, -1)], axis=1
        )
        return (carry, joined)

    begin = jnp.zeros(queries.shape, jnp.float32)
    grad_query, parts = lax.scan(attend_step, begin, jnp.arange(count, dtype=jnp.int32))
    return (grad_query * scale, parts)


def body(
    hidden_states,
    unit_order,
    piece_starts,
    first_gain,
    first_shift,
    second_gain,
    second_shift,
    merged_weight,
    merged_bias,
    output_weight,
    output_bias,
    expand_weight,
    expand_bias,
    contract_weight,
    contract_bias,
    out_cotangent,
):
    shards = (
        first_gain,
        first_shift,
        second_gain,
        second_shift,
        merged_weight,
        merged_bias,
        output_weight,
        output_bias,
        expand_weight,
        expand_bias,
        contract_weight,
        contract_bias,
    )
    gathered = (
        lax.all_gather(shards[0], "fsdp", axis=0, tiled=True),
        lax.all_gather(shards[1], "fsdp", axis=0, tiled=True),
        lax.all_gather(shards[2], "fsdp", axis=0, tiled=True),
        lax.all_gather(shards[3], "fsdp", axis=0, tiled=True),
        lax.all_gather(shards[4], "fsdp", axis=0, tiled=True),
        lax.all_gather(shards[5], "fsdp", axis=0, tiled=True),
        lax.all_gather(shards[6], "fsdp", axis=0, tiled=True),
        lax.all_gather(shards[7], "fsdp", axis=0, tiled=True),
        lax.all_gather(shards[8], "fsdp", axis=0, tiled=True),
        lax.all_gather(shards[9], "fsdp", axis=0, tiled=True),
        lax.all_gather(shards[10], "fsdp", axis=0, tiled=True),
        lax.all_gather(shards[11], "fsdp", axis=0, tiled=True),
    )
    hidden = hidden_states[0].astype(jnp.float32)
    tokens = hidden.shape[0]
    width = hidden.shape[1]
    heads = width // HEAD
    length = tokens * lax.axis_size("seq")
    span = min(length, 512)
    count = length // span
    col_pos = unit_positions(unit_order[0])
    col_lab = piece_labels(col_pos, piece_starts[0])
    offset = lax.axis_index("seq") * tokens
    row_pos = lax.dynamic_slice_in_dim(col_pos, offset, tokens, 0)
    row_lab = lax.dynamic_slice_in_dim(col_lab, offset, tokens, 0)
    cosine, sine = rotary_tables(row_pos)
    first = norm_rows(
        hidden, gathered[0].astype(jnp.float32), gathered[1].astype(jnp.float32)
    ).astype(jnp.bfloat16)
    queries, keys, values = merged_parts(first, gathered[4], gathered[5], cosine, sine)
    keys_all, values_all = (
        lax.all_gather(keys, "seq", axis=0, tiled=True),
        lax.all_gather(values, "seq", axis=0, tiled=True),
    )
    view = block_view(queries, keys_all, values_all, row_pos, row_lab, col_pos, col_lab, span)
    logsum = log_sums(view, count, heads, tokens)
    mixed, unused = mix_values(view, count, logsum, heads, tokens, None)
    mixed = mixed.reshape(tokens, width).astype(jnp.bfloat16)
    attention = jnp.dot(mixed, gathered[6], preferred_element_type=jnp.float32) + gathered[
        7
    ].astype(jnp.float32)
    second = norm_rows(
        hidden, gathered[2].astype(jnp.float32), gathered[3].astype(jnp.float32)
    ).astype(jnp.bfloat16)
    expanded = jnp.dot(second, gathered[8], preferred_element_type=jnp.float32) + gathered[
        9
    ].astype(jnp.float32)
    active = gelu_exact(expanded).astype(jnp.bfloat16)
    feed = jnp.dot(active, gathered[10], preferred_element_type=jnp.float32) + gathered[11].astype(
        jnp.float32
    )
    output = (hidden + attention + feed).astype(jnp.bfloat16)
    weights = (
        lax.all_gather(shards[0], "fsdp", axis=0, tiled=True),
        lax.all_gather(shards[1], "fsdp", axis=0, tiled=True),
        lax.all_gather(shards[2], "fsdp", axis=0, tiled=True),
        lax.all_gather(shards[3], "fsdp", axis=0, tiled=True),
        lax.all_gather(shards[4], "fsdp", axis=0, tiled=True),
        lax.all_gather(shards[5], "fsdp", axis=0, tiled=True),
        lax.all_gather(shards[6], "fsdp", axis=0, tiled=True),
        lax.all_gather(shards[7], "fsdp", axis=0, tiled=True),
        lax.all_gather(shards[8], "fsdp", axis=0, tiled=True),
        lax.all_gather(shards[9], "fsdp", axis=0, tiled=True),
        lax.all_gather(shards[10], "fsdp", axis=0, tiled=True),
        lax.all_gather(shards[11], "fsdp", axis=0, tiled=True),
    )
    cotangent = out_cotangent[0]
    upstream = cotangent.astype(jnp.float32)
    normed_one, first_pull = jax.vjp(
        norm_rows, hidden, weights[0].astype(jnp.float32), weights[1].astype(jnp.float32)
    )
    first = normed_one.astype(jnp.bfloat16)
    queries, keys, values = merged_parts(first, weights[4], weights[5], cosine, sine)
    keys_back, values_back = (
        lax.all_gather(keys, "seq", axis=0, tiled=True),
        lax.all_gather(values, "seq", axis=0, tiled=True),
    )
    view = block_view(queries, keys_back, values_back, row_pos, row_lab, col_pos, col_lab, span)
    grad_mixed = jnp.einsum(
        "te,de->td", cotangent, weights[6], preferred_element_type=jnp.float32
    ).astype(jnp.bfloat16)
    grad_rows = grad_mixed.reshape(tokens, heads, HEAD)
    mixed, delta = mix_values(view, count, logsum, heads, tokens, grad_rows)
    mixed = mixed.reshape(tokens, width).astype(jnp.bfloat16)
    grad_query, parts = attend_back(view, count, logsum, delta, grad_rows, queries)
    term = parts.reshape(length, 2 * width)
    own_grads = lax.psum_scatter(
        term.astype(jnp.bfloat16), "seq", scatter_dimension=0, tiled=True
    ).astype(jnp.float32)
    normed_two, second_pull = jax.vjp(
        norm_rows, hidden, weights[2].astype(jnp.float32), weights[3].astype(jnp.float32)
    )
    second = normed_two.astype(jnp.bfloat16)
    expanded = jnp.dot(second, weights[8], preferred_element_type=jnp.float32) + weights[9].astype(
        jnp.float32
    )
    activated, gelu_pull = jax.vjp(gelu_exact, expanded)
    active = activated.astype(jnp.bfloat16)
    grad_active = jnp.einsum(
        "te,fe->tf", cotangent, weights[10], preferred_element_type=jnp.float32
    )
    grad_expanded = gelu_pull(grad_active)[0].astype(jnp.bfloat16)
    grad_second = jnp.einsum(
        "tf,df->td", grad_expanded, weights[8], preferred_element_type=jnp.float32
    )
    unused, turn_pull = jax.vjp(rotate, grad_query, cosine, sine)
    query_back = turn_pull(grad_query)[0].reshape(tokens, width)
    key_back = turn_pull(own_grads[:, :width].reshape(tokens, heads, HEAD))[0].reshape(
        tokens, width
    )
    grad_merged = jnp.concatenate([query_back, key_back, own_grads[:, width:]], axis=1).astype(
        jnp.bfloat16
    )
    grad_first = jnp.einsum(
        "tc,dc->td", grad_merged, weights[4], preferred_element_type=jnp.float32
    )
    first_term, first_gain_grad, first_shift_grad = first_pull(grad_first)
    second_term, second_gain_grad, second_shift_grad = second_pull(grad_second)
    input_gradient = upstream + first_term + second_term
    row_total = jnp.sum(upstream, axis=0)
    local_grads = (
        first_gain_grad,
        first_shift_grad,
        second_gain_grad,
        second_shift_grad,
        jnp.einsum("td,tc->dc", first, grad_merged, preferred_element_type=jnp.float32),
        jnp.sum(grad_merged.astype(jnp.float32), axis=0),
        jnp.einsum("td,te->de", mixed, cotangent, preferred_element_type=jnp.float32),
        row_total,
        jnp.einsum("td,tf->df", second, grad_expanded, preferred_element_type=jnp.float32),
        jnp.sum(grad_expanded.astype(jnp.float32), axis=0),
        jnp.einsum("tf,te->fe", active, cotangent, preferred_element_type=jnp.float32),
        row_total,
    )
    owned = (
        lax.psum_scatter(
            local_grads[0].astype(jnp.bfloat16), "fsdp", scatter_dimension=0, tiled=True
        ).astype(jnp.float32),
        lax.psum_scatter(
            local_grads[1].astype(jnp.bfloat16), "fsdp", scatter_dimension=0, tiled=True
        ).astype(jnp.float32),
        lax.psum_scatter(
            local_grads[2].astype(jnp.bfloat16), "fsdp", scatter_dimension=0, tiled=True
        ).astype(jnp.float32),
        lax.psum_scatter(
            local_grads[3].astype(jnp.bfloat16), "fsdp", scatter_dimension=0, tiled=True
        ).astype(jnp.float32),
        lax.psum_scatter(
            local_grads[4].astype(jnp.bfloat16), "fsdp", scatter_dimension=0, tiled=True
        ).astype(jnp.float32),
        lax.psum_scatter(
            local_grads[5].astype(jnp.bfloat16), "fsdp", scatter_dimension=0, tiled=True
        ).astype(jnp.float32),
        lax.psum_scatter(
            local_grads[6].astype(jnp.bfloat16), "fsdp", scatter_dimension=0, tiled=True
        ).astype(jnp.float32),
        lax.psum_scatter(
            local_grads[7].astype(jnp.bfloat16), "fsdp", scatter_dimension=0, tiled=True
        ).astype(jnp.float32),
        lax.psum_scatter(
            local_grads[8].astype(jnp.bfloat16), "fsdp", scatter_dimension=0, tiled=True
        ).astype(jnp.float32),
        lax.psum_scatter(
            local_grads[9].astype(jnp.bfloat16), "fsdp", scatter_dimension=0, tiled=True
        ).astype(jnp.float32),
        lax.psum_scatter(
            local_grads[10].astype(jnp.bfloat16), "fsdp", scatter_dimension=0, tiled=True
        ).astype(jnp.float32),
        lax.psum_scatter(
            local_grads[11].astype(jnp.bfloat16), "fsdp", scatter_dimension=0, tiled=True
        ).astype(jnp.float32),
    )
    summed = lax.psum(
        (
            owned[0],
            owned[1],
            owned[2],
            owned[3],
            owned[4],
            owned[5],
            owned[6],
            owned[7],
            owned[8],
            owned[9],
            owned[10],
            owned[11],
        ),
        ("rep", "seq"),
    )
    return (
        output[None],
        input_gradient[None],
        summed[0],
        summed[1],
        summed[2],
        summed[3],
        summed[4],
        summed[5],
        summed[6],
        summed[7],
        summed[8],
        summed[9],
        summed[10],
        summed[11],
    )


def solution(mesh):
    in_specs = (
        P(("rep", "fsdp"), "seq", None),
        P(("rep", "fsdp"), None),
        P(("rep", "fsdp"), None),
        P("fsdp"),
        P("fsdp"),
        P("fsdp"),
        P("fsdp"),
        P("fsdp", None),
        P("fsdp"),
        P("fsdp", None),
        P("fsdp"),
        P("fsdp", None),
        P("fsdp"),
        P("fsdp", None),
        P("fsdp"),
        P(("rep", "fsdp"), "seq", None),
    )
    out_specs = (
        P(("rep", "fsdp"), "seq", None),
        P(("rep", "fsdp"), "seq", None),
        P("fsdp"),
        P("fsdp"),
        P("fsdp"),
        P("fsdp"),
        P("fsdp", None),
        P("fsdp"),
        P("fsdp", None),
        P("fsdp"),
        P("fsdp", None),
        P("fsdp"),
        P("fsdp", None),
        P("fsdp"),
    )
    return jax.shard_map(body, mesh=mesh, in_specs=in_specs, out_specs=out_specs, check_vma=False)
```

profile of v0, /device:TPU:0, one launch (start us, length us, event | category | flops | bytes accessed | tf_op | source)
XLA Modules:
  0.0 2002.2 jit_solution(2659681047609094985)
XLA Ops:
  24.2 68.5 %all-gather.14.cloned.1.call-done = bf16[1024,3072]{1,0:T(8,128)(2,1)} async-done(((bf16[512,3072]{1,0:T(8,128)(2,1)}), bf16[1024,3072]{1,0:T(8,128)(2,1)}) %all-gather.14.cloned.1.call-update) | async-done | bytes 6291472 | tf_op jit(solution)/shard_map/all_gather | solution.py:215
  105.8 21.6 %all-gather.20.cloned.1.call-done = bf16[1024,1024]{1,0:T(8,128)(2,1)} async-done(((bf16[512,1024]{1,0:T(8,128)(2,1)}), bf16[1024,1024]{1,0:T(8,128)(2,1)}) %all-gather.20.cloned.1.call-update) | async-done | bytes 2097168 | tf_op jit(solution)/shard_map/all_gather | solution.py:217
  132.7 72.4 %all-gather.18.cloned.1.call-done = bf16[2048,1024]{0,1:T(8,128)(2,1)} async-done(((bf16[256,1024]{0,1:T(8,128)(2,1)}), bf16[2048,1024]{0,1:T(8,128)(2,1)}) %all-gather.18.cloned.1.call-update) | async-done | bytes 4194320 | tf_op jit(solution)/shard_map/all_gather | solution.py:242
  205.1 50.3 %while.50 = (s32[]{:T(128)}, f32[16,256]{1,0:T(8,128)S(1)}, f32[16,256]{1,0:T(8,128)S(1)}, s32[4]{0:T(128)S(1)}, s32[2048]{0:T(1024)S(1)}, /*index=5*/s32[256]{0...) while((s32[]{:T(128)}, f32[16,256]{1,0:T(8,128)S(1)}, ...), condition=%wide.region_6.7_spmd.clone, body=%wide.region_3.6_spmd.clone.sunk | while | flops 285757696 | bytes 21069532 | solution.py:117
  255.4 23.9 %all-gather.16.cloned.1.call-done = bf16[2048,1024]{1,0:T(8,128)(2,1)} async-done(((bf16[256,1024]{1,0:T(8,128)(2,1)}), bf16[2048,1024]{1,0:T(8,128)(2,1)}) %all-gather.16.cloned.1.call-update) | async-done | bytes 4194320 | tf_op jit(solution)/shard_map/all_gather | solution.py:243
  279.3 6.5 copy.87
  285.8 68.0 %while.52 = (s32[]{:T(128)}, f32[256,16,64]{0,2,1:T(8,128)S(1)}, f32[16,256]{1,0:T(8,128)S(1)}, s32[4]{0:T(128)S(1)}, bf16[2048,1024]{0,1:T(8,128)(2,1)}, /*inde...) while((s32[]{:T(128)}, f32[256,16,64]{0,2,1:T(8,128)S(1)}, ...), condition=%wide.region_11.12_spmd.clone, body=%wide.region_9.11_spmd.clone.sunk | while | flops 825233664 | bytes 71810864 | solution.py:141
  294.5 6.2 fusion.185
  354.8 104.4 %while.53 = (s32[]{:T(128)}, f32[256,16,64]{0,2,1:T(8,128)}, bf16[4,512,2048]{2,1,0:T(8,128)(2,1)}, s32[4]{0:T(128)S(1)}, bf16[2048,1024]{0,1:T(8,128)(2,1)}, /*...) while((s32[]{:T(128)}, f32[256,16,64]{0,2,1:T(8,128)}, ...), condition=%wide.region_13.14_spmd.clone, body=%wide.region_12.13_spmd.clone.sunk | while | flops 1369440512 | bytes 116850520 | solution.py:174
  394.4 6.2 fusion.200
  475.4 16.5 multiply_convert_fusion
  491.8 11.5 fusion.100
  504.6 5.9 convolution_convert_fusion.1
  510.8 7.3 convolution_convert_fusion
  520.4 121.3 %reduce-scatter.6.cloned.1.call-done = bf16[256,2048]{1,0:T(8,128)(2,1)} async-done(((bf16[2048,2048]{1,0:T(8,128)(2,1)}), bf16[256,2048]{1,0:T(8,128)(2,1)}) %reduce-scatter.6.cloned.1.call-update) | async-done | bytes 1048592 | tf_op jit(solution)/shard_map/reduce_scatter | solution.py:297
  652.8 5.7 convolution_convert_fusion.2
  670.6 7.5 fusion.103
  678.1 6.7 convolution_add_fusion.3
  684.8 31.2 %while.51 = (s32[]{:T(128)}, f32[256,16,64]{0,2,1:T(8,128)}, s32[4]{0:T(128)S(1)}, bf16[2048,1024]{0,1:T(8,128)(2,1)}, s32[2048]{0:T(1024)S(1)}, /*index=5*/s32[...) while((s32[]{:T(128)}, f32[256,16,64]{0,2,1:T(8,128)}, ...), condition=%wide.region_8.9_spmd.clone, body=%wide.region_7.8_spmd.clone.sunk | while | flops 546308352 | bytes 9207525 | solution.py:141
  720.8 56.3 %reduce-scatter.12.cloned.1.call-done = bf16[512,4096]{1,0:T(8,128)(2,1)} async-done(((bf16[1024,4096]{1,0:T(8,128)(2,1)}), bf16[512,4096]{1,0:T(8,128)(2,1)}) %reduce-scatter.12.cloned.1.call-update) | async-done | bytes 4194320 | tf_op jit(solution)/shard_map/reduce_scatter | solution.py:370
  777.1 101.5 %reduce-scatter.14.cloned.1.call-done = bf16[2048,1024]{1,0:T(8,128)(2,1)} async-done(((bf16[4096,1024]{1,0:T(8,128)(2,1)}), bf16[2048,1024]{1,0:T(8,128)(2,1)}) %reduce-scatter.14.cloned.1.call-update) | async-done | bytes 4194320 | tf_op jit(solution)/shard_map/reduce_scatter | solution.py:376
  886.3 7.6 all-reduce.16
  896.0 63.2 %reduce-scatter.8.cloned.1.call-done = bf16[512,3072]{1,0:T(8,128)(2,1)} async-done(((bf16[1024,3072]{1,0:T(8,128)(2,1)}), bf16[512,3072]{1,0:T(8,128)(2,1)}) %reduce-scatter.8.cloned.1.call-update) | async-done | bytes 3145744 | tf_op jit(solution)/shard_map/reduce_scatter | solution.py:358
  959.1 1035.7 %all-reduce.18 = (f32[512]{0:T(512)}, f32[512]{0:T(512)}, f32[512]{0:T(512)}, f32[512]{0:T(512)}, f32[512,3072]{1,0:T(8,128)}, /*index=5*/f32[1536]{0:T(1024)}, ...) all-reduce(f32[512]{0:T(512)S(1)} %dynamic-slice_convert_fusion.6, ...), channel_id=1, replica_groups=mesh['rep'=2,'fsdp'=2,'seq'=8] {'rep','seq'}, use_global_device_ids=true, to_apply=%region_21.22 | all-reduce | flops 6297600 | bytes 37797888 | tf_op jit(solution)/shard_map/psum | solution.py:383
  (407 shorter events, 322.3 us)
Async XLA Ops:
  7.2 85.5 %all-gather.14.cloned.1.call-start = ((), (), s32[]{:S(2)}) async-start(), calls=%async_computation.5 | async-start | bytes 9437184 | tf_op jit(solution)/shard_map/all_gather | solution.py:215
  8.0 119.4 %all-gather.20.cloned.1.call-start = ((), (), s32[]{:S(2)}) async-start(), calls=%async_computation.8 | async-start | bytes 3145728 | tf_op jit(solution)/shard_map/all_gather | solution.py:217
  8.7 196.4 %all-gather.18.cloned.1.call-start = ((), (), s32[]{:S(2)}) async-start(), calls=%async_computation.7 | async-start | bytes 4718592 | tf_op jit(solution)/shard_map/all_gather | solution.py:242
  18.6 74.1 %copy-start.32 = (f32[2,1,512]{2,1,0:T(1,128)}, f32[2,1,512]{2,1,0:T(1,128)S(1)}, u32[]{:S(2)}) copy-start(f32[2,1,512]{2,1,0:T(1,128)S(1)} %convert_element_type.213) | copy-start | bytes 12292
  23.0 69.7 %copy-start.24 = (f32[2,1,512]{2,1,0:T(1,128)}, f32[2,1,512]{2,1,0:T(1,128)S(1)}, u32[]{:S(2)}) copy-start(f32[2,1,512]{2,1,0:T(1,128)S(1)} %convert_element_type.212) | copy-start | bytes 12292
  23.9 68.8 %copy-start.22 = (f32[256]{0:T(256)}, f32[256]{0:T(256)S(1)}, u32[]{:S(2)}) copy-start(f32[256]{0:T(256)S(1)} %broadcast_multiply_fusion.2) | copy-start | bytes 3076
  24.2 68.5 %copy-start.28 = (f32[256]{0:T(256)}, f32[256]{0:T(256)S(1)}, u32[]{:S(2)}) copy-start(f32[256]{0:T(256)S(1)} %fusion.67) | copy-start | bytes 3076
  24.2 68.5 %copy-start.26 = (f32[256]{0:T(256)}, f32[256]{0:T(256)S(1)}, u32[]{:S(2)}) copy-start(f32[256]{0:T(256)S(1)} %fusion.84) | copy-start | bytes 3076
  101.6 177.7 %all-gather.16.cloned.1.call-start = ((), (), s32[]{:S(2)}) async-start(), calls=%async_computation.6 | async-start | bytes 4718592 | tf_op jit(solution)/shard_map/all_gather | solution.py:243
  103.9 23.6 %copy-start.5 = (bf16[1,256,1024]{2,1,0:T(8,128)(2,1)S(1)}, bf16[1,256,1024]{2,1,0:T(8,128)(2,1)}, u32[]{:S(2)}) copy-start(bf16[1,256,1024]{2,1,0:T(8,128)(2,1)} %param.39) | copy-start | bytes 1572868
  103.9 371.5 %all-gather.22.cloned.1.call-start = ((), (), s32[]{:S(2)}) async-start(), calls=%async_computation.9 | async-start | bytes 12582912 | tf_op jit(solution)/shard_map/all_gather | solution.py:219
  104.5 387.4 %all-gather.24.cloned.1.call-start = ((), (), s32[]{:S(2)}) async-start(), calls=%async_computation.10 | async-start | bytes 12582912 | tf_op jit(solution)/shard_map/all_gather | solution.py:221
  105.0 536.7 %reduce-scatter.6.cloned.1.call-start = ((), (), s32[]{:S(2)}) async-start(), calls=%async_computation.11 | async-start | bytes 9437184 | tf_op jit(solution)/shard_map/reduce_scatter | solution.py:297
  459.2 16.1 copy-start.4
  459.3 16.1 copy-start.23
  459.3 261.6 %reduce-scatter.10.cloned.1.call-start = ((), (), s32[]{:S(2)}) async-start(), calls=%async_computation.13 | async-start | bytes 3145728 | tf_op jit(solution)/shard_map/reduce_scatter | solution.py:364
  475.3 301.9 %reduce-scatter.12.cloned.1.call-start = ((), (), s32[]{:S(2)}) async-start(), calls=%async_computation.14 | async-start | bytes 12582912 | tf_op jit(solution)/shard_map/reduce_scatter | solution.py:370
  510.6 368.1 %reduce-scatter.14.cloned.1.call-start = ((), (), s32[]{:S(2)}) async-start(), calls=%async_computation.15 | async-start | bytes 12582912 | tf_op jit(solution)/shard_map/reduce_scatter | solution.py:376
  518.1 441.1 %reduce-scatter.8.cloned.1.call-start = ((), (), s32[]{:S(2)}) async-start(), calls=%async_computation.12 | async-start | bytes 9437184 | tf_op jit(solution)/shard_map/reduce_scatter | solution.py:358
  519.5 128.4 %copy-start.21 = (f32[256,16]{0,1:T(8,128)S(1)}, f32[256,16]{0,1:T(8,128)}, u32[]{:S(2)}) copy-start(f32[256,16]{0,1:T(8,128)} %get-tuple-element.739) | copy-start | bytes 49156
  520.4 128.6 %copy-start.20 = (f32[256,16]{0,1:T(8,128)S(1)}, f32[256,16]{0,1:T(8,128)}, u32[]{:S(2)}) copy-start(f32[256,16]{0,1:T(8,128)} %get-tuple-element.738) | copy-start | bytes 49156
  716.0 162.7 %copy-start.12 = (bf16[256,1024]{1,0:T(8,128)(2,1)S(1)}, bf16[256,1024]{1,0:T(8,128)(2,1)}, u32[]{:S(2)}) copy-start(bf16[256,1024]{1,0:T(8,128)(2,1)} %copy-done.11) | copy-start | bytes 1572868
  716.0 162.7 %copy-start.14 = (bf16[256,1024]{1,0:T(8,128)(2,1)S(1)}, bf16[256,1024]{1,0:T(8,128)(2,1)}, u32[]{:S(2)}) copy-start(bf16[256,1024]{1,0:T(8,128)(2,1)} %copy-done.13) | copy-start | bytes 1572868
  716.0 164.0 %copy-start.8 = (f32[256,1024]{1,0:T(8,128)S(1)}, f32[256,1024]{1,0:T(8,128)}, u32[]{:S(2)}) copy-start(f32[256,1024]{1,0:T(8,128)} %fusion.103) | copy-start | bytes 3145732
  (46 other events, 266.2 us)
Sparse Core Ops, SparseCore 0:
  9.6 83.0 all-gather.13
  94.3 33.1 all-gather.19
  130.0 75.0 all-gather.17
  207.6 71.5 all-gather.15
  280.6 102.2 all-gather.21
  384.4 104.1 all-gather.23
  492.8 148.8 reduce-scatter.5
  644.0 30.9 reduce-scatter.9
  677.9 99.2 reduce-scatter.11
  779.4 99.2 reduce-scatter.13
  881.5 77.5 reduce-scatter.7
where the time goes:
time: 2010 us; the launch traced here: 2000 us
  blocking collectives  1080 us (54%)
  waiting for transfers between devices  531 us (26%)
  matrix products  237 us (12%)
  local copies, waits for them, and re-layouts  81.2 us (4%)
  other arithmetic  44.6 us (2%)
    psum x1, blocking collectives, body(): lax.psum((owned[0], owned[1], owned[2], owned[3], owned[4], owned[5], own...  1040 us
    reduce_scatter x1, waiting for transfers between devices, body(): lax.psum_scatter(term.astype(jnp.bfloat16), 'seq', scatter_dimension=0, t...  121 us
    reduce_scatter x1, waiting for transfers between devices, body(): lax.psum_scatter(local_grads[10].astype(jnp.bfloat16), 'fsdp', scatter_di...  102 us
    all_gather x1, waiting for transfers between devices, body(): lax.all_gather(keys, 'seq', axis=0, tiled=True)  72.4 us
    all_gather x1, waiting for transfers between devices, body(): lax.all_gather(shards[4], 'fsdp', axis=0, tiled=True)  68.5 us
    reduce_scatter x1, waiting for transfers between devices, body(): lax.psum_scatter(local_grads[4].astype(jnp.bfloat16), 'fsdp', scatter_dim...  63.2 us
    reduce_scatter x1, waiting for transfers between devices, body(): lax.psum_scatter(local_grads[8].astype(jnp.bfloat16), 'fsdp', scatter_dim...  56.3 us
    dot_general x12, matrix products, view(): jnp.einsum('thd,khd->htk', queries, key_rows, preferred_element_type=jnp....  43.8 us
  transfers between devices with their start and end apart: 11, of which 8 were waited for; matrix products, arithmetic and copies ran while one was open for 18% of the time, Pallas kernels for 0%

commit v1 on v0

--- a/solution.py
+++ b/solution.py
@@ -1,8 +1,11 @@
+import functools
 import math
 
 import jax
 import jax.numpy as jnp
 from jax import lax
+from jax.experimental import pallas as pl
+from jax.experimental.pallas import tpu as pltpu
 from jax.sharding import PartitionSpec as P
 
 HEAD = 64
@@ -415,6 +418,704 @@
     )
 
 
+MESH = pl.DeviceIdType.MESH
+GROUP = 4
+HALF = ROT // 2
+SPAN = 512
+
+
+def position_here():
+    return (lax.axis_index("rep"), lax.axis_index("fsdp"), lax.axis_index("seq"))
+
+
+def greet(partners):
+    barrier = pltpu.get_barrier_semaphore()
+    for partner in partners:
+        pl.semaphore_signal(barrier, inc=1, device_id=partner, device_id_type=MESH)
+    pl.semaphore_wait(barrier, len(partners))
+
+
+def exchange_kernel(
+    hid, cot, ints, vec, wm, we, hid_all, cot_all, ints_all, vec_all, wm_all, we_all, send, recv, local
+):
+    c, y, s = position_here()
+    me = 2 * c + y
+    core = (1 - c, y, s)
+    across = (c, 1 - y, s)
+    greet((core, across))
+    head_cols = wm_all.shape[2] // 3
+    width = wm.shape[1] // 3
+    ff = we_all.shape[2]
+    other = 2 * (1 - y) + c
+    own = 2 * y + c
+
+    def remote(index, src, dst, target):
+        copy = pltpu.make_async_remote_copy(
+            src_ref=src,
+            dst_ref=dst,
+            send_sem=send.at[index],
+            recv_sem=recv.at[index],
+            device_id=target,
+            device_id_type=MESH,
+        )
+        copy.start()
+        return copy
+
+    first = [
+        remote(0, hid, hid_all.at[me], across),
+        remote(1, cot, cot_all.at[me], across),
+        remote(2, ints, ints_all.at[me], across),
+    ]
+    rest = [remote(3, vec, vec_all.at[y], across)]
+    for j in range(3):
+        cols = pl.ds(pl.multiple_of(j * width + other * head_cols, head_cols), head_cols)
+        rest.append(
+            remote(
+                4 + j, wm.at[:, cols], wm_all.at[y, :, pl.ds(j * head_cols, head_cols)], across
+            )
+        )
+    cols = pl.ds(pl.multiple_of(other * ff, ff), ff)
+    rest.append(remote(7, we.at[:, cols], we_all.at[y], across))
+    rest += [
+        remote(8, hid, hid_all.at[me], core),
+        remote(9, cot, cot_all.at[me], core),
+        remote(10, ints, ints_all.at[me], core),
+    ]
+    moves = [(hid, hid_all.at[me]), (cot, cot_all.at[me]), (ints, ints_all.at[me]), (vec, vec_all.at[y])]
+    for j in range(3):
+        cols = pl.ds(pl.multiple_of(j * width + own * head_cols, head_cols), head_cols)
+        moves.append((wm.at[:, cols], wm_all.at[y, :, pl.ds(j * head_cols, head_cols)]))
+    cols = pl.ds(pl.multiple_of(own * ff, ff), ff)
+    moves.append((we.at[:, cols], we_all.at[y]))
+    locals_ = []
+    for index, (src, dst) in enumerate(moves):
+        copy = pltpu.make_async_copy(src, dst, local.at[index])
+        copy.start()
+        locals_.append(copy)
+    beside = 2 * c + 1 - y
+    for index, (copy, full) in enumerate(zip(first, (hid_all, cot_all, ints_all))):
+        copy.wait_recv()
+        rest.append(remote(11 + index, full.at[beside], full.at[beside], core))
+    for copy in first:
+        copy.wait_send()
+    for copy in rest:
+        copy.wait()
+    for copy in locals_:
+        copy.wait()
+
+
+def exchange(hid, cot, ints, vec, wm, we):
+    tokens, width = hid.shape
+    rows = wm.shape[0]
+    any_spec = pl.BlockSpec(memory_space=pl.ANY)
+    shapes = (
+        jax.ShapeDtypeStruct((GROUP,) + hid.shape, hid.dtype),
+        jax.ShapeDtypeStruct((GROUP,) + cot.shape, cot.dtype),
+        jax.ShapeDtypeStruct((GROUP,) + ints.shape, ints.dtype),
+        jax.ShapeDtypeStruct((2,) + vec.shape, vec.dtype),
+        jax.ShapeDtypeStruct((2, rows, wm.shape[1] // GROUP), wm.dtype),
+        jax.ShapeDtypeStruct((2, rows, we.shape[1] // GROUP), we.dtype),
+    )
+    return pl.pallas_call(
+        exchange_kernel,
+        out_shape=shapes,
+        in_specs=[any_spec] * 6,
+        out_specs=[any_spec] * 6,
+        scratch_shapes=[
+            pltpu.SemaphoreType.DMA((14,)),
+            pltpu.SemaphoreType.DMA((14,)),
+            pltpu.SemaphoreType.DMA((8,)),
+        ],
+        compiler_params=pltpu.CompilerParams(collective_id=0, has_side_effects=True),
+        name="exchange",
+    )(hid, cot, ints, vec, wm, we)
+
+
+def scatter_kernel(count, src, dst, send, recv, local):
+    c, y, s = position_here()
+    rows, lanes = dst.shape[2], dst.shape[3]
+    peers = [(c, y, lax.rem(s + d, count)) for d in range(1, count)]
+    greet(peers)
+
+    def part(target):
+        return src.at[
+            :,
+            pl.ds(pl.multiple_of((target // 2) * rows, rows), rows),
+            pl.ds(pl.multiple_of(lax.rem(target, 2) * lanes, lanes), lanes),
+        ]
+
+    copies = []
+    for d in range(1, count):
+        target = lax.rem(s + d, count)
+        copy = pltpu.make_async_remote_copy(
+            src_ref=part(target),
+            dst_ref=dst.at[:, s],
+            send_sem=send.at[d],
+            recv_sem=recv.at[d],
+            device_id=(c, y, target),
+            device_id_type=MESH,
+        )
+        copy.start()
+        copies.append(copy)
+    own = pltpu.make_async_copy(part(s), dst.at[:, s], local)
+    own.start()
+    own.wait()
+    for copy in copies:
+        copy.wait()
+
+
+def gather_kernel(count, src, dst, send, recv, local):
+    c, y, s = position_here()
+    rows, lanes = src.shape[2], src.shape[3]
+    peers = [(c, y, lax.rem(s + d, count)) for d in range(1, count)]
+    greet(peers)
+    place = dst.at[
+        :,
+        pl.ds(pl.multiple_of((s // 2) * rows, rows), rows),
+        pl.ds(pl.multiple_of(lax.rem(s, 2) * lanes, lanes), lanes),
+    ]
+    copies = []
+    for d in range(1, count):
+        target = lax.rem(s + d, count)
+        copy = pltpu.make_async_remote_copy(
+            src_ref=src.at[:, target],
+            dst_ref=place,
+            send_sem=send.at[d],
+            recv_sem=recv.at[d],
+            device_id=(c, y, target),
+            device_id_type=MESH,
+        )
+        copy.start()
+        copies.append(copy)
+    own = pltpu.make_async_copy(src.at[:, s], place, local)
+    own.start()
+    own.wait()
+    for copy in copies:
+        copy.wait()
+
+
+def swap_tokens(kernel, identity, name, array, shape, count):
+    any_spec = pl.BlockSpec(memory_space=pl.ANY)
+    return pl.pallas_call(
+        functools.partial(kernel, count),
+        out_shape=jax.ShapeDtypeStruct(shape, array.dtype),
+        in_specs=[any_spec],
+        out_specs=any_spec,
+        scratch_shapes=[
+            pltpu.SemaphoreType.DMA((count,)),
+            pltpu.SemaphoreType.DMA((count,)),
+            pltpu.SemaphoreType.DMA,
+        ],
+        compiler_params=pltpu.CompilerParams(collective_id=identity, has_side_effects=True),
+        name=name,
+    )(array)
+
+
+def attention_kernel(
+    ints,
+    parts,
+    cosine,
+    sine_up,
+    sine_down,
+    out,
+    masked,
+    flat,
+    scores,
+    slopes,
+    key_sum,
+    value_sum,
+    mixed_sum,
+    query_sum,
+    units,
+    pieces,
+):
+    length = parts.shape[1]
+    scale = 1.0 / math.sqrt(HEAD)
+    blocks = length // SPAN
+    lanes = lax.broadcasted_iota(jnp.int32, (UNIT, 2 * HEAD), 1)
+    lower = lanes < HEAD
+
+    def arrange(index, carry):
+        here = pl.multiple_of(index * UNIT, UNIT)
+        place = pl.multiple_of(ints[0, index] * UNIT, UNIT)
+        for which in range(4):
+            rows = parts[which, pl.ds(here, UNIT), :].astype(jnp.float32)
+            if which == 0:
+                rows = rows * scale
+            masked[which, 0, pl.ds(place, UNIT), :] = jnp.where(lower, rows, 0.0).astype(
+                jnp.bfloat16
+            )
+            masked[which, 1, pl.ds(place, UNIT), :] = jnp.where(lower, 0.0, rows).astype(
+                jnp.bfloat16
+            )
+            flat[which, :, pl.ds(place, UNIT)] = rows.T.astype(jnp.bfloat16)
+        return carry
+
+    lax.fori_loop(0, units, arrange, 0)
+    key_sum[...] = jnp.zeros_like(key_sum)
+    value_sum[...] = jnp.zeros_like(value_sum)
+
+    def labels(positions):
+        found = jnp.full(positions.shape, -1, jnp.int32)
+        for piece in range(pieces):
+            start = ints[0, units + piece]
+            found = jnp.where(
+                (positions >= start) & (positions < start + PIECE), piece, found
+            )
+        return found
+
+    def dot(a, b):
+        return jnp.dot(a, b, preferred_element_type=jnp.float32)
+
+    for block in range(blocks):
+        begin = block * SPAN
+        last = SPAN + (UNIT if block + 1 < blocks else 0)
+        columns = pl.ds(begin, SPAN)
+        row_at = begin + lax.broadcasted_iota(jnp.int32, (1, SPAN), 1)
+        col_at = begin + lax.broadcasted_iota(jnp.int32, (last, 1), 0)
+        row_lab = labels(row_at)
+        col_lab = labels(col_at)
+        allowed = (col_at <= row_at) | (
+            (col_lab == row_lab) & (row_lab >= 0)
+        )
+
+        def one_head(head, carry):
+            queries = flat[0, :, columns]
+            grads = flat[3, :, columns]
+            side = pl.ds(pl.multiple_of(head * HEAD, HEAD), HEAD)
+
+            def score_tile(start, size, top, mask):
+                rows = pl.ds(start, size)
+                tile = dot(masked[1, head, rows, :], queries)
+                if mask is not None:
+                    tile = jnp.where(mask, tile, NEGATIVE)
+                scores[rows, :] = tile
+                return jnp.maximum(top, jnp.max(tile, axis=0, keepdims=True))
+
+            top = lax.fori_loop(
+                0,
+                block,
+                lambda j, top: score_tile(pl.multiple_of(j * SPAN, SPAN), SPAN, top, None),
+                jnp.full((1, SPAN), NEGATIVE, jnp.float32),
+            )
+            top = score_tile(begin, last, top, allowed)
+
+            def weight_tile(start, size, sums):
+                total, delta = sums
+                rows = pl.ds(start, size)
+                weights = jnp.exp(scores[rows, :] - top)
+                slope = dot(masked[2, head, rows, :], grads)
+                scores[rows, :] = weights
+                slopes[rows, :] = slope
+                return (
+                    total + jnp.sum(weights, axis=0, keepdims=True),
+                    delta + jnp.sum(weights * slope, axis=0, keepdims=True),
+                )
+
+            zero = jnp.zeros((1, SPAN), jnp.float32)
+            sums = lax.fori_loop(
+                0,
+                block,
+                lambda j, sums: weight_tile(pl.multiple_of(j * SPAN, SPAN), SPAN, sums),
+                (zero, zero),
+            )
+            total, delta = weight_tile(begin, last, sums)
+            inverse = 1.0 / total
+            delta = delta * inverse
+
+            def grad_tile(start, size, sums):
+                mixed, query = sums
+                rows = pl.ds(start, size)
+                probs = scores[rows, :] * inverse
+                grad = (probs * (slopes[rows, :] - delta)).astype(jnp.bfloat16)
+                probs = probs.astype(jnp.bfloat16)
+                value_sum[rows, :] += dot(probs, masked[3, head, columns, :])
+                key_sum[rows, :] += dot(grad, masked[0, head, columns, :])
+                mixed = mixed + dot(flat[2, side, rows], probs)
+                query = query + dot(flat[1, side, rows], grad)
+                return (mixed, query)
+
+            none = jnp.zeros((HEAD, SPAN), jnp.float32)
+            sums = lax.fori_loop(
+                0,
+                block,
+                lambda j, sums: grad_tile(pl.multiple_of(j * SPAN, SPAN), SPAN, sums),
+                (none, none),
+            )
+            mixed, query = grad_tile(begin, last, sums)
+            mixed_sum[side, columns] = mixed
+            query_sum[side, columns] = query * scale
+            return carry
+
+        lax.fori_loop(0, 2, one_head, 0)
+
+    def turn_back(rows, at):
+        up = pltpu.roll(rows, 2 * HEAD - HALF, 1)
+        down = pltpu.roll(rows, HALF, 1)
+        return (
+            rows * cosine[at, :] + up * sine_up[at, :] - down * sine_down[at, :]
+        )
+
+    def finish(index, carry):
+        at = pl.ds(pl.multiple_of(index * UNIT, UNIT), UNIT)
+        key_sum[at, :] = turn_back(key_sum[at, :], at)
+        masked[0, 0, at, :] = mixed_sum[:, at].T.astype(jnp.bfloat16)
+        masked[1, 0, at, :] = turn_back(query_sum[:, at].T, at).astype(jnp.bfloat16)
+        return carry
+
+    lax.fori_loop(0, units, finish, 0)
+
+    def restore(index, carry):
+        here = pl.ds(pl.multiple_of(index * UNIT, UNIT), UNIT)
+        place = pl.ds(pl.multiple_of(ints[0, index] * UNIT, UNIT), UNIT)
+        out[0, here, :] = masked[0, 0, place, :]
+        out[1, here, :] = masked[1, 0, place, :]
+        out[2, here, :] = key_sum[place, :].astype(jnp.bfloat16)
+        out[3, here, :] = value_sum[place, :].astype(jnp.bfloat16)
+        return carry
+
+    lax.fori_loop(0, units, restore, 0)
+
+
+def attend(ints, parts, cosine, sine_up, sine_down, units, pieces):
+    length = parts.shape[1]
+    vmem = pl.BlockSpec(memory_space=pltpu.VMEM)
+    flops = 6 * 2 * 2 * HEAD * length * length // 2
+    return pl.pallas_call(
+        functools.partial(attention_kernel, units=units, pieces=pieces),
+        out_shape=jax.ShapeDtypeStruct(parts.shape, parts.dtype),
+        in_specs=[pl.BlockSpec(memory_space=pltpu.SMEM)] + [vmem] * 4,
+        out_specs=vmem,
+        scratch_shapes=[
+            pltpu.VMEM((4, 2, length, 2 * HEAD), jnp.bfloat16),
+            pltpu.VMEM((4, 2 * HEAD, length), jnp.bfloat16),
+            pltpu.VMEM((length, SPAN), jnp.float32),
+            pltpu.VMEM((length, SPAN), jnp.float32),
+            pltpu.VMEM((length, 2 * HEAD), jnp.float32),
+            pltpu.VMEM((length, 2 * HEAD), jnp.float32),
+            pltpu.VMEM((2 * HEAD, length), jnp.float32),
+            pltpu.VMEM((2 * HEAD, length), jnp.float32),
+        ],
+        compiler_params=pltpu.CompilerParams(vmem_limit_bytes=48 << 20),
+        cost_estimate=pl.CostEstimate(
+            flops=flops * 4, bytes_accessed=8 << 20, transcendentals=length * length
+        ),
+        name="attend",
+    )(ints, parts, cosine, sine_up, sine_down)
+
+
+def total_kernel(outs, terms, out_sum, term_sum, near, far, pair, send, recv):
+    c, y, s = position_here()
+    core = (1 - c, y, s)
+    across = (c, 1 - y, s)
+    greet((core, across))
+    copies = []
+    for index, src in enumerate((outs, terms)):
+        copy = pltpu.make_async_remote_copy(
+            src_ref=src.at[pl.ds(2 * (1 - c), 2)],
+            dst_ref=near.at[index],
+            send_sem=send.at[index],
+            recv_sem=recv.at[index],
+            device_id=core,
+            device_id_type=MESH,
+        )
+        copy.start()
+        copies.append(copy)
+    later = []
+    for index, src in enumerate((outs, terms)):
+        copies[index].wait()
+        pair[index] = (
+            src[2 * c + 1 - y].astype(jnp.float32) + near[index, 1 - y].astype(jnp.float32)
+        ).astype(jnp.bfloat16)
+        copy = pltpu.make_async_remote_copy(
+            src_ref=pair.at[index],
+            dst_ref=far.at[index],
+            send_sem=send.at[2 + index],
+            recv_sem=recv.at[2 + index],
+            device_id=across,
+            device_id_type=MESH,
+        )
+        copy.start()
+        later.append(copy)
+    for index, (src, dst) in enumerate(((outs, out_sum), (terms, term_sum))):
+        dst[...] = src[2 * c + y].astype(jnp.float32) + near[index, y].astype(jnp.float32)
+    for index, dst in enumerate((out_sum, term_sum)):
+        later[index].wait()
+        dst[...] += far[index].astype(jnp.float32)
+
+
+def total_group(outs, terms):
+    shape = outs.shape[1:]
+    vmem = pl.BlockSpec(memory_space=pltpu.VMEM)
+    return pl.pallas_call(
+        total_kernel,
+        out_shape=(jax.ShapeDtypeStruct(shape, jnp.float32),) * 2,
+        in_specs=[vmem] * 2,
+        out_specs=[vmem] * 2,
+        scratch_shapes=[
+            pltpu.VMEM((2, 2) + shape, jnp.bfloat16),
+            pltpu.VMEM((2,) + shape, jnp.bfloat16),
+            pltpu.VMEM((2,) + shape, jnp.bfloat16),
+            pltpu.SemaphoreType.DMA((4,)),
+            pltpu.SemaphoreType.DMA((4,)),
+        ],
+        compiler_params=pltpu.CompilerParams(
+            collective_id=3, has_side_effects=True, vmem_limit_bytes=32 << 20
+        ),
+        name="total_group",
+    )(outs, terms)
+
+
+def lane_tables(positions, lanes):
+    lane = jnp.arange(lanes, dtype=jnp.int32) % HEAD
+    inverse = jnp.exp((lane % HALF).astype(jnp.float32) * (-2.0 * math.log(10000.0) / ROT))
+    angles = positions.astype(jnp.float32)[:, None] * inverse[None, :]
+    cosine = jnp.where(lane[None, :] < ROT, jnp.cos(angles), 1.0)
+    sine = jnp.sin(angles)
+    up = jnp.where(lane[None, :] < HALF, sine, 0.0)
+    down = jnp.where((lane[None, :] >= HALF) & (lane[None, :] < ROT), sine, 0.0)
+    return (cosine, up, down)
+
+
+def turn_lanes(values, tables):
+    cosine, up, down = tables
+    return (
+        values * cosine
+        - jnp.roll(values, -HALF, axis=1) * up
+        + jnp.roll(values, HALF, axis=1) * down
+    )
+
+
+def group_body(
+    hidden_states,
+    unit_order,
+    piece_starts,
+    first_gain,
+    first_shift,
+    second_gain,
+    second_shift,
+    merged_weight,
+    merged_bias,
+    output_weight,
+    output_bias,
+    expand_weight,
+    expand_bias,
+    contract_weight,
+    contract_bias,
+    out_cotangent,
+):
+    c, y, s = position_here()
+    quarter = 2 * y + c
+    count = lax.axis_size("seq")
+    tokens, width = hidden_states.shape[1:]
+    length = tokens * count
+    units = unit_order.shape[1]
+    pieces = piece_starts.shape[1]
+    rows = GROUP * tokens
+    part = width // GROUP
+    ff_part = expand_weight.shape[1] // GROUP
+    vectors = (
+        first_gain,
+        first_shift,
+        second_gain,
+        second_shift,
+        merged_bias,
+        output_bias,
+        expand_bias,
+        contract_bias,
+    )
+    sizes = [v.shape[0] for v in vectors]
+    packed = jnp.concatenate(vectors).reshape(-1, 128)
+    ints = jnp.concatenate([unit_order[0], piece_starts[0]])
+    ints = jnp.broadcast_to(jnp.pad(ints, (0, 128 - ints.shape[0]))[None], (8, 128))
+    hid_all, cot_all, ints_all, vec_all, wm_all, we_all = exchange(
+        hidden_states[0], out_cotangent[0], ints, packed, merged_weight, expand_weight
+    )
+    vec_all = vec_all.reshape(2, -1)
+    whole = []
+    at = 0
+    for size in sizes:
+        whole.append(vec_all[:, at : at + size].reshape(-1).astype(jnp.float32))
+        at += size
+    gain_one, shift_one, gain_two, shift_two, bias_merged, bias_out, bias_expand, bias_contract = whole
+    wm = wm_all.reshape(width, 3 * part)
+    we = we_all.reshape(width, ff_part)
+    wo = lax.dynamic_slice_in_dim(output_weight, c * part, part, 0)
+    wc = lax.dynamic_slice_in_dim(contract_weight, c * ff_part, ff_part, 0)
+    cots = cot_all.reshape(rows, width)
+    hidden = hid_all.reshape(rows, width).astype(jnp.float32)
+    mean = jnp.mean(hidden, axis=1, keepdims=True)
+    centred = hidden - mean
+    rstd = lax.rsqrt(jnp.mean(centred * centred, axis=1, keepdims=True) + EPS)
+    xhat = centred * rstd
+    first = (xhat * gain_one + shift_one).astype(jnp.bfloat16)
+    second = (xhat * gain_two + shift_two).astype(jnp.bfloat16)
+    own_bias = lax.dynamic_slice_in_dim(
+        bias_merged.reshape(3, GROUP, part), quarter, 1, 1
+    ).reshape(3 * part)
+    merged = jnp.dot(first, wm, preferred_element_type=jnp.float32) + own_bias
+    own_units = tokens // UNIT
+    local_units = lax.dynamic_slice_in_dim(ints_all[:, 0, :], s * own_units, own_units, 1)
+    positions = (
+        local_units.reshape(-1)[:, None] * UNIT + jnp.arange(UNIT, dtype=jnp.int32)[None, :]
+    ).reshape(-1)
+    tables = lane_tables(positions, part)
+    queries = turn_lanes(merged[:, :part], tables).astype(jnp.bfloat16)
+    keys = turn_lanes(merged[:, part : 2 * part], tables).astype(jnp.bfloat16)
+    values = merged[:, 2 * part :].astype(jnp.bfloat16)
+    grad_mixed = lax.dot_general(
+        cots, wo, (((1,), (1,)), ((), ())), preferred_element_type=jnp.float32
+    ).astype(jnp.bfloat16)
+    sent = jnp.stack([queries, keys, values, grad_mixed])
+    got = swap_tokens(
+        scatter_kernel, 1, "scatter", sent, (4, count, tokens, 2 * HEAD), count
+    ).reshape(4, length, 2 * HEAD)
+    own_ints = lax.dynamic_index_in_dim(ints_all[:, 0, :], s // 2, 0, keepdims=True)
+    sorted_tables = lane_tables(jnp.arange(length, dtype=jnp.int32), 2 * HEAD)
+    done = attend(own_ints, got, *sorted_tables, units, pieces)
+    back = swap_tokens(
+        gather_kernel,
+        2,
+        "gather",
+        done.reshape(4, count, tokens, 2 * HEAD),
+        (4, rows, part),
+        count,
+    )
+    mixed = back[0]
+    grad_merged = jnp.concatenate([back[1], back[2], back[3]], axis=1)
+
+    own_expand = lax.dynamic_slice_in_dim(bias_expand, quarter * ff_part, ff_part, 0)
+    expanded = jnp.dot(second, we, preferred_element_type=jnp.float32) + own_expand
+    activated, gelu_pull = jax.vjp(gelu_exact, expanded)
+    active = activated.astype(jnp.bfloat16)
+    grad_active = lax.dot_general(
+        cots, wc, (((1,), (1,)), ((), ())), preferred_element_type=jnp.float32
+    )
+    grad_expanded = gelu_pull(grad_active)[0].astype(jnp.bfloat16)
+
+    def against(a, b):
+        return lax.dot_general(a, b, (((0,), (0,)), ((), ())), preferred_element_type=jnp.float32)
+
+    def swap_halves(own, other):
+        got = lax.ppermute(other, "fsdp", [(0, 1), (1, 0)])
+        return jnp.where(y == 0, jnp.stack([own, got]), jnp.stack([got, own]))
+
+    half = width // 2
+    d_expand = against(second, grad_expanded).astype(jnp.bfloat16)
+    d_contract = against(active, cots).astype(jnp.bfloat16)
+    feed_part = jnp.concatenate(
+        [d_expand[:half], d_expand[half:], d_contract[:half], d_contract[half:]], axis=1
+    )
+    feed_part = lax.psum_scatter(feed_part, "seq", scatter_dimension=0, tiled=True)
+    d_merged = against(first, grad_merged).astype(jnp.bfloat16)
+    d_output = against(mixed, cots).astype(jnp.bfloat16)
+    d_output = jnp.concatenate([d_output[:, :half], d_output[:, half:]], axis=0)
+    attn_part = jnp.concatenate([d_merged[:half], d_merged[half:], d_output], axis=1)
+    attn_part = lax.psum_scatter(attn_part, "seq", scatter_dimension=0, tiled=True)
+
+    def spread(piece, cols):
+        parts = piece[:, : 2 * cols].reshape(-1, 2, cols)
+        own = lax.dynamic_index_in_dim(parts, y, 1, keepdims=False)
+        other = lax.dynamic_index_in_dim(parts, 1 - y, 1, keepdims=False)
+        pair = swap_halves(own, other)
+        piece = jnp.concatenate([pair[0], pair[1], piece[:, 2 * cols :]], axis=1)
+        piece = lax.all_gather(piece, "seq", axis=0, tiled=True)
+        return lax.all_gather(piece, "rep", axis=0)
+
+    feed_all = spread(feed_part, ff_part)
+    attn_all = spread(attn_part, 3 * part)
+    expand_out = feed_all[:, :, : 2 * ff_part].reshape(2, half, 2, ff_part)
+    expand_out = expand_out.transpose(1, 2, 0, 3).reshape(half, GROUP * ff_part)
+    contract_out = feed_all[:, :, 2 * ff_part :].reshape(2, half, 2, width)
+    contract_out = contract_out.transpose(0, 2, 1, 3).reshape(2 * ff_part, width)
+    merged_out = attn_all[:, :, : 6 * part].reshape(2, half, 2, 3, part)
+    merged_out = merged_out.transpose(1, 3, 2, 0, 4).reshape(half, 3 * width)
+    output_out = attn_all[:, :, 6 * part :].reshape(2, 2, part, half)
+    output_out = output_out.transpose(0, 2, 1, 3).reshape(2 * part, width)
+
+    out_partial = jnp.dot(mixed, wo, preferred_element_type=jnp.float32) + jnp.dot(
+        active, wc, preferred_element_type=jnp.float32
+    )
+    grad_first = lax.dot_general(
+        grad_merged, wm, (((1,), (1,)), ((), ())), preferred_element_type=jnp.float32
+    )
+    grad_second = lax.dot_general(
+        grad_expanded, we, (((1,), (1,)), ((), ())), preferred_element_type=jnp.float32
+    )
+    term_partial = grad_first * gain_one + grad_second * gain_two
+    shape = (GROUP, tokens, width)
+    out_sum, term_sum = total_group(
+        out_partial.astype(jnp.bfloat16).reshape(shape),
+        term_partial.astype(jnp.bfloat16).reshape(shape),
+    )
+    own_hidden = hidden_states[0].astype(jnp.float32)
+    own_mean = jnp.mean(own_hidden, axis=1, keepdims=True)
+    own_centred = own_hidden - own_mean
+    own_rstd = lax.rsqrt(jnp.mean(own_centred * own_centred, axis=1, keepdims=True) + EPS)
+    own_xhat = own_centred * own_rstd
+    output = (own_hidden + out_sum + bias_out + bias_contract).astype(jnp.bfloat16)
+    upstream = out_cotangent[0].astype(jnp.float32)
+    input_gradient = upstream + own_rstd * (
+        term_sum
+        - jnp.mean(term_sum, axis=1, keepdims=True)
+        - own_xhat * jnp.mean(term_sum * own_xhat, axis=1, keepdims=True)
+    )
+    merged_bias_part = jnp.sum(grad_merged.astype(jnp.float32), axis=0).reshape(3, 1, part)
+    slot = (jnp.arange(GROUP, dtype=jnp.int32) == quarter).astype(jnp.float32)
+    merged_bias_part = (merged_bias_part * slot[None, :, None]).reshape(-1)
+    expand_bias_part = jnp.sum(grad_expanded.astype(jnp.float32), axis=0)
+    expand_bias_part = (expand_bias_part[None, :] * slot[:, None]).reshape(-1)
+    small = jnp.concatenate(
+        [
+            jnp.sum(grad_first * xhat, axis=0),
+            jnp.sum(grad_first, axis=0),
+            jnp.sum(grad_second * xhat, axis=0),
+            jnp.sum(grad_second, axis=0),
+            jnp.sum(upstream, axis=0),
+            merged_bias_part,
+            expand_bias_part,
+        ]
+    )
+    small = lax.psum(small, ("rep", "fsdp", "seq"))
+
+    def own_half(begin, size):
+        return lax.dynamic_slice_in_dim(small, begin + y * (size // 2), size // 2, 0)
+
+    row_total = own_half(4 * width, width)
+    return (
+        output[None],
+        input_gradient[None],
+        own_half(0, width),
+        own_half(width, width),
+        own_half(2 * width, width),
+        own_half(3 * width, width),
+        merged_out.astype(jnp.float32),
+        own_half(5 * width, 3 * width),
+        output_out.astype(jnp.float32),
+        row_total,
+        expand_out.astype(jnp.float32),
+        own_half(8 * width, GROUP * ff_part),
+        contract_out.astype(jnp.float32),
+        row_total,
+    )
+
+
+def fits_groups(mesh, args):
+    hidden, order = args[0], args[1]
+    count = mesh.shape["seq"]
+    tokens = hidden.shape[1] // count
+    heads = hidden.shape[2] // HEAD
+    return (
+        mesh.shape["rep"] == 2
+        and mesh.shape["fsdp"] == 2
+        and hidden.shape[0] == GROUP
+        and count == heads // 2
+        and tokens % UNIT == 0
+        and hidden.shape[1] % SPAN == 0
+        and order.shape[1] + args[2].shape[1] <= 128
+    )
+
+
 def solution(mesh):
     in_specs = (
         P(("rep", "fsdp"), "seq", None),
@@ -450,4 +1151,12 @@
         P("fsdp", None),
         P("fsdp"),
     )
-    return jax.shard_map(body, mesh=mesh, in_specs=in_specs, out_specs=out_specs, check_vma=False)
+
+    def run(*args):
+        chosen = group_body if fits_groups(mesh, args) else body
+        mapped = jax.shard_map(
+            chosen, mesh=mesh, in_specs=in_specs, out_specs=out_specs, check_vma=False
+        )
+        return mapped(*args)
+
+    return run

time: 2010 us -> 793 us (0.39)
  blocking collectives: 1080 us -> 38.3 us
  waiting for transfers between devices: 531 us -> 257 us
  Pallas kernels: 0 us -> 241 us
  matrix products: 237 us -> 61.1 us
  local copies, waits for them, and re-layouts: 81.2 us -> 119 us
    psum x1, blocking collectives: 1040 us -> 38.3 us  [group_body(): small = lax.psum(small, ('rep', 'fsdp', 'seq'))]
    reduce_scatter x5 -> x1, waiting for transfers between devices: 342 us -> 62 us  [group_body(): lax.psum_scatter(attn_part, 'seq', scatter_dimension=0, tiled=True)]
    pallas_call x0 -> x5, Pallas kernels: none -> 241 us  [the longest x1 92.3 us: exchange(): pl.pallas_call(exchange_kernel, out_shape=shapes, in_specs=[any_spec] * 6...]
    dot_general x52 -> x12, matrix products: 237 us -> 61.1 us  [the longest x1 24.4 us: group_body(): jnp.dot(second, we, preferred_element_type=jnp.float32) + own_expand]
    unnamed x11 -> x7, waiting for transfers between devices: 2.55 us -> 81.3 us
    all_gather x6 -> x4, waiting for transfers between devices: 186 us -> 108 us  [the longest x2 108 us: spread(): piece = lax.all_gather(piece, 'seq', axis=0, tiled=True)]
    convert_element_type x1 -> x8, local copies, waits for them, and re-layouts: 2.06 us -> 61.8 us  [the longest x3 39 us: group_body(): expand_out.astype(jnp.float32)]
    all_gather x8 -> x0, blocking collectives: 35.9 us -> none  [the longest x1 5.28 us: body(): lax.all_gather(shards[5], 'fsdp', axis=0, tiled=True)]
  transfers between devices with their start and end apart: 11 -> 8, of which waited for: 8 -> 6; matrix products, arithmetic and copies ran while one was open for 18% -> 10% of each run, Pallas kernels for 0% -> 4%
where the time goes in v1:
time: 793 us; the launch traced here: 782 us
  waiting for transfers between devices  257 us (32%)
  Pallas kernels  241 us (30%)
  local copies, waits for them, and re-layouts  119 us (15%)
  matrix products  61.1 us (8%)
  other arithmetic  47.4 us (6%)
  blocking collectives  38.3 us (5%)
  between operations  15.3 us (2%)
    all_gather x2, waiting for transfers between devices, spread(): piece = lax.all_gather(piece, 'seq', axis=0, tiled=True)  108 us
    pallas_call x1, Pallas kernels, exchange(): pl.pallas_call(exchange_kernel, out_shape=shapes, in_specs=[any_spec] * 6...  92.3 us
    pallas_call x2, Pallas kernels, swap_tokens(): pl.pallas_call(functools.partial(kernel, count), out_shape=jax.ShapeDtype...  86.9 us
    unnamed x7, waiting for transfers between devices  81.3 us
    reduce_scatter x1, waiting for transfers between devices, group_body(): lax.psum_scatter(attn_part, 'seq', scatter_dimension=0, tiled=True)  62 us
    convert_element_type x3, local copies, waits for them, and re-layouts, group_body(): expand_out.astype(jnp.float32)  39 us
    psum x1, blocking collectives, group_body(): small = lax.psum(small, ('rep', 'fsdp', 'seq'))  38.3 us
    unnamed x102, local copies, waits for them, and re-layouts  36.4 us
  transfers between devices with their start and end apart: 8, of which 6 were waited for; matrix products, arithmetic and copies ran while one was open for 10% of the time, Pallas kernels for 4%

profile of v1, /device:TPU:0, one launch (start us, length us, event | category | flops | bytes accessed | tf_op | source)
XLA Modules:
  0.0 782.3 jit_solution(4985360677649749031)
XLA Ops:
  15.3 92.3 %exchange.1 = (bf16[4,256,1024]{2,1,0:T(8,128)(2,1)}, bf16[4,256,1024]{2,1,0:T(8,128)(2,1)}, s32[4,8,128]{2,1,0:T(8,128)}, bf16[2,52,128]{2,1,0:T(8,128)(2,1)}, ...) custom-call(bf16[256,1024]{1,0:T(8,128)(2,1)} %bitcast.164, bf16[256,1024]{1,0:T(8,128)(2,1)} %bitcast.171, ...), custom_call_target="tpu_custom_call" | custom-call | tf_op jit(solution)/shard_map/exchange/pallas_call | solution.py:519
  125.9 7.0 fusion.49
  134.5 38.4 %scatter.1 = bf16[4,8,256,128]{3,2,1,0:T(8,128)(2,1)} custom-call(bf16[4,1024,256]{2,1,0:T(8,128)(2,1)} %pad_maximum_fusion.1.src), custom_call_target="tpu_custom_call" | custom-call | tf_op jit(solution)/shard_map/scatter/pallas_call | solution.py:599
  176.7 32.6 %attend.1 = bf16[4,2048,128]{2,1,0:T(8,128)(2,1)S(1)} custom-call(s32[1,128]{1,0:T(1,128)S(1)} %fusion.68.ints, bf16[4,2048,128]{2,1,0:T(8,128)(2,1)} %bitcast.175, f32[2048,128]{1,0:T(8,128)S(1)} %get-tuple-element.122.cosine, f32[2048,128]{1,0:T(8,128)S(1)} %get-tuple-element.121.sine_up, f32[2048,128]{1,0:T(8,128)S(1)} %get-tuple-element.120.sine_down), custom_call_target="tpu_custom_call" | custom-call | flops 12884901888 | bytes 8388608 | tf_op jit(solution)/shard_map/attend/pallas_call | solution.py:784
  210.6 48.4 %gather.1 = bf16[4,1024,256]{2,1,0:T(8,128)(2,1)} custom-call(bf16[4,8,256,128]{3,2,1,0:T(8,128)(2,1)} %bitcast.159), custom_call_target="tpu_custom_call" | custom-call | tf_op jit(solution)/shard_map/gather/pallas_call | solution.py:599
  266.4 24.4 %multiply_convert_fusion = (bf16[1024,1024]{1,0:T(8,128)(2,1)}, f32[1024,1024]{1,0:T(8,128)S(1)}, f32[1024,1024]{1,0:T(8,128)S(1)}) fusion(f32[1024]{0:T(1024)S(1)} %dynamic_slice.61, bf16[1024,1024]{1,0:T(8,128)(2,1)S(1)} %bitcast.173, bf16[1024,1024]{1,0:T(8,128)(2,1)S(1)} %bitcast.204), kind=kOutput, calls=%fused_computation.17 | convolution fusion | flops 2216689664 | bytes 14684160 | tf_op jit(solution)/shard_map/dot_general | solution.py:988
  290.9 4.7 convert_reduce_fusion
  295.6 6.1 fusion.72
  320.9 6.3 copy.66
  327.3 62.0 %reduce-scatter.7.cloned.1.call-done = bf16[64,2048]{1,0:T(8,128)(2,1)} async-done(((bf16[512,2048]{1,0:T(8,128)(2,1)}), bf16[64,2048]{1,0:T(8,128)(2,1)}) %reduce-scatter.7.cloned.1.call-update) | async-done | bytes 262160 | tf_op jit(solution)/shard_map/reduce_scatter | solution.py:1014
  399.4 81.2 %reduce-scatter.9.cloned.1.call-done = bf16[64,4096]{1,0:T(8,128)(2,1)} async-done(((bf16[512,4096]{1,0:T(8,128)(2,1)}), bf16[64,4096]{1,0:T(8,128)(2,1)}) %reduce-scatter.9.cloned.1.call-update) | async-done | bytes 524304
  488.6 5.0 collective-permute-done.1
  499.6 33.1 %all-gather.7.cloned.1.call-done = bf16[512,2048]{1,0:T(8,128)(2,1)} async-done(((bf16[64,2048]{1,0:T(8,128)(2,1)}), bf16[512,2048]{1,0:T(8,128)(2,1)}) %all-gather.7.cloned.1.call-update) | async-done | bytes 2097168 | tf_op jit(solution)/shard_map/all_gather | solution.py:1022
  532.8 74.6 %all-gather.9.cloned.1.call-done = bf16[512,4096]{1,0:T(8,128)(2,1)} async-done(((bf16[64,4096]{1,0:T(8,128)(2,1)}), bf16[512,4096]{1,0:T(8,128)(2,1)}) %all-gather.9.cloned.1.call-update) | async-done | bytes 4194320 | tf_op jit(solution)/shard_map/all_gather | solution.py:1022
  615.7 29.2 %total_group.1 = (f32[256,1024]{1,0:T(8,128)S(1)}, f32[256,1024]{1,0:T(8,128)S(1)}) custom-call(bf16[4,256,1024]{2,1,0:T(8,128)(2,1)S(1)} %bitcast.157, bf16[4,256,1024]{2,1,0:T(8,128)(2,1)S(1)} %bitcast.158), custom_call_target="tpu_custom_call" | custom-call | tf_op jit(solution)/shard_map/total_group/pallas_call | solution.py:850
  647.5 38.3 %psum.7 = f32[12288]{0:T(1024)S(1)} all-reduce(f32[12288]{0:T(1024)S(1)} %bitcast_dynamic-update-slice_fusion), channel_id=1, replica_groups=mesh['rep'=2,'fsdp'=2,'seq'=8] {'rep','fsdp','seq'}, use_global_device_ids=true, to_apply=%region_13.14 | all-reduce | flops 12288 | bytes 98304 | tf_op jit(solution)/shard_map/psum | solution.py:1079
  696.2 6.6 copy.55
  702.8 6.2 copy.56
  709.0 6.6 copy.61
  715.5 11.6 %slice_convert_fusion = (f32[2,512,2048]{2,1,0:T(8,128)}, f32[2,512,2048]{2,1,0:T(8,128)}) fusion(bf16[2,512,4096]{2,1,0:T(8,128)(2,1)} %bitcast.165), kind=kLoop, calls=%fused_computation.4 | loop fusion | flops 4194304 | bytes 25165824 | tf_op jit(solution)/shard_map/convert_element_type | solution.py:1098
  727.1 8.4 %copy.91 = f32[2,64,2,8,1024]{4,3,1,2,0:T(8,128)} copy(f32[2,64,2,8,1024]{4,3,2,1,0:T(8,128)} %bitcast.160) | data formatting | bytes 16777216 | tf_op jit(solution)/shard_map/convert_element_type | solution.py:1098
  735.5 11.7 %reshape.395 = f32[2,512,2,1024]{3,2,1,0:T(2,128)} reshape(f32[2,512,2048]{2,1,0:T(8,128)} %get-tuple-element.67) | data formatting | bytes 16777216 | tf_op jit(solution)/shard_map/convert_element_type | solution.py:1096
  747.3 15.5 %copy.92 = f32[2,512,2,1024]{3,0,2,1:T(2,128)} copy(f32[2,512,2,1024]{3,2,1,0:T(2,128)} %reshape.395) | data formatting | bytes 16777216 | tf_op jit(solution)/shard_map/convert_element_type | solution.py:1096
  762.7 11.8 %reshape.391 = f32[512,4096]{1,0:T(8,128)} reshape(f32[512,2,2,1024]{3,2,1,0:T(2,128)} %bitcast.161) | data formatting | bytes 16777216 | tf_op jit(solution)/shard_map/convert_element_type | solution.py:1096
  (200 shorter events, 105.0 us)
Async XLA Ops:
  7.2 115.5 %copy-start = (bf16[512,1024]{1,0:T(8,128)(2,1)S(1)}, bf16[512,1024]{1,0:T(8,128)(2,1)}, u32[]{:S(2)}) copy-start(bf16[512,1024]{1,0:T(8,128)(2,1)} %param.25) | copy-start | bytes 3145732
  7.2 382.1 %reduce-scatter.7.cloned.1.call-start = ((), (), s32[]{:S(2)}) async-start(), calls=%async_computation.6 | async-start | bytes 2359296 | tf_op jit(solution)/shard_map/reduce_scatter | solution.py:1014
  107.7 5.4 copy-start.4
  125.9 7.1 copy-start.20
  262.1 4.3 copy-start.13
  266.4 24.5 %copy-start.27 = (bf16[2048,1024]{1,0:T(8,128)(2,1)S(1)}, bf16[2048,1024]{1,0:T(8,128)(2,1)}, u32[]{:S(2)}) copy-start(bf16[2048,1024]{1,0:T(8,128)(2,1)} %param.29) | copy-start | bytes 12582916
  266.4 24.4 %copy-start.28 = (bf16[4,256,1024]{2,1,0:T(8,128)(2,1)S(1)}, bf16[4,256,1024]{2,1,0:T(8,128)(2,1)}, u32[]{:S(2)}) copy-start(bf16[4,256,1024]{2,1,0:T(8,128)(2,1)} %get-tuple-element.26) | copy-start | bytes 6291460
  290.9 4.7 copy-start.5
  295.5 6.2 copy-start.31
  295.6 6.2 copy-start.14
  295.6 6.2 copy-start.16
  295.6 6.2 copy-start.18
  309.2 171.5 %reduce-scatter.9.cloned.1.call-start = ((), (), s32[]{:S(2)}) async-start(), calls=%async_computation.7 | async-start | bytes 4718592
  327.3 205.4 %all-gather.7.cloned.1.call-start = ((), (), s32[]{:S(2)}) async-start(), calls=%async_computation.2 | async-start | bytes 2359296 | tf_op jit(solution)/shard_map/all_gather | solution.py:1022
  393.9 4.7 collective-permute-start
  399.4 208.0 %all-gather.9.cloned.1.call-start = ((), (), s32[]{:S(2)}) async-start(), calls=%async_computation.3 | async-start | bytes 4718592 | tf_op jit(solution)/shard_map/all_gather | solution.py:1022
  485.2 8.4 %collective-permute-start.1 = (bf16[64,1024]{0,1:T(8,128)(2,1)}, bf16[64,1024]{0,1:T(8,128)(2,1)}, u32[]{:S(2)}, u32[]{:S(2)}) collective-permute-start(bf16[64,1024]{0,1:T(8,128)(2,1)} %get-tuple-element.97), channel_id=1, source_target_pairs={{0,8},{8,0},{1,9},{9,1},{2,10},{10,2},{3,11},{11,3},{4,12},{12,4},... | collective-permute-start | bytes 393224 | tf_op jit(solution)/shard_map/ppermute | solution.py:1000
  499.5 188.2 %all-gather.11.cloned.1.call-start = ((), (), s32[]{:S(2)}) async-start(), calls=%async_computation.4 | async-start | bytes 6291456 | tf_op jit(solution)/shard_map/all_gather | solution.py:1023
  532.7 182.8 %all-gather.13.cloned.1.call-start = ((), (), s32[]{:S(2)}) async-start(), calls=%async_computation.5 | async-start | bytes 12582912 | tf_op jit(solution)/shard_map/all_gather | solution.py:1023
  613.7 31.2 %copy-start.25 = (f32[1024]{0:T(1024)S(1)}, f32[1024]{0:T(1024)}, u32[]{:S(2)}) copy-start(f32[1024]{0:T(1024)} %get-tuple-element.69) | copy-start | bytes 12292
  613.8 31.2 %copy-start.24 = (f32[1024]{0:T(1024)S(1)}, f32[1024]{0:T(1024)}, u32[]{:S(2)}) copy-start(f32[1024]{0:T(1024)} %get-tuple-element.70) | copy-start | bytes 12292
  613.8 31.2 %copy-start.6 = (bf16[1,256,1024]{2,1,0:T(8,128)(2,1)S(1)}, bf16[1,256,1024]{2,1,0:T(8,128)(2,1)}, u32[]{:S(2)}) copy-start(bf16[1,256,1024]{2,1,0:T(8,128)(2,1)} %param.16) | copy-start | bytes 1572868
  615.7 30.1 %copy-start.11 = (bf16[1,256,1024]{2,1,0:T(8,128)(2,1)S(1)}, bf16[1,256,1024]{2,1,0:T(8,128)(2,1)}, u32[]{:S(2)}) copy-start(bf16[1,256,1024]{2,1,0:T(8,128)(2,1)} %param.31) | copy-start | bytes 1572868
  687.7 86.8 %copy-start.23 = (f32[512]{0:T(512)}, f32[512]{0:T(512)S(1)}, u32[]{:S(2)}) copy-start(f32[512]{0:T(512)S(1)} %get-tuple-element.161) | copy-start | bytes 6148
  (18 other events, 48.6 us)
Sparse Core Ops, SparseCore 0:
  309.3 79.9 reduce-scatter.6
  393.5 87.1 reduce-scatter.8
  483.6 49.0 all-gather.6
  535.5 71.8 all-gather.8
  608.8 14.2 all-gather.10
  624.6 18.6 all-gather.12

commit v2 on v0

--- a/solution.py
+++ b/solution.py
@@ -1,8 +1,11 @@
+import functools
 import math
 
 import jax
 import jax.numpy as jnp
 from jax import lax
+from jax.experimental import pallas as pl
+from jax.experimental.pallas import tpu as pltpu
 from jax.sharding import PartitionSpec as P
 
 HEAD = 64
@@ -415,6 +418,1625 @@
     )
 
 
+MESH = pl.DeviceIdType.MESH
+GROUP = 8
+LINE = 4
+HALF = ROT // 2
+SPAN = 512
+CHUNK = 32
+FEED_CHUNK = 16
+
+
+def place_here():
+    c, y, s = (lax.axis_index("rep"), lax.axis_index("fsdp"), lax.axis_index("seq"))
+    x = lax.rem(s, 2)
+    return (c, y, x, s // 2)
+
+
+def device_at(c, y, x, z):
+    return (c, y, 2 * z + x)
+
+
+def greet(partners):
+    barrier = pltpu.get_barrier_semaphore()
+    for partner in partners:
+        pl.semaphore_signal(barrier, inc=1, device_id=partner, device_id_type=MESH)
+    pl.semaphore_wait(barrier, len(partners))
+
+
+def remote(src, dst, send, recv, target):
+    return pltpu.make_async_remote_copy(
+        src_ref=src,
+        dst_ref=dst,
+        send_sem=send,
+        recv_sem=recv,
+        device_id=target,
+        device_id_type=MESH,
+    )
+
+
+def dot_rows(a, b):
+    return lax.dot_general(a, b, (((1,), (1,)), ((), ())), preferred_element_type=jnp.float32)
+
+
+def dot_tokens(a, b):
+    return lax.dot_general(a, b, (((0,), (0,)), ((), ())), preferred_element_type=jnp.float32)
+
+
+def dot_plain(a, b):
+    return jnp.dot(a, b, preferred_element_type=jnp.float32)
+
+
+class TokenExchange:
+    def __init__(self, place, send, recv):
+        self.place, self.send, self.recv = place, send, recv
+        self.count = 0
+        self.sends = []
+
+    def go(self, src, dst, target):
+        copy = remote(src, dst, self.send.at[self.count], self.recv.at[self.count], target)
+        self.count += 1
+        copy.start()
+        self.sends.append(copy)
+        return copy
+
+    def blocks(self, cc):
+        c, y, x, z = self.place
+
+        def block(yy, xx):
+            return (2 * cc + yy) * 2 + xx
+
+        return (block(y, x), block(y, 1 - x), block(1 - y, x), block(1 - y, 1 - x))
+
+    def start(self, src, full):
+        c, y, x, z = self.place
+        self.full = full
+        me = self.blocks(c)[0]
+        self.from_x = self.go(src, full.at[me], device_at(c, y, 1 - x, z))
+        self.from_y = self.go(src, full.at[me], device_at(c, 1 - y, x, z))
+        self.from_core = [self.go(src, full.at[me], device_at(1 - c, y, x, z))]
+
+    def relay(self):
+        c, y, x, z = self.place
+        full = self.full
+        me, near_x, near_y, far = self.blocks(c)
+        half = full.shape[1] // 2
+        core = device_at(1 - c, y, x, z)
+        upper, lower = pl.ds(0, half), pl.ds(half, half)
+        self.from_x.wait_recv()
+        second = self.go(
+            full.at[near_x, lower], full.at[near_x, lower], device_at(c, 1 - y, x, z)
+        )
+        self.from_core.append(self.go(full.at[near_x], full.at[near_x], core))
+        self.from_y.wait_recv()
+        first = self.go(full.at[near_y, upper], full.at[near_y, upper], device_at(c, y, 1 - x, z))
+        self.from_core.append(self.go(full.at[near_y], full.at[near_y], core))
+        self.corner = (first, second)
+
+    def relay_corner(self):
+        c, y, x, z = self.place
+        far = self.blocks(c)[3]
+        for copy in self.corner:
+            copy.wait_recv()
+        self.from_core.append(
+            self.go(self.full.at[far], self.full.at[far], device_at(1 - c, y, x, z))
+        )
+
+    def wait_core(self, index):
+        self.from_core[index].wait_recv()
+
+    def finish(self):
+        for copy in self.sends:
+            copy.wait_send()
+
+
+def column_block(part, at):
+    return pl.ds(pl.multiple_of(at, part), part)
+
+
+def enter_kernel(
+    hid,
+    ints,
+    vec,
+    wm,
+    unit_cos,
+    unit_sin,
+    row_cos,
+    row_sin,
+    hid_all,
+    ints_all,
+    vec_all,
+    wm_all,
+    heads,
+    second,
+    units,
+    rotated,
+    send,
+    recv,
+    local,
+):
+    place = place_here()
+    c, y, x, z = place
+    core = device_at(1 - c, y, x, z)
+    over_x = device_at(c, y, 1 - x, z)
+    over_y = device_at(c, 1 - y, x, z)
+    lanes = wm_all.shape[2] // 3
+    width = wm.shape[1] // 3
+    tokens = hid.shape[0]
+    own = 4 * y + 2 * x + c
+    other = 4 * (1 - y) + 2 * x + c
+    moved = []
+
+    def keep(src, dst):
+        copy = pltpu.make_async_copy(src, dst, local.at[len(moved)])
+        copy.start()
+        moved.append(copy)
+        return copy
+
+    me = (2 * c + y) * 2 + x
+    own_block = keep(hid, hid_all.at[me])
+    keep(ints, ints_all.at[2 * c + y])
+    keep(vec, vec_all.at[y])
+    for j in range(3):
+        keep(
+            wm.at[:, column_block(lanes, j * width + own * lanes)],
+            wm_all.at[y, :, pl.ds(j * lanes, lanes)],
+        )
+    greet((core, over_x, over_y))
+    tokens_move = TokenExchange(place, send, recv)
+    go = tokens_move.go
+    ints_y = go(ints, ints_all.at[2 * c + y], over_y)
+    vec_y = go(vec, vec_all.at[y], over_y)
+    ints_core = [go(ints, ints_all.at[2 * c + y], core)]
+    tokens_move.start(hid, hid_all)
+    weights = [
+        go(
+            wm.at[:, column_block(lanes, j * width + other * lanes)],
+            wm_all.at[y, :, pl.ds(j * lanes, lanes)],
+            over_y,
+        )
+        for j in range(3)
+    ]
+    ints_y.wait_recv()
+    ints_core.append(go(ints_all.at[2 * c + 1 - y], ints_all.at[2 * c + 1 - y], core))
+    vec_y.wait_recv()
+    for copy in moved:
+        copy.wait()
+    for copy in ints_core:
+        copy.wait_recv()
+    to_units = pltpu.make_async_copy(ints_all, units, local.at[0])
+    to_units.start()
+    to_units.wait()
+
+    def vector(row):
+        return jnp.concatenate(
+            [vec_all[h, row + i : row + i + 1, :] for h in range(2) for i in range(4)], axis=1
+        )
+
+    gain_one, shift_one, gain_two, shift_two = [vector(4 * i) for i in range(4)]
+    bias = []
+    for j in range(3):
+        at = j * GROUP + own
+        bias.append(vec_all[at // 12, pl.ds(16 + lax.rem(at, 12), 1), :])
+    bias = jnp.concatenate(bias, axis=1)
+
+    def normal(block):
+        raw = hid_all[block].astype(jnp.float32)
+        mean = jnp.mean(raw, axis=1, keepdims=True)
+        centred = raw - mean
+        rstd = lax.rsqrt(jnp.mean(centred * centred, axis=1, keepdims=True) + EPS)
+        xhat = centred * rstd
+        rows = pl.ds(pl.multiple_of(block * tokens, tokens), tokens)
+        second[rows, :] = (xhat * gain_two + shift_two).astype(jnp.bfloat16)
+        return (xhat * gain_one + shift_one).astype(jnp.bfloat16)
+
+    unit_index = lax.broadcasted_iota(jnp.int32, unit_cos.shape, 0)
+    lane = lax.rem(lax.broadcasted_iota(jnp.int32, row_cos.shape, 1), HEAD)
+
+    def project(block):
+        rows = pl.ds(pl.multiple_of(block * tokens, tokens), tokens)
+        sequence, side = block // 2, lax.rem(block, 2)
+        normed = normal(block)
+        half = wm.shape[0]
+        merged = (
+            dot_plain(normed[:, :half], wm_all[0])
+            + dot_plain(normed[:, half:], wm_all[1])
+            + bias
+        )
+        count = tokens // UNIT
+        for u in range(count):
+            unit = units[sequence, 0, (2 * z + side) * count + u]
+            here = pl.ds(u * UNIT, UNIT)
+            chosen = unit_index == unit
+            base_cos = jnp.sum(jnp.where(chosen, unit_cos[...], 0.0), axis=0, keepdims=True)
+            base_sin = jnp.sum(jnp.where(chosen, unit_sin[...], 0.0), axis=0, keepdims=True)
+            sine = base_sin * row_cos[...] + base_cos * row_sin[...]
+            rotated[0, here, :] = base_cos * row_cos[...] - base_sin * row_sin[...]
+            rotated[1, here, :] = jnp.where(lane < HALF, sine, 0.0)
+            rotated[2, here, :] = jnp.where(lane < HALF, 0.0, sine)
+        for j in range(2):
+            values = merged[:, j * lanes : (j + 1) * lanes]
+            turned = (
+                values * rotated[0]
+                - pltpu.roll(values, lanes - HALF, 1) * rotated[1]
+                + pltpu.roll(values, HALF, 1) * rotated[2]
+            )
+            heads[j, rows, :] = turned.astype(jnp.bfloat16)
+        heads[2, rows, :] = merged[:, 2 * lanes :].astype(jnp.bfloat16)
+
+    tokens_move.relay()
+    for copy in weights:
+        copy.wait_recv()
+    mine, theirs = tokens_move.blocks(c), tokens_move.blocks(1 - c)
+    for index in range(3):
+        project(mine[index])
+    tokens_move.relay_corner()
+    for index in range(3):
+        tokens_move.wait_core(index)
+        project(theirs[index])
+    project(mine[3])
+    tokens_move.wait_core(3)
+    project(theirs[3])
+    tokens_move.finish()
+
+
+def enter(hid, ints, vec, wm, tables):
+    tokens, width = hid.shape
+    rows = wm.shape[0]
+    lanes = width // GROUP
+    vmem = pl.BlockSpec(memory_space=pltpu.VMEM)
+    any_spec = pl.BlockSpec(memory_space=pl.ANY)
+    return pl.pallas_call(
+        enter_kernel,
+        out_shape=(
+            jax.ShapeDtypeStruct((GROUP,) + hid.shape, hid.dtype),
+            jax.ShapeDtypeStruct((4,) + ints.shape, ints.dtype),
+            jax.ShapeDtypeStruct((2,) + vec.shape, vec.dtype),
+            jax.ShapeDtypeStruct((2, rows, 3 * lanes), wm.dtype),
+            jax.ShapeDtypeStruct((3, GROUP * tokens, lanes), jnp.bfloat16),
+            jax.ShapeDtypeStruct((GROUP * tokens, width), jnp.bfloat16),
+        ),
+        in_specs=[any_spec] * 4 + [vmem] * 4,
+        out_specs=[vmem, any_spec, vmem, vmem, vmem, vmem],
+        scratch_shapes=[
+            pltpu.SMEM((4,) + ints.shape, jnp.int32),
+            pltpu.VMEM((3, tokens, lanes), jnp.float32),
+            pltpu.SemaphoreType.DMA((20,)),
+            pltpu.SemaphoreType.DMA((20,)),
+            pltpu.SemaphoreType.DMA((8,)),
+        ],
+        compiler_params=pltpu.CompilerParams(
+            collective_id=0, has_side_effects=True, vmem_limit_bytes=48 << 20
+        ),
+        name="enter",
+    )(hid, ints, vec, wm, *tables)
+
+
+def greet_line(place, more=()):
+    c, y, x, z = place
+    barrier = pltpu.get_barrier_semaphore()
+    partners = (device_at(1 - c, y, x, z), device_at(c, y, 1 - x, z), device_at(c, 1 - y, x, z))
+    for partner in partners:
+        pl.semaphore_signal(barrier, inc=1, device_id=partner, device_id_type=MESH)
+
+    @pl.when(z > 0)
+    def _():
+        pl.semaphore_signal(barrier, inc=1, device_id=device_at(c, y, x, z - 1), device_id_type=MESH)
+
+    @pl.when(z < LINE - 1)
+    def _():
+        pl.semaphore_signal(barrier, inc=1, device_id=device_at(c, y, x, z + 1), device_id_type=MESH)
+
+    @pl.when((z > 0) & (z < LINE - 1))
+    def _():
+        pl.semaphore_wait(barrier, 5)
+
+    @pl.when((z == 0) | (z == LINE - 1))
+    def _():
+        pl.semaphore_wait(barrier, 4)
+
+
+TILE = 256
+
+
+def feed_kernel(
+    heads,
+    second,
+    cot,
+    we,
+    wo,
+    wc,
+    bias,
+    got,
+    cot_all,
+    we_all,
+    active,
+    grad_expanded,
+    feed_grad,
+    sums,
+    slope,
+    grad_heads,
+    send,
+    recv,
+    token_send,
+    token_recv,
+    local,
+):
+    place = place_here()
+    c, y, x, z = place
+    rows = got.shape[2]
+    tokens = cot.shape[0]
+    ff = we_all.shape[2]
+    half = we.shape[0]
+    own = 4 * y + 2 * x + c
+    other = 4 * (1 - y) + 2 * x + c
+    core = device_at(1 - c, y, x, z)
+    over_x = device_at(c, y, 1 - x, z)
+    over_y = device_at(c, 1 - y, x, z)
+    peers = [lax.rem(z + d, LINE) for d in range(1, LINE)]
+    mine = pl.ds(pl.multiple_of(z * rows, rows), rows)
+    me = (2 * c + y) * 2 + x
+    keeps = [
+        pltpu.make_async_copy(we.at[:, column_block(ff, own * ff)], we_all.at[y], local.at[0]),
+        pltpu.make_async_copy(cot, cot_all.at[me], local.at[1]),
+        pltpu.make_async_copy(heads.at[:, mine], got.at[pl.ds(0, 3), z], local.at[2]),
+    ]
+    for copy in keeps:
+        copy.start()
+    greet([device_at(c, y, x, peer) for peer in peers] + [core, over_x, over_y])
+    tokens_move = TokenExchange(place, token_send, token_recv)
+    weight = tokens_move.go(we.at[:, column_block(ff, other * ff)], we_all.at[y], over_y)
+    tokens_move.start(cot, cot_all)
+    copies = []
+    for index, peer in enumerate(peers):
+        copy = remote(
+            heads.at[:, pl.ds(pl.multiple_of(peer * rows, rows), rows)],
+            got.at[pl.ds(0, 3), z],
+            send.at[0, index],
+            recv.at[0, index],
+            device_at(c, y, x, peer),
+        )
+        copy.start()
+        copies.append(copy)
+    for copy in keeps[:2]:
+        copy.wait()
+    weight.wait_recv()
+    sums[...] = jnp.zeros_like(sums)
+
+    def forward(index, carry):
+        at = pl.ds(pl.multiple_of(index * TILE, TILE), TILE)
+        normed = second[at, :]
+        expanded = (
+            dot_plain(normed[:, :half], we_all[0])
+            + dot_plain(normed[:, half:], we_all[1])
+            + bias[...]
+        )
+        below = 0.5 * (1.0 + lax.erf(expanded * math.sqrt(0.5)))
+        density = jnp.exp(expanded * expanded * -0.5) * (1.0 / math.sqrt(2.0 * math.pi))
+        active[at, :] = (expanded * below).astype(jnp.bfloat16)
+        slope[at, :] = below + expanded * density
+        return carry
+
+    tiles = second.shape[0] // TILE
+    lax.fori_loop(0, tiles // 2, forward, 0)
+    tokens_move.relay()
+    lax.fori_loop(tiles // 2, tiles, forward, 0)
+    tokens_move.relay_corner()
+
+    def backward(block):
+        at = pl.ds(pl.multiple_of(block * tokens, tokens), tokens)
+        cots = cot_all[block]
+        grad_heads[at, :] = dot_rows(cots, wo[...]).astype(jnp.bfloat16)
+        grad = (dot_rows(cots, wc[...]) * slope[at, :]).astype(jnp.bfloat16)
+        grad_expanded[at, :] = grad
+        sums[...] += jnp.sum(grad.astype(jnp.float32), axis=0, keepdims=True)
+
+    ours, theirs = tokens_move.blocks(c), tokens_move.blocks(1 - c)
+    for index in range(4):
+        backward(ours[index])
+    for index in range(4):
+        tokens_move.wait_core(index)
+        backward(theirs[index])
+    for index, peer in enumerate(peers):
+        copy = remote(
+            grad_heads.at[pl.ds(pl.multiple_of(peer * rows, rows), rows)],
+            got.at[3, z],
+            send.at[1, index],
+            recv.at[1, index],
+            device_at(c, y, x, peer),
+        )
+        copy.start()
+        copies.append(copy)
+    last = pltpu.make_async_copy(grad_heads.at[mine], got.at[3, z], local.at[0])
+    last.start()
+    for index in range(2 * half // TILE):
+        block = dot_tokens(second[:, pl.ds(index * TILE, TILE)], grad_expanded[...])
+        side, row = divmod(index * TILE, half)
+        feed_grad[pl.ds(row, TILE), pl.ds(side * ff, ff)] = block.astype(jnp.bfloat16)
+    cots = cot_all[...].reshape(GROUP * tokens, 2 * half)
+    for index in range(ff // TILE):
+        block = dot_tokens(active[:, pl.ds(index * TILE, TILE)], cots)
+        feed_grad[pl.ds(index * TILE, TILE), pl.ds(2 * ff, 2 * half)] = block.astype(jnp.bfloat16)
+    keeps[2].wait()
+    last.wait()
+    for copy in copies:
+        copy.wait()
+    tokens_move.finish()
+
+
+def feed_forward(heads, second, cot, we, wo, wc, bias):
+    rows, width = second.shape
+    ff = we.shape[1] // GROUP
+    lanes = heads.shape[2]
+    vmem = pl.BlockSpec(memory_space=pltpu.VMEM)
+    any_spec = pl.BlockSpec(memory_space=pl.ANY)
+    return pl.pallas_call(
+        feed_kernel,
+        out_shape=(
+            jax.ShapeDtypeStruct((4, LINE, rows // LINE, lanes), heads.dtype),
+            jax.ShapeDtypeStruct((GROUP,) + cot.shape, cot.dtype),
+            jax.ShapeDtypeStruct((2, we.shape[0], ff), we.dtype),
+            jax.ShapeDtypeStruct((rows, ff), jnp.bfloat16),
+            jax.ShapeDtypeStruct((rows, ff), jnp.bfloat16),
+            jax.ShapeDtypeStruct((width // 2, 2 * ff + width), jnp.bfloat16),
+            jax.ShapeDtypeStruct((1, ff), jnp.float32),
+        ),
+        in_specs=[any_spec, vmem, any_spec, any_spec, vmem, vmem, vmem],
+        out_specs=[any_spec] + [vmem] * 6,
+        scratch_shapes=[
+            pltpu.VMEM((rows, ff), jnp.float32),
+            pltpu.VMEM((rows, lanes), jnp.bfloat16),
+            pltpu.SemaphoreType.DMA((2, LINE - 1)),
+            pltpu.SemaphoreType.DMA((2, LINE - 1)),
+            pltpu.SemaphoreType.DMA((12,)),
+            pltpu.SemaphoreType.DMA((12,)),
+            pltpu.SemaphoreType.DMA((3,)),
+        ],
+        compiler_params=pltpu.CompilerParams(
+            collective_id=1, has_side_effects=True, vmem_limit_bytes=56 << 20
+        ),
+        name="feed_forward",
+    )(heads, second, cot, we, wo, wc, bias)
+
+
+class LineReduce:
+    LAG = 2
+
+    def __init__(self, grad, result, inbox, sems, swap, size, place):
+        self.grad, self.result, self.inbox, self.sems, self.swap = grad, result, inbox, sems, swap
+        self.c, self.y, self.x, self.z = place
+        self.size = size
+        self.each = grad.shape[0] // size // 2
+        self.slots = self.each + (LINE - 1) * self.LAG
+
+    def rows(self, chunk):
+        return pl.ds(pl.multiple_of(chunk * self.size, self.size), self.size)
+
+    def lanes(self, which):
+        return pl.ds(pl.multiple_of(which * self.swap, self.swap), self.swap)
+
+    def ahead(self, chunk, half):
+        up = 1 if half == 0 else -1
+        rows = self.rows(chunk)
+        return remote(
+            self.grad.at[rows],
+            self.inbox.at[rows],
+            self.sems.at[0, chunk],
+            self.sems.at[1, chunk],
+            device_at(self.c, self.y, self.x, self.z + up),
+        )
+
+    def across(self, chunk):
+        rows = self.rows(chunk)
+        return remote(
+            self.grad.at[rows, self.lanes(1 - self.y)],
+            self.result.at[rows, self.lanes(self.y)],
+            self.sems.at[2, chunk],
+            self.sems.at[3, chunk],
+            device_at(self.c, 1 - self.y, self.x, self.z),
+        )
+
+    def slot(self, t):
+        for half in range(2):
+            at = self.z if half == 0 else LINE - 1 - self.z
+            step = t - self.LAG * at
+            chunk = jnp.clip(step, 0, self.each - 1) + half * self.each
+
+            @pl.when((step >= 0) & (step < self.each))
+            def _():
+                rows = self.rows(chunk)
+
+                @pl.when(at > 0)
+                def _():
+                    self.ahead(chunk, half).wait_recv()
+                    total = self.grad[rows].astype(jnp.float32) + self.inbox[rows].astype(
+                        jnp.float32
+                    )
+                    self.grad[rows] = total.astype(jnp.bfloat16)
+
+                @pl.when(at < LINE - 1)
+                def _():
+                    self.ahead(chunk, half).start()
+
+                @pl.when(at == LINE - 1)
+                def _():
+                    self.across(chunk).start()
+                    own = self.lanes(self.y)
+                    plain = pl.ds(2 * self.swap, self.grad.shape[1] - 2 * self.swap)
+                    self.result[rows, own] = self.grad[rows, own]
+                    self.result[rows, plain] = self.grad[rows, plain]
+
+    def drain(self):
+        for half in range(2):
+            at = self.z if half == 0 else LINE - 1 - self.z
+
+            def finish(step, carry):
+                chunk = step + half * self.each
+
+                @pl.when(at < LINE - 1)
+                def _():
+                    self.ahead(chunk, half).wait_send()
+
+                @pl.when(at == LINE - 1)
+                def _():
+                    self.across(chunk).wait()
+
+                return carry
+
+            lax.fori_loop(0, self.each, finish, 0)
+
+
+class LineSpread:
+    def __init__(self, result, sems, size, place):
+        self.result, self.sems = result, sems
+        self.c, self.y, self.x, self.z = place
+        self.size = size
+        self.each = result.shape[2] // size // 2
+        self.slots = self.each + LINE
+
+    def move(self, kind, chunk, half):
+        c, y, x, z = self.c, self.y, self.x, self.z
+        up = 1 if half == 0 else -1
+        rows = pl.ds(pl.multiple_of(chunk * self.size, self.size), self.size)
+        side = 1 - x if kind == 3 else x
+        target = (
+            device_at(c, y, x, z - up),
+            device_at(c, y, 1 - x, z),
+            device_at(1 - c, y, x, z),
+            device_at(1 - c, y, x, z),
+        )[kind]
+        part = self.result.at[c, side, rows]
+        return remote(
+            part, part, self.sems.at[2 * kind, chunk], self.sems.at[2 * kind + 1, chunk], target
+        )
+
+    def slot(self, t):
+        for half in range(2):
+            at = self.z if half == 0 else LINE - 1 - self.z
+
+            def event(delay, run):
+                step = t - delay
+                chunk = jnp.clip(step, 0, self.each - 1) + half * self.each
+
+                @pl.when((step >= 0) & (step < self.each))
+                def _():
+                    run(chunk)
+
+            def spread(chunk):
+                @pl.when(at < LINE - 1)
+                def _():
+                    self.move(0, chunk, half).wait_recv()
+
+                @pl.when(at > 0)
+                def _():
+                    self.move(0, chunk, half).start()
+
+                self.move(1, chunk, half).start()
+                self.move(2, chunk, half).start()
+
+            def late(chunk):
+                self.move(1, chunk, half).wait_recv()
+                self.move(3, chunk, half).start()
+
+            event(LINE - 1 - at, spread)
+            event(LINE - at, late)
+
+    def drain(self):
+        for half in range(2):
+            at = self.z if half == 0 else LINE - 1 - self.z
+
+            def finish(step, carry):
+                chunk = step + half * self.each
+
+                @pl.when(at > 0)
+                def _():
+                    self.move(0, chunk, half).wait_send()
+
+                self.move(1, chunk, half).wait_send()
+                self.move(2, chunk, half).wait()
+                self.move(3, chunk, half).wait()
+                return carry
+
+            lax.fori_loop(0, self.each, finish, 0)
+
+
+class LineSum:
+    LAG = 1
+    KINDS = 8
+
+    def __init__(self, grad, result, inbox, sems, swap, size, place):
+        self.grad, self.result, self.inbox, self.sems, self.swap = grad, result, inbox, sems, swap
+        self.c, self.y, self.x, self.z = place
+        self.size = size
+        self.count = grad.shape[0] // size
+        self.split = (self.count + 1) // 2
+        self.slots = self.split + 6 * self.LAG
+
+    def rows(self, chunk):
+        return pl.ds(pl.multiple_of(chunk * self.size, self.size), self.size)
+
+    def moves(self, chunk, half):
+        c, y, x, z = self.c, self.y, self.x, self.z
+        up = 1 if half == 0 else -1
+        rows = self.rows(chunk)
+        grad, result, swap = self.grad, self.result, self.swap
+        mine = result.at[c, x, rows]
+        beside = result.at[c, 1 - x, rows]
+        lower, upper = device_at(c, y, x, z - up), device_at(c, y, x, z + up)
+
+        def lanes(which):
+            return pl.ds(pl.multiple_of(which * swap, swap), swap)
+
+        makers = {
+            "near": (0, lambda: (grad.at[rows], self.inbox.at[0, rows], upper)),
+            "far": (1, lambda: (grad.at[rows], self.inbox.at[1, rows], lower)),
+            "swap": (
+                2,
+                lambda: (
+                    grad.at[rows, lanes(1 - y)],
+                    result.at[c, x, rows, lanes(y)],
+                    device_at(c, 1 - y, x, z),
+                ),
+            ),
+            "down": (3, lambda: (mine, mine, lower)),
+            "out": (4, lambda: (mine, mine, upper)),
+            "side": (5, lambda: (mine, mine, device_at(c, y, 1 - x, z))),
+            "core": (6, lambda: (mine, mine, device_at(1 - c, y, x, z))),
+            "late": (7, lambda: (beside, beside, device_at(1 - c, y, x, z))),
+        }
+
+        def make(name):
+            kind, parts = makers[name]
+            src, dst, target = parts()
+            return remote(
+                src, dst, self.sems.at[2 * kind, chunk], self.sems.at[2 * kind + 1, chunk], target
+            )
+
+        return make
+
+    def slot(self, t):
+        for half in range(2):
+            self.half_slot(t, half)
+
+    def extent(self, half):
+        size = self.split if half == 0 else self.count - self.split
+        base = 0 if half == 0 else self.split
+        at = self.z if half == 0 else LINE - 1 - self.z
+        return (size, base, at)
+
+    def half_slot(self, t, half):
+        size, base, at = self.extent(half)
+        lag = self.LAG
+        swap = self.swap
+        owner = at == 1
+
+        def event(delay, run):
+            chunk = t - delay
+            index = jnp.clip(chunk, 0, size - 1) + base
+
+            @pl.when((chunk >= 0) & (chunk < size))
+            def _():
+                run(index, self.moves(index, half))
+
+        def reduce(index, moves):
+            rows = self.rows(index)
+
+            @pl.when(at == 0)
+            def _():
+                moves("near").start()
+
+            @pl.when(at == 2)
+            def _():
+                moves("far").wait_recv()
+                total = self.grad[rows].astype(jnp.float32) + self.inbox[1, rows].astype(
+                    jnp.float32
+                )
+                self.grad[rows] = total.astype(jnp.bfloat16)
+
+            @pl.when(at >= 2)
+            def _():
+                moves("far").start()
+
+            @pl.when(owner)
+            def _():
+                moves("near").wait_recv()
+                moves("far").wait_recv()
+                total = (
+                    self.grad[rows].astype(jnp.float32)
+                    + self.inbox[0, rows].astype(jnp.float32)
+                    + self.inbox[1, rows].astype(jnp.float32)
+                )
+                self.grad[rows] = total.astype(jnp.bfloat16)
+                moves("swap").start()
+                own = pl.ds(pl.multiple_of(self.y * swap, swap), swap)
+                plain = pl.ds(2 * swap, self.grad.shape[1] - 2 * swap)
+                self.result[self.c, self.x, rows, own] = self.grad[rows, own]
+                self.result[self.c, self.x, rows, plain] = self.grad[rows, plain]
+
+        event(jnp.where(owner, 2 * lag, jnp.where(at == 2, lag, 0)), reduce)
+
+        def spread(index, moves):
+            @pl.when(owner)
+            def _():
+                moves("swap").wait_recv()
+                moves("down").start()
+
+            @pl.when(at == 0)
+            def _():
+                moves("down").wait_recv()
+
+            @pl.when(at >= 2)
+            def _():
+                moves("out").wait_recv()
+
+            @pl.when((at == 1) | (at == 2))
+            def _():
+                moves("out").start()
+
+            moves("side").start()
+            moves("core").start()
+
+        wait = jnp.where(owner, 3 * lag, jnp.where(at == 3, 5 * lag, 4 * lag))
+        event(wait, spread)
+
+        def late(index, moves):
+            moves("side").wait_recv()
+            moves("late").start()
+
+        event(wait + lag, late)
+
+    def drain(self):
+        for half in range(2):
+            size, base, at = self.extent(half)
+
+            def finish(chunk, carry):
+                moves = self.moves(chunk + base, half)
+
+                @pl.when(at == 0)
+                def _():
+                    moves("near").wait_send()
+
+                @pl.when(at >= 2)
+                def _():
+                    moves("far").wait_send()
+
+                @pl.when(at == 1)
+                def _():
+                    moves("swap").wait_send()
+                    moves("down").wait_send()
+
+                @pl.when((at == 1) | (at == 2))
+                def _():
+                    moves("out").wait_send()
+
+                moves("side").wait_send()
+                moves("core").wait()
+                moves("late").wait()
+                return carry
+
+            lax.fori_loop(0, size, finish, 0)
+
+
+def attention_kernel(
+    ints,
+    parts,
+    unit_cos,
+    unit_sin,
+    row_cos,
+    row_sin,
+    feed_grad,
+    out,
+    feed_sum,
+    masked,
+    flat,
+    scores,
+    slopes,
+    key_sum,
+    value_sum,
+    mixed_sum,
+    query_sum,
+    feed_own,
+    feed_inbox,
+    feed_sems,
+    local,
+    *,
+    units,
+    pieces,
+    swap,
+):
+    here = place_here()
+    greet_line(here)
+    load = pltpu.make_async_copy(feed_grad, feed_own, local)
+    load.start()
+    line = LineReduce(feed_own, feed_sum, feed_inbox, feed_sems, swap, FEED_CHUNK, here)
+    length = parts.shape[1]
+    scale = 1.0 / math.sqrt(HEAD)
+    blocks = length // SPAN
+    lanes = lax.broadcasted_iota(jnp.int32, (UNIT, 2 * HEAD), 1)
+    lower = lanes < HEAD
+
+    def arrange(index, carry):
+        at = pl.ds(pl.multiple_of(index * UNIT, UNIT), UNIT)
+        for which in range(4):
+            rows = jnp.zeros((UNIT, 2 * HEAD), jnp.bfloat16)
+            for unit in range(units):
+                rows = jnp.where(
+                    ints[0, unit] == index, parts[which, pl.ds(unit * UNIT, UNIT), :], rows
+                )
+            rows = rows.astype(jnp.float32)
+            if which == 0:
+                rows = rows * scale
+            masked[which, 0, at, :] = jnp.where(lower, rows, 0.0).astype(jnp.bfloat16)
+            masked[which, 1, at, :] = jnp.where(lower, 0.0, rows).astype(jnp.bfloat16)
+            flat[which, :, at] = rows.T.astype(jnp.bfloat16)
+        return carry
+
+    lax.fori_loop(0, units, arrange, 0)
+    load.wait()
+    key_sum[...] = jnp.zeros_like(key_sum)
+    value_sum[...] = jnp.zeros_like(value_sum)
+
+    def labels(positions):
+        found = jnp.full(positions.shape, -1, jnp.int32)
+        for piece in range(pieces):
+            start = ints[0, units + piece]
+            found = jnp.where(
+                (positions >= start) & (positions < start + PIECE), piece, found
+            )
+        return found
+
+    def dot(a, b):
+        return jnp.dot(a, b, preferred_element_type=jnp.float32)
+
+    for block in range(blocks):
+        begin = block * SPAN
+        last = SPAN + (UNIT if block + 1 < blocks else 0)
+        columns = pl.ds(begin, SPAN)
+        row_at = begin + lax.broadcasted_iota(jnp.int32, (1, SPAN), 1)
+        col_at = begin + lax.broadcasted_iota(jnp.int32, (last, 1), 0)
+        row_lab = labels(row_at)
+        col_lab = labels(col_at)
+        allowed = (col_at <= row_at) | (
+            (col_lab == row_lab) & (row_lab >= 0)
+        )
+
+        def one_head(head, carry):
+            slot = 3 * (2 * block + head)
+            line.slot(slot)
+            queries = flat[0, :, columns]
+            grads = flat[3, :, columns]
+            side = pl.ds(pl.multiple_of(head * HEAD, HEAD), HEAD)
+
+            def score_tile(start, size, top, mask):
+                rows = pl.ds(start, size)
+                tile = dot(masked[1, head, rows, :], queries)
+                if mask is not None:
+                    tile = jnp.where(mask, tile, NEGATIVE)
+                scores[rows, :] = tile
+                return jnp.maximum(top, jnp.max(tile, axis=0, keepdims=True))
+
+            top = lax.fori_loop(
+                0,
+                block,
+                lambda j, top: score_tile(pl.multiple_of(j * SPAN, SPAN), SPAN, top, None),
+                jnp.full((1, SPAN), NEGATIVE, jnp.float32),
+            )
+            top = score_tile(begin, last, top, allowed)
+
+            def weight_tile(start, size, sums):
+                total, delta = sums
+                rows = pl.ds(start, size)
+                weights = jnp.exp(scores[rows, :] - top)
+                slope = dot(masked[2, head, rows, :], grads)
+                scores[rows, :] = weights
+                slopes[rows, :] = slope
+                return (
+                    total + jnp.sum(weights, axis=0, keepdims=True),
+                    delta + jnp.sum(weights * slope, axis=0, keepdims=True),
+                )
+
+            line.slot(slot + 1)
+            zero = jnp.zeros((1, SPAN), jnp.float32)
+            sums = lax.fori_loop(
+                0,
+                block,
+                lambda j, sums: weight_tile(pl.multiple_of(j * SPAN, SPAN), SPAN, sums),
+                (zero, zero),
+            )
+            total, delta = weight_tile(begin, last, sums)
+            inverse = 1.0 / total
+            delta = delta * inverse
+
+            def grad_tile(start, size, sums):
+                mixed, query = sums
+                rows = pl.ds(start, size)
+                probs = scores[rows, :] * inverse
+                grad = (probs * (slopes[rows, :] - delta)).astype(jnp.bfloat16)
+                probs = probs.astype(jnp.bfloat16)
+                value_sum[rows, :] += dot(probs, masked[3, head, columns, :])
+                key_sum[rows, :] += dot(grad, masked[0, head, columns, :])
+                mixed = mixed + dot(flat[2, side, rows], probs)
+                query = query + dot(flat[1, side, rows], grad)
+                return (mixed, query)
+
+            line.slot(slot + 2)
+            none = jnp.zeros((HEAD, SPAN), jnp.float32)
+            sums = lax.fori_loop(
+                0,
+                block,
+                lambda j, sums: grad_tile(pl.multiple_of(j * SPAN, SPAN), SPAN, sums),
+                (none, none),
+            )
+            mixed, query = grad_tile(begin, last, sums)
+            mixed_sum[side, columns] = mixed
+            query_sum[side, columns] = query * scale
+            return carry
+
+        lax.fori_loop(0, 2, one_head, 0)
+
+    lane = lax.rem(lax.broadcasted_iota(jnp.int32, row_cos.shape, 1), HEAD)
+
+    def finish(index, carry):
+        at = pl.ds(pl.multiple_of(index * UNIT, UNIT), UNIT)
+        base_cos, base_sin = unit_cos[pl.ds(index, 1), :], unit_sin[pl.ds(index, 1), :]
+        cosine = base_cos * row_cos[...] - base_sin * row_sin[...]
+        sine = base_sin * row_cos[...] + base_cos * row_sin[...]
+        sine_up = jnp.where(lane < HALF, sine, 0.0)
+        sine_down = jnp.where(lane < HALF, 0.0, sine)
+
+        def turn_back(rows):
+            up = pltpu.roll(rows, 2 * HEAD - HALF, 1)
+            down = pltpu.roll(rows, HALF, 1)
+            return rows * cosine + up * sine_up - down * sine_down
+
+        masked[0, 0, at, :] = mixed_sum[:, at].T.astype(jnp.bfloat16)
+        masked[1, 0, at, :] = turn_back(query_sum[:, at].T).astype(jnp.bfloat16)
+        masked[2, 0, at, :] = turn_back(key_sum[at, :]).astype(jnp.bfloat16)
+        masked[3, 0, at, :] = value_sum[at, :].astype(jnp.bfloat16)
+        return carry
+
+    lax.fori_loop(0, units, finish, 0)
+
+    def restore(index, carry):
+        here = pl.ds(pl.multiple_of(index * UNIT, UNIT), UNIT)
+        for which in range(4):
+            rows = jnp.zeros((UNIT, 2 * HEAD), jnp.bfloat16)
+            for unit in range(units):
+                rows = jnp.where(
+                    ints[0, index] == unit, masked[which, 0, pl.ds(unit * UNIT, UNIT), :], rows
+                )
+            out[which, here, :] = rows
+        return carry
+
+    lax.fori_loop(0, units, restore, 0)
+
+    def more(slot, carry):
+        line.slot(slot)
+        return carry
+
+    lax.fori_loop(6 * blocks, max(line.slots, 6 * blocks), more, 0)
+    line.drain()
+
+
+def attend(ints, parts, tables, feed_grad, units, pieces, swap):
+    length = parts.shape[1]
+    vmem = pl.BlockSpec(memory_space=pltpu.VMEM)
+    return pl.pallas_call(
+        functools.partial(attention_kernel, units=units, pieces=pieces, swap=swap),
+        out_shape=(
+            jax.ShapeDtypeStruct(parts.shape, parts.dtype),
+            jax.ShapeDtypeStruct(feed_grad.shape, feed_grad.dtype),
+        ),
+        in_specs=[pl.BlockSpec(memory_space=pltpu.SMEM)]
+        + [vmem] * 5
+        + [pl.BlockSpec(memory_space=pl.ANY)],
+        out_specs=[vmem, vmem],
+        scratch_shapes=[
+            pltpu.VMEM((4, 2, length, 2 * HEAD), jnp.bfloat16),
+            pltpu.VMEM((4, 2 * HEAD, length), jnp.bfloat16),
+            pltpu.VMEM((length, SPAN), jnp.float32),
+            pltpu.VMEM((length, SPAN), jnp.float32),
+            pltpu.VMEM((length, 2 * HEAD), jnp.float32),
+            pltpu.VMEM((length, 2 * HEAD), jnp.float32),
+            pltpu.VMEM((2 * HEAD, length), jnp.float32),
+            pltpu.VMEM((2 * HEAD, length), jnp.float32),
+            pltpu.VMEM(feed_grad.shape, jnp.bfloat16),
+            pltpu.VMEM(feed_grad.shape, jnp.bfloat16),
+            pltpu.SemaphoreType.DMA((4, feed_grad.shape[0] // FEED_CHUNK)),
+            pltpu.SemaphoreType.DMA,
+        ],
+        compiler_params=pltpu.CompilerParams(
+            collective_id=2, has_side_effects=True, vmem_limit_bytes=56 << 20
+        ),
+        name="attend",
+    )(ints, parts, *tables, feed_grad)
+
+
+def close_kernel(
+    done,
+    active,
+    grad_expanded,
+    we,
+    wc,
+    wm,
+    wo,
+    hidden,
+    cots,
+    vectors,
+    feed_sums,
+    feed_sum,
+    attn_all,
+    feed_all,
+    out_sum,
+    term_sum,
+    parts,
+    first,
+    stats,
+    outs,
+    terms,
+    attn_own,
+    attn_inbox,
+    near,
+    four,
+    mid,
+    two,
+    far,
+    totals,
+    send,
+    recv,
+    attn_sems,
+    feed_sems,
+    sems,
+    local,
+    *,
+    swap,
+):
+    place = place_here()
+    c, y, x, z = place
+    core = device_at(1 - c, y, x, z)
+    over_x = device_at(c, y, 1 - x, z)
+    over_y = device_at(c, 1 - y, x, z)
+    barrier = pltpu.get_barrier_semaphore()
+    peers = [lax.rem(z + d, LINE) for d in range(1, LINE)]
+    partners = [device_at(c, y, x, peer) for peer in peers] + [core, over_x, over_y]
+    for partner in partners:
+        pl.semaphore_signal(barrier, inc=1, device_id=partner, device_id_type=MESH)
+    pl.semaphore_wait(barrier, len(partners))
+    rows = done.shape[2]
+    lanes = done.shape[3]
+    mine = pl.ds(pl.multiple_of(z * rows, rows), rows)
+    copies = []
+    for index, peer in enumerate(peers):
+        for which in (1, 2, 3, 0):
+            copy = remote(
+                done.at[which, peer],
+                parts.at[mine, pl.ds(which * lanes, lanes)],
+                send.at[index, which],
+                recv.at[index, which],
+                device_at(c, y, x, peer),
+            )
+            copy.start()
+            copies.append(copy)
+    owns = []
+    for which in range(4):
+        copy = pltpu.make_async_copy(
+            done.at[which, z], parts.at[mine, pl.ds(which * lanes, lanes)], local.at[which]
+        )
+        copy.start()
+        owns.append(copy)
+    spread = LineSpread(feed_all, feed_sems, CHUNK, place)
+    own_half = CHUNK * spread.each
+
+    @pl.when((z == 0) | (z == LINE - 1))
+    def _():
+        at = pl.ds(pl.multiple_of(jnp.where(z == 0, own_half, 0), own_half), own_half)
+        copy = pltpu.make_async_copy(feed_sum.at[at], feed_all.at[c, x, at], local.at[4])
+        copy.start()
+        copy.wait()
+
+    gain_one, shift_one, gain_two = vectors[0:1, :], vectors[1:2, :], vectors[2:3, :]
+    width = hidden.shape[1]
+    half = width // 2
+    tokens = outs.shape[1]
+    totals[...] = jnp.zeros_like(totals)
+
+    def normed(at, mean, rstd):
+        return (hidden[at, :].astype(jnp.float32) - mean) * rstd
+
+    def before(index, carry):
+        spread.slot(index)
+        at = pl.ds(pl.multiple_of(index * TILE, TILE), TILE)
+        raw = hidden[at, :].astype(jnp.float32)
+        mean = jnp.mean(raw, axis=1, keepdims=True)
+        centred = raw - mean
+        rstd = lax.rsqrt(jnp.mean(centred * centred, axis=1, keepdims=True) + EPS)
+        stats[0, at, :] = jnp.broadcast_to(mean, (TILE, stats.shape[2]))
+        stats[1, at, :] = jnp.broadcast_to(rstd, (TILE, stats.shape[2]))
+        xhat = centred * rstd
+        first[at, :] = (xhat * gain_one + shift_one).astype(jnp.bfloat16)
+        grad_second = dot_rows(grad_expanded[at, :], we[...])
+        terms[index] = (grad_second * gain_two).astype(jnp.bfloat16)
+        outs[index] = dot_plain(active[at, :], wc[...]).astype(jnp.bfloat16)
+        totals[2:3, :] += jnp.sum(grad_second * xhat, axis=0, keepdims=True)
+        totals[3:4, :] += jnp.sum(grad_second, axis=0, keepdims=True)
+        totals[4:5, :] += jnp.sum(cots[at, :].astype(jnp.float32), axis=0, keepdims=True)
+        return carry
+
+    shown = hidden.shape[0] // TILE
+    lax.fori_loop(0, shown, before, 0)
+
+    def spread_rest(t, carry):
+        spread.slot(t)
+        return carry
+
+    lax.fori_loop(shown, spread.slots, spread_rest, 0)
+    for copy in owns:
+        copy.wait()
+    for copy in copies:
+        copy.wait()
+
+    def after(index, carry):
+        at = pl.ds(pl.multiple_of(index * TILE, TILE), TILE)
+        grads = parts[at, pl.ds(lanes, 3 * lanes)]
+        grad_first = dot_rows(grads, wm[...])
+        xhat = normed(at, stats[0, at, 0:1], stats[1, at, 0:1])
+        terms[index] = (terms[index].astype(jnp.float32) + grad_first * gain_one).astype(
+            jnp.bfloat16
+        )
+        outs[index] = (
+            outs[index].astype(jnp.float32) + dot_plain(parts[at, pl.ds(0, lanes)], wo[...])
+        ).astype(jnp.bfloat16)
+        totals[0:1, :] += jnp.sum(grad_first * xhat, axis=0, keepdims=True)
+        totals[1:2, :] += jnp.sum(grad_first, axis=0, keepdims=True)
+        totals[5:6, pl.ds(0, 3 * lanes)] += jnp.sum(
+            grads.astype(jnp.float32), axis=0, keepdims=True
+        )
+        return carry
+
+    lax.fori_loop(0, hidden.shape[0] // TILE, after, 0)
+    arrays = (outs, terms)
+    nears = []
+    for a in range(2):
+        copy = remote(
+            arrays[a].at[pl.ds(pl.multiple_of(4 * (1 - c), 4), 4)],
+            near.at[a],
+            sems.at[0, a],
+            sems.at[1, a],
+            core,
+        )
+        copy.start()
+        nears.append(copy)
+    for index in range(width // TILE):
+        block = dot_tokens(first[:, pl.ds(index * TILE, TILE)], parts[:, pl.ds(lanes, 3 * lanes)])
+        side, row = divmod(index * TILE, half)
+        attn_own[pl.ds(row, TILE), pl.ds(side * swap, swap)] = block.astype(jnp.bfloat16)
+    block = dot_tokens(parts[:, pl.ds(0, lanes)], cots[...]).astype(jnp.bfloat16)
+    wide = 2 * lanes
+    for index in range(width // wide):
+        attn_own[pl.ds(index * lanes, lanes), pl.ds(2 * swap, wide)] = block[
+            :, index * wide : (index + 1) * wide
+        ]
+    lines = []
+    fill = jnp.zeros((1, swap), jnp.float32)
+    for index in range(5):
+        for begin in range(0, width, swap):
+            stop = min(begin + swap, width)
+            line = totals[index : index + 1, begin:stop]
+            if stop - begin < swap:
+                line = jnp.concatenate([line, fill[:, : swap - (stop - begin)]], axis=1)
+            lines.append(line)
+    lines.append(totals[5:6, 0:swap])
+    ff = feed_sums.shape[1]
+    for begin in range(0, ff, swap):
+        stop = min(begin + swap, ff)
+        line = feed_sums[:, begin:stop]
+        if stop - begin < swap:
+            line = jnp.concatenate([line, fill[:, : swap - (stop - begin)]], axis=1)
+        lines.append(line)
+    lines += [fill] * (attn_own.shape[0] - half - len(lines))
+    small = jnp.concatenate(lines, axis=0).astype(jnp.bfloat16)
+    tail = pl.ds(half, attn_own.shape[0] - half)
+    attn_own[tail, pl.ds(0, swap)] = small
+    attn_own[tail, pl.ds(swap, swap)] = small
+    attn_own[tail, pl.ds(2 * swap, wide)] = jnp.zeros((small.shape[0], wide), jnp.bfloat16)
+
+    attn = LineSum(attn_own, attn_all, attn_inbox, attn_sems, swap, CHUNK, place)
+
+    def step(t, carry):
+        attn.slot(t)
+        return carry
+
+    lax.fori_loop(0, 2, step, 0)
+    mids = []
+    for a in range(2):
+        nears[a].wait()
+        for j in range(4):
+            total = arrays[a][4 * c + j].astype(jnp.float32) + near[a, j].astype(jnp.float32)
+            if a == 0:
+                four[a, j % 2, j // 2] = total.astype(jnp.bfloat16)
+            else:
+                four[a, j // 2, j % 2] = total.astype(jnp.bfloat16)
+        copy = remote(
+            four.at[a, 1 - x if a == 0 else 1 - y],
+            mid.at[a],
+            sems.at[0, 2 + a],
+            sems.at[1, 2 + a],
+            over_x if a == 0 else over_y,
+        )
+        copy.start()
+        mids.append(copy)
+    lax.fori_loop(2, 9, step, 0)
+    fars = []
+    for a in range(2):
+        mids[a].wait()
+        mine_at, away = (x, y) if a == 0 else (y, x)
+        two[a] = (
+            four[a, mine_at, 1 - away].astype(jnp.float32) + mid[a, 1 - away].astype(jnp.float32)
+        ).astype(jnp.bfloat16)
+        copy = remote(
+            two.at[a],
+            far.at[a],
+            sems.at[0, 4 + a],
+            sems.at[1, 4 + a],
+            over_y if a == 0 else over_x,
+        )
+        copy.start()
+        fars.append(copy)
+    lax.fori_loop(9, attn.slots, step, 0)
+    for a, dst in enumerate((out_sum, term_sum)):
+        fars[a].wait()
+        mine_at, away = (x, y) if a == 0 else (y, x)
+        dst[...] = (
+            four[a, mine_at, away].astype(jnp.float32)
+            + mid[a, away].astype(jnp.float32)
+            + far[a].astype(jnp.float32)
+        )
+    attn.drain()
+    spread.drain()
+
+
+def close(
+    done,
+    active,
+    grad_expanded,
+    we,
+    wc,
+    wm,
+    wo,
+    hidden,
+    cots,
+    vectors,
+    feed_sums,
+    feed_sum,
+    tokens,
+):
+    rows, width = hidden.shape
+    lanes = done.shape[3]
+    swap = 3 * lanes
+    block = (tokens, width)
+    vmem = pl.BlockSpec(memory_space=pltpu.VMEM)
+    any_spec = pl.BlockSpec(memory_space=pl.ANY)
+    grad_shape = (width // 2 + CHUNK, 2 * swap + 2 * lanes)
+    scratch = [
+        pltpu.VMEM((rows, 4 * lanes), jnp.bfloat16),
+        pltpu.VMEM((rows, width), jnp.bfloat16),
+        pltpu.VMEM((2, rows, 128), jnp.float32),
+        pltpu.VMEM((GROUP,) + block, jnp.bfloat16),
+        pltpu.VMEM((GROUP,) + block, jnp.bfloat16),
+        pltpu.VMEM(grad_shape, jnp.bfloat16),
+        pltpu.VMEM((2,) + grad_shape, jnp.bfloat16),
+        pltpu.VMEM((2, 4) + block, jnp.bfloat16),
+        pltpu.VMEM((2, 2, 2) + block, jnp.bfloat16),
+        pltpu.VMEM((2, 2) + block, jnp.bfloat16),
+        pltpu.VMEM((2,) + block, jnp.bfloat16),
+        pltpu.VMEM((2,) + block, jnp.bfloat16),
+        pltpu.VMEM((8, width), jnp.float32),
+        pltpu.SemaphoreType.DMA((LINE - 1, 4)),
+        pltpu.SemaphoreType.DMA((LINE - 1, 4)),
+        pltpu.SemaphoreType.DMA((2 * LineSum.KINDS, grad_shape[0] // CHUNK)),
+        pltpu.SemaphoreType.DMA((8, feed_sum.shape[0] // CHUNK)),
+        pltpu.SemaphoreType.DMA((2, 6)),
+        pltpu.SemaphoreType.DMA((5,)),
+    ]
+    return pl.pallas_call(
+        functools.partial(close_kernel, swap=swap),
+        out_shape=(
+            jax.ShapeDtypeStruct((2, 2) + grad_shape, jnp.bfloat16),
+            jax.ShapeDtypeStruct((2, 2) + feed_sum.shape, jnp.bfloat16),
+            jax.ShapeDtypeStruct(block, jnp.float32),
+            jax.ShapeDtypeStruct(block, jnp.float32),
+        ),
+        in_specs=[any_spec] + [vmem] * 10 + [any_spec],
+        out_specs=[vmem, any_spec, vmem, vmem],
+        scratch_shapes=scratch,
+        compiler_params=pltpu.CompilerParams(
+            collective_id=3, has_side_effects=True, vmem_limit_bytes=60 << 20
+        ),
+        name="close",
+    )(
+        done, active, grad_expanded, we, wc, wm, wo, hidden, cots, vectors, feed_sums, feed_sum
+    )
+
+
+def widen_kernel(
+    feed_all,
+    attn_all,
+    expand,
+    contract,
+    merged,
+    output,
+    feed,
+    attn,
+    expand_wide,
+    contract_wide,
+    merged_wide,
+    output_wide,
+    loads,
+    stores,
+    *,
+    swap,
+    lanes,
+    ff,
+):
+    half = feed.shape[2]
+    gets = []
+    for index, (src, dst) in enumerate(((feed_all, feed), (attn_all, attn))):
+        for part in range(4):
+            copy = pltpu.make_async_copy(
+                src.at[part // 2, part % 2], dst.at[part // 2, part % 2], loads.at[index, part]
+            )
+            copy.start()
+            gets.append(copy)
+    puts = []
+
+    def put(src, dst):
+        copy = pltpu.make_async_copy(src, dst, stores.at[len(puts)])
+        copy.start()
+        puts.append(copy)
+
+    for part in range(4):
+        c, x = part // 2, part % 2
+        gets[part].wait()
+        for y in range(2):
+            at = pl.ds((4 * y + 2 * x + c) * ff, ff)
+            expand_wide[:, at] = feed[c, x, :, pl.ds(y * ff, ff)].astype(jnp.float32)
+            put(expand_wide.at[:, at], expand.at[:, at])
+        at = pl.ds((2 * x + c) * ff, ff)
+        contract_wide[at, :] = feed[c, x, :, pl.ds(2 * ff, 2 * half)].astype(jnp.float32)
+        put(contract_wide.at[at], contract.at[at])
+    for copy in gets[4:]:
+        copy.wait()
+    width = 2 * half
+    for j in range(3):
+        for octant in range(GROUP):
+            c, x, y = octant % 2, octant // 2 % 2, octant // 4
+            at = pl.ds(j * width + octant * lanes, lanes)
+            merged_wide[:, at] = attn[
+                c, x, pl.ds(0, half), pl.ds(y * swap + j * lanes, lanes)
+            ].astype(jnp.float32)
+        at = pl.ds(j * width, width)
+        put(merged_wide.at[:, at], merged.at[:, at])
+    for part in range(4):
+        c, x = part % 2, part // 2
+        for index in range(half // lanes):
+            output_wide[pl.ds(part * lanes, lanes), pl.ds(2 * lanes * index, 2 * lanes)] = attn[
+                c, x, pl.ds(index * lanes, lanes), pl.ds(2 * swap, 2 * lanes)
+            ].astype(jnp.float32)
+    put(output_wide, output)
+    for copy in puts:
+        copy.wait()
+
+
+def widen(feed_all, attn_all, swap, lanes, ff):
+    half = feed_all.shape[2]
+    width = 2 * half
+    shapes = ((half, GROUP * ff), (4 * ff, width), (half, 3 * width), (4 * lanes, width))
+    any_spec = pl.BlockSpec(memory_space=pl.ANY)
+    return pl.pallas_call(
+        functools.partial(widen_kernel, swap=swap, lanes=lanes, ff=ff),
+        out_shape=tuple(jax.ShapeDtypeStruct(shape, jnp.float32) for shape in shapes),
+        in_specs=[any_spec] * 2,
+        out_specs=[any_spec] * 4,
+        scratch_shapes=[
+            pltpu.VMEM(feed_all.shape, jnp.bfloat16),
+            pltpu.VMEM(attn_all.shape, jnp.bfloat16),
+        ]
+        + [pltpu.VMEM(shape, jnp.float32) for shape in shapes]
+        + [pltpu.SemaphoreType.DMA((2, 4)), pltpu.SemaphoreType.DMA((16,))],
+        compiler_params=pltpu.CompilerParams(vmem_limit_bytes=48 << 20),
+        name="widen",
+    )(feed_all, attn_all)
+
+
+def turn_tables(positions, lanes):
+    lane = jnp.arange(lanes, dtype=jnp.int32) % HEAD
+    inverse = jnp.exp((lane % HALF).astype(jnp.float32) * (-2.0 * math.log(10000.0) / ROT))
+    angles = positions.astype(jnp.float32)[:, None] * inverse[None, :]
+    turned = lane[None, :] < ROT
+    return (jnp.where(turned, jnp.cos(angles), 1.0), jnp.where(turned, jnp.sin(angles), 0.0))
+
+
+def group_body(
+    hidden_states,
+    unit_order,
+    piece_starts,
+    first_gain,
+    first_shift,
+    second_gain,
+    second_shift,
+    merged_weight,
+    merged_bias,
+    output_weight,
+    output_bias,
+    expand_weight,
+    expand_bias,
+    contract_weight,
+    contract_bias,
+    out_cotangent,
+):
+    c, y, x, z = place_here()
+    tokens, width = hidden_states.shape[1:]
+    length = tokens * 2 * LINE
+    units = unit_order.shape[1]
+    pieces = piece_starts.shape[1]
+    rows = GROUP * tokens
+    part = width // GROUP
+    ff_part = expand_weight.shape[1] // GROUP
+    half = width // 2
+    vectors = (
+        first_gain,
+        first_shift,
+        second_gain,
+        second_shift,
+        merged_bias,
+        output_bias,
+        expand_bias,
+        contract_bias,
+    )
+    sizes = [v.shape[0] for v in vectors]
+    packed = jnp.concatenate(vectors).astype(jnp.float32).reshape(-1, 128)
+    ints = jnp.concatenate([unit_order[0], piece_starts[0]])
+    ints = jnp.broadcast_to(jnp.pad(ints, (0, 128 - ints.shape[0]))[None], (8, 128))
+    tables = turn_tables(jnp.arange(units, dtype=jnp.int32) * UNIT, part) + turn_tables(
+        jnp.arange(UNIT, dtype=jnp.int32), part
+    )
+    hid_all, ints_all, vec_all, wm_all, heads, second = enter(
+        hidden_states[0], ints, packed, merged_weight, tables
+    )
+    inner = 2 * x + c
+    wo = lax.dynamic_slice_in_dim(output_weight, inner * part, part, 0)
+    wc = lax.dynamic_slice_in_dim(contract_weight, inner * ff_part, ff_part, 0)
+    own_expand = lax.dynamic_slice_in_dim(expand_bias, inner * ff_part, ff_part, 0)
+    got, cot_all, we_all, active, grad_expanded, feed_grad, feed_sums = feed_forward(
+        heads,
+        second,
+        out_cotangent[0],
+        expand_weight,
+        wo,
+        wc,
+        own_expand.astype(jnp.float32)[None],
+    )
+    vec_all = vec_all.reshape(2, -1)
+    whole = []
+    at = 0
+    for size in sizes:
+        whole.append(vec_all[:, at : at + size].reshape(-1))
+        at += size
+    gain_one, shift_one, gain_two, shift_two, bias_merged, bias_out, bias_expand, bias_contract = whole
+    wm = wm_all.reshape(width, 3 * part)
+    we = we_all.reshape(width, ff_part)
+    cots = cot_all.reshape(rows, width)
+    own_ints = lax.dynamic_index_in_dim(ints_all[:, 0], z, 0, keepdims=True)
+    done, feed_sum = attend(
+        own_ints,
+        got.reshape(4, length, part),
+        tables,
+        feed_grad,
+        units,
+        pieces,
+        ff_part,
+    )
+    swap = 3 * part
+    lines = CHUNK
+    attn_all, feed_all, out_sum, term_sum = close(
+        done.reshape(4, LINE, 2 * tokens, part),
+        active,
+        grad_expanded,
+        we,
+        wc,
+        wm,
+        wo,
+        hid_all.reshape(rows, width),
+        cots,
+        jnp.stack([gain_one, shift_one, gain_two]),
+        feed_sums,
+        feed_sum,
+        tokens,
+    )
+    expand_out, contract_out, merged_out, output_out = widen(
+        feed_all, attn_all, swap, part, ff_part
+    )
+    own_hidden = hidden_states[0].astype(jnp.float32)
+    own_mean = jnp.mean(own_hidden, axis=1, keepdims=True)
+    own_centred = own_hidden - own_mean
+    own_rstd = lax.rsqrt(jnp.mean(own_centred * own_centred, axis=1, keepdims=True) + EPS)
+    own_xhat = own_centred * own_rstd
+    output = (own_hidden + out_sum + bias_out + bias_contract).astype(jnp.bfloat16)
+    upstream = out_cotangent[0].astype(jnp.float32)
+    input_gradient = upstream + own_rstd * (
+        term_sum
+        - jnp.mean(term_sum, axis=1, keepdims=True)
+        - own_xhat * jnp.mean(term_sum * own_xhat, axis=1, keepdims=True)
+    )
+
+    sums = attn_all[:, :, half : half + lines, : 2 * swap].astype(jnp.float32)
+    sums = sums.reshape(2, 2, lines, 2, swap).transpose(3, 1, 0, 2, 4).reshape(GROUP, lines, swap)
+    per = -(-width // swap)
+    shared = jnp.sum(sums[:, : 4 * per], axis=0).reshape(4, per * swap)[:, :width]
+    row_total = sums[0, 4 * per : 5 * per].reshape(-1)[:width]
+    merged_sums = sums[:, 5 * per].reshape(GROUP, 3, part).transpose(1, 0, 2).reshape(-1)
+    expand_sums = sums[:, 5 * per + 1 : 5 * per + 1 - (-ff_part // swap)]
+    expand_sums = expand_sums.reshape(GROUP, -1)[:, :ff_part].reshape(-1)
+
+    def own_half(vector):
+        size = vector.shape[0] // 2
+        return lax.dynamic_slice_in_dim(vector, y * size, size, 0)
+
+    row_total = own_half(row_total)
+    return (
+        output[None],
+        input_gradient[None],
+        own_half(shared[0]),
+        own_half(shared[1]),
+        own_half(shared[2]),
+        own_half(shared[3]),
+        merged_out,
+        own_half(merged_sums),
+        output_out,
+        row_total,
+        expand_out,
+        own_half(expand_sums),
+        contract_out,
+        row_total,
+    )
+
+
+def fits_groups(mesh, args):
+    hidden, order = args[0], args[1]
+    count = mesh.shape["seq"]
+    tokens = hidden.shape[1] // count
+    return (
+        mesh.shape["rep"] == 2
+        and mesh.shape["fsdp"] == 2
+        and count == 2 * LINE
+        and hidden.shape[0] == LINE
+        and hidden.shape[2] == GROUP * 2 * HEAD
+        and tokens % UNIT == 0
+        and hidden.shape[1] % SPAN == 0
+        and order.shape[1] + args[2].shape[1] <= 128
+    )
+
+
 def solution(mesh):
     in_specs = (
         P(("rep", "fsdp"), "seq", None),
@@ -450,4 +2072,12 @@
         P("fsdp", None),
         P("fsdp"),
     )
-    return jax.shard_map(body, mesh=mesh, in_specs=in_specs, out_specs=out_specs, check_vma=False)
+
+    def run(*args):
+        chosen = group_body if fits_groups(mesh, args) else body
+        mapped = jax.shard_map(
+            chosen, mesh=mesh, in_specs=in_specs, out_specs=out_specs, check_vma=False
+        )
+        return mapped(*args)
+
+    return run

time: 2010 us -> 395 us (0.20)
  blocking collectives: 1080 us -> 0 us
  waiting for transfers between devices: 531 us -> 0 us
  Pallas kernels: 0 us -> 357 us
  matrix products: 237 us -> 0 us
  local copies, waits for them, and re-layouts: 81.2 us -> 17.9 us
  other arithmetic: 44.6 us -> 11.4 us
    psum x1 -> x0, blocking collectives: 1040 us -> none  [body(): lax.psum((owned[0], owned[1], owned[2], owned[3], owned[4], owned[5], own...]
    pallas_call x0 -> x5, Pallas kernels: none -> 357 us  [the longest x1 188 us: close(): pl.pallas_call(functools.partial(close_kernel, swap=swap), out_shape=(jax...]
    reduce_scatter x5 -> x0, waiting for transfers between devices: 342 us -> none  [the longest x1 121 us: body(): lax.psum_scatter(term.astype(jnp.bfloat16), 'seq', scatter_dimension=0, t...]
    dot_general x52 -> x0, matrix products: 237 us -> none  [the longest x12 43.8 us: view(): jnp.einsum('thd,khd->htk', queries, key_rows, preferred_element_type=jnp....]
    all_gather x6 -> x0, waiting for transfers between devices: 186 us -> none  [the longest x1 72.4 us: body(): lax.all_gather(keys, 'seq', axis=0, tiled=True)]
    all_gather x8 -> x0, blocking collectives: 35.9 us -> none  [the longest x1 5.28 us: body(): lax.all_gather(shards[5], 'fsdp', axis=0, tiled=True)]
    dynamic_slice x65 -> x8, local copies, waits for them, and re-layouts: 38 us -> 6.05 us  [the longest x5 2.54 us: own_half(): return lax.dynamic_slice_in_dim(vector, y * size, size, 0)]
  transfers between devices with their start and end apart: 11 -> 0, of which waited for: 8 -> 0; matrix products, arithmetic and copies ran while one was open for 18% -> 0% of each run, Pallas kernels for 0% -> 0%
where the time goes in v2:
time: 395 us; the launch traced here: 388 us
  Pallas kernels  357 us (90%)
  local copies, waits for them, and re-layouts  17.9 us (5%)
  other arithmetic  11.4 us (3%)
    pallas_call x1, Pallas kernels, close(): pl.pallas_call(functools.partial(close_kernel, swap=swap), out_shape=(jax...  188 us
    pallas_call x1, Pallas kernels, attend(): pl.pallas_call(functools.partial(attention_kernel, units=units, pieces=pi...  66 us
    pallas_call x1, Pallas kernels, feed_forward(): pl.pallas_call(feed_kernel, out_shape=(jax.ShapeDtypeStruct((4, LINE, row...  54.7 us
    pallas_call x1, Pallas kernels, enter(): pl.pallas_call(enter_kernel, out_shape=(jax.ShapeDtypeStruct((GROUP,) + h...  38.7 us
    unnamed x43, local copies, waits for them, and re-layouts  10.8 us
    pallas_call x1, Pallas kernels, widen(): pl.pallas_call(functools.partial(widen_kernel, swap=swap, lanes=lanes, ff...  10.5 us

profile of v2, /device:TPU:0, one launch (start us, length us, event | category | flops | bytes accessed | tf_op | source)
XLA Modules:
  0.0 388.2 jit_solution(5576671964730591733)
XLA Ops:
  0.7 0.9 pad_add_fusion
  1.6 1.2 convert_reduce_fusion
  2.8 1.3 fusion.9
  4.1 1.3 dynamic-slice_convert_fusion
  5.5 0.9 dynamic-update-slice
  6.3 0.9 dynamic-update-slice.1
  7.2 0.9 dynamic-update-slice.2
  8.0 0.9 dynamic-update-slice.3
  8.9 0.9 dynamic-update-slice.4
  9.8 0.9 dynamic-update-slice.5
  10.6 0.7 constant_dynamic-update-slice_fusion.1
  12.5 0.7 constant_dynamic-slice_fusion.5.wo
  13.2 2.3 constant_dynamic-slice_fusion.4.wc
  15.5 38.7 %enter.1 = (bf16[8,256,1024]{2,1,0:T(8,128)(2,1)}, s32[4,8,128]{2,1,0:T(8,128)S(1)}, f32[2,52,128]{2,1,0:T(8,128)S(1)}, bf16[2,512,384]{2,1,0:T(8,128)(2,1)S(1)}...) custom-call(bf16[256,1024]{1,0:T(8,128)(2,1)S(1)} %bitcast.70, s32[8,128]{1,0:T(8,128)S(1)} %broadcast_in_dim.75.ints, ...), custom_call_target="tpu_custom_call" | custom-call | tf_op jit(solution)/shard_map/enter/pallas_call | solution.py:689
  54.2 1.1 copy-done.4
  55.3 0.9 copy-done.5
  57.4 54.7 %feed_forward.1 = (bf16[4,4,512,128]{3,2,1,0:T(8,128)(2,1)}, bf16[8,256,1024]{2,1,0:T(8,128)(2,1)}, bf16[2,512,512]{2,1,0:T(8,128)(2,1)}, bf16[2048,512]{1,0:T(8...) custom-call(bf16[3,2048,128]{2,1,0:T(8,128)(2,1)} %copy-done.4, ...), custom_call_target="tpu_custom_call" | custom-call | tf_op jit(solution)/shard_map/feed_forward/pallas_call | solution.py:873
  112.1 66.0 %attend.1 = (bf16[4,2048,128]{2,1,0:T(8,128)(2,1)}, bf16[512,2048]{1,0:T(8,128)(2,1)}) custom-call(s32[1,128]{1,0:T(1,128)} %fusion.18.ints, bf16[4,2048,128]{2,1,0:T(8,128)(2,1)} %bitcast.76, f32[16,128]{1,0:T(8,128)} %copy-done.9, f32[16,128]{1,0:T(8,128)} %copy-done.8, f32[128,128]{1,0:T(8,128)} %copy-done.7, f32[128,128]{1,0:T(8,128)} %copy-done.6, ...), custom_call_target="tpu_custom_call" | custom-call | tf_op jit(solution)/shard_map/attend/pallas_call | solution.py:1444
  178.2 187.6 %close.1 = (bf16[2,2,544,1024]{3,2,1,0:T(8,128)(2,1)}, bf16[2,2,512,2048]{3,2,1,0:T(8,128)(2,1)}, f32[256,1024]{1,0:T(8,128)}, f32[256,1024]{1,0:T(8,128)}) custom-call(bf16[4,4,512,128]{3,2,1,0:T(8,128)(2,1)} %bitcast.75, bf16[2048,512]{1,0:T(8,128)(2,1)} %get-tuple-element.43.active, bf16[2048,512]{1,0:T(8,128)(2,1)} %get-tuple-element.44.grad_expanded, ...), custom_call_target="tpu_custom_call" | custom-call | tf_op jit(solution)/shard_map/close/pallas_call | solution.py:1761
  365.7 1.6 fusion.23
  367.3 3.1 fusion.8
  370.4 1.0 slice_convert_fusion
  374.3 2.3 copy-done.3
  376.6 10.5 %widen.1 = (f32[512,4096]{1,0:T(8,128)}, f32[2048,1024]{1,0:T(8,128)}, f32[512,3072]{1,0:T(8,128)}, f32[512,1024]{1,0:T(8,128)}) custom-call(bf16[2,2,512,2048]{3,2,1,0:T(8,128)(2,1)} %get-tuple-element.55.feed_all, bf16[2,2,544,1024]{3,2,1,0:T(8,128)(2,1)S(1)} %copy-done.3), custom_call_target="tpu_custom_call" | custom-call | tf_op jit(solution)/shard_map/widen/pallas_call | solution.py:1855
  (65 shorter events, 5.9 us)
Async XLA Ops:
  0.6 11.8 %copy-start = (bf16[512,1024]{1,0:T(8,128)(2,1)S(1)}, bf16[512,1024]{1,0:T(8,128)(2,1)}, u32[]{:S(2)}) copy-start(bf16[512,1024]{1,0:T(8,128)(2,1)} %param.25) | copy-start | bytes 3145732
  0.7 14.8 %copy-start.2 = (bf16[1,256,1024]{2,1,0:T(8,128)(2,1)S(1)}, bf16[1,256,1024]{2,1,0:T(8,128)(2,1)}, u32[]{:S(2)}) copy-start(bf16[1,256,1024]{2,1,0:T(8,128)(2,1)} %param.16) | copy-start | bytes 1572868
  12.1 100.0 %copy-start.8 = (f32[16,128]{1,0:T(8,128)}, f32[16,128]{1,0:T(8,128)S(1)}, u32[]{:S(2)}) copy-start(f32[16,128]{1,0:T(8,128)S(1)} %get-tuple-element.75.unit_sin) | copy-start | bytes 24580
  12.1 100.0 %copy-start.9 = (f32[16,128]{1,0:T(8,128)}, f32[16,128]{1,0:T(8,128)S(1)}, u32[]{:S(2)}) copy-start(f32[16,128]{1,0:T(8,128)S(1)} %get-tuple-element.76.unit_cos) | copy-start | bytes 24580
  12.5 99.6 %copy-start.6 = (f32[128,128]{1,0:T(8,128)}, f32[128,128]{1,0:T(8,128)S(1)}, u32[]{:S(2)}) copy-start(f32[128,128]{1,0:T(8,128)S(1)} %get-tuple-element.73.row_sin) | copy-start | bytes 196612
  12.5 99.6 %copy-start.7 = (f32[128,128]{1,0:T(8,128)}, f32[128,128]{1,0:T(8,128)S(1)}, u32[]{:S(2)}) copy-start(f32[128,128]{1,0:T(8,128)S(1)} %get-tuple-element.74.row_cos) | copy-start | bytes 196612
  54.2 1.1 copy-start.4
  55.3 0.9 copy-start.5
  178.1 189.2 %copy-start.10 = (bf16[1,256,1024]{2,1,0:T(8,128)(2,1)S(1)}, bf16[1,256,1024]{2,1,0:T(8,128)(2,1)}, u32[]{:S(2)}) copy-start(bf16[1,256,1024]{2,1,0:T(8,128)(2,1)} %param.31) | copy-start | bytes 1572868
  371.7 15.4 %copy-start.11 = (f32[512]{0:T(512)}, f32[512]{0:T(512)S(1)}, u32[]{:S(2)}) copy-start(f32[512]{0:T(512)S(1)} %dynamic_slice.58) | copy-start | bytes 6148
  373.7 14.0 %copy-start.1 = (bf16[512,1024]{1,0:T(8,128)(2,1)S(1)}, bf16[512,1024]{1,0:T(8,128)(2,1)}, u32[]{:S(2)}) copy-start(bf16[512,1024]{1,0:T(8,128)(2,1)} %param.25) | copy-start | bytes 3145732
  374.3 2.3 copy-start.3

commit v3 on v2

--- a/solution.py
+++ b/solution.py
@@ -744,8 +744,8 @@
     second,
     cot,
     we,
-    wo,
-    wc,
+    wo_src,
+    wc_src,
     bias,
     got,
     cot_all,
@@ -756,6 +756,8 @@
     sums,
     slope,
     grad_heads,
+    wo,
+    wc,
     send,
     recv,
     token_send,
@@ -776,10 +778,18 @@
     peers = [lax.rem(z + d, LINE) for d in range(1, LINE)]
     mine = pl.ds(pl.multiple_of(z * rows, rows), rows)
     me = (2 * c + y) * 2 + x
+    inner = 2 * x + c
+
+    def rows_of(src, dst):
+        count = dst.shape[0]
+        return src.at[pl.ds(pl.multiple_of(inner * count, count), count)]
+
     keeps = [
         pltpu.make_async_copy(we.at[:, column_block(ff, own * ff)], we_all.at[y], local.at[0]),
         pltpu.make_async_copy(cot, cot_all.at[me], local.at[1]),
-        pltpu.make_async_copy(heads.at[:, mine], got.at[pl.ds(0, 3), z], local.at[2]),
+        pltpu.make_async_copy(rows_of(wo_src, wo), wo, local.at[2]),
+        pltpu.make_async_copy(rows_of(wc_src, wc), wc, local.at[3]),
+        pltpu.make_async_copy(heads.at[:, mine], got.at[pl.ds(0, 3), z], local.at[4]),
     ]
     for copy in keeps:
         copy.start()
@@ -798,7 +808,7 @@
         )
         copy.start()
         copies.append(copy)
-    for copy in keeps[:2]:
+    for copy in keeps[:4]:
         copy.wait()
     weight.wait_recv()
     sums[...] = jnp.zeros_like(sums)
@@ -857,7 +867,7 @@
     for index in range(ff // TILE):
         block = dot_tokens(active[:, pl.ds(index * TILE, TILE)], cots)
         feed_grad[pl.ds(index * TILE, TILE), pl.ds(2 * ff, 2 * half)] = block.astype(jnp.bfloat16)
-    keeps[2].wait()
+    keeps[4].wait()
     last.wait()
     for copy in copies:
         copy.wait()
@@ -881,16 +891,18 @@
             jax.ShapeDtypeStruct((width // 2, 2 * ff + width), jnp.bfloat16),
             jax.ShapeDtypeStruct((1, ff), jnp.float32),
         ),
-        in_specs=[any_spec, vmem, any_spec, any_spec, vmem, vmem, vmem],
+        in_specs=[any_spec, vmem] + [any_spec] * 4 + [vmem],
         out_specs=[any_spec] + [vmem] * 6,
         scratch_shapes=[
             pltpu.VMEM((rows, ff), jnp.float32),
             pltpu.VMEM((rows, lanes), jnp.bfloat16),
+            pltpu.VMEM((lanes, width), jnp.bfloat16),
+            pltpu.VMEM((ff, width), jnp.bfloat16),
             pltpu.SemaphoreType.DMA((2, LINE - 1)),
             pltpu.SemaphoreType.DMA((2, LINE - 1)),
             pltpu.SemaphoreType.DMA((12,)),
             pltpu.SemaphoreType.DMA((12,)),
-            pltpu.SemaphoreType.DMA((3,)),
+            pltpu.SemaphoreType.DMA((5,)),
         ],
         compiler_params=pltpu.CompilerParams(
             collective_id=1, has_side_effects=True, vmem_limit_bytes=56 << 20
@@ -899,178 +911,17 @@
     )(heads, second, cot, we, wo, wc, bias)
 
 
-class LineReduce:
-    LAG = 2
-
-    def __init__(self, grad, result, inbox, sems, swap, size, place):
-        self.grad, self.result, self.inbox, self.sems, self.swap = grad, result, inbox, sems, swap
-        self.c, self.y, self.x, self.z = place
-        self.size = size
-        self.each = grad.shape[0] // size // 2
-        self.slots = self.each + (LINE - 1) * self.LAG
-
-    def rows(self, chunk):
-        return pl.ds(pl.multiple_of(chunk * self.size, self.size), self.size)
-
-    def lanes(self, which):
-        return pl.ds(pl.multiple_of(which * self.swap, self.swap), self.swap)
-
-    def ahead(self, chunk, half):
-        up = 1 if half == 0 else -1
-        rows = self.rows(chunk)
-        return remote(
-            self.grad.at[rows],
-            self.inbox.at[rows],
-            self.sems.at[0, chunk],
-            self.sems.at[1, chunk],
-            device_at(self.c, self.y, self.x, self.z + up),
-        )
-
-    def across(self, chunk):
-        rows = self.rows(chunk)
-        return remote(
-            self.grad.at[rows, self.lanes(1 - self.y)],
-            self.result.at[rows, self.lanes(self.y)],
-            self.sems.at[2, chunk],
-            self.sems.at[3, chunk],
-            device_at(self.c, 1 - self.y, self.x, self.z),
-        )
-
-    def slot(self, t):
-        for half in range(2):
-            at = self.z if half == 0 else LINE - 1 - self.z
-            step = t - self.LAG * at
-            chunk = jnp.clip(step, 0, self.each - 1) + half * self.each
-
-            @pl.when((step >= 0) & (step < self.each))
-            def _():
-                rows = self.rows(chunk)
-
-                @pl.when(at > 0)
-                def _():
-                    self.ahead(chunk, half).wait_recv()
-                    total = self.grad[rows].astype(jnp.float32) + self.inbox[rows].astype(
-                        jnp.float32
-                    )
-                    self.grad[rows] = total.astype(jnp.bfloat16)
-
-                @pl.when(at < LINE - 1)
-                def _():
-                    self.ahead(chunk, half).start()
-
-                @pl.when(at == LINE - 1)
-                def _():
-                    self.across(chunk).start()
-                    own = self.lanes(self.y)
-                    plain = pl.ds(2 * self.swap, self.grad.shape[1] - 2 * self.swap)
-                    self.result[rows, own] = self.grad[rows, own]
-                    self.result[rows, plain] = self.grad[rows, plain]
-
-    def drain(self):
-        for half in range(2):
-            at = self.z if half == 0 else LINE - 1 - self.z
-
-            def finish(step, carry):
-                chunk = step + half * self.each
-
-                @pl.when(at < LINE - 1)
-                def _():
-                    self.ahead(chunk, half).wait_send()
-
-                @pl.when(at == LINE - 1)
-                def _():
-                    self.across(chunk).wait()
-
-                return carry
-
-            lax.fori_loop(0, self.each, finish, 0)
-
-
-class LineSpread:
-    def __init__(self, result, sems, size, place):
-        self.result, self.sems = result, sems
-        self.c, self.y, self.x, self.z = place
-        self.size = size
-        self.each = result.shape[2] // size // 2
-        self.slots = self.each + LINE
-
-    def move(self, kind, chunk, half):
-        c, y, x, z = self.c, self.y, self.x, self.z
-        up = 1 if half == 0 else -1
-        rows = pl.ds(pl.multiple_of(chunk * self.size, self.size), self.size)
-        side = 1 - x if kind == 3 else x
-        target = (
-            device_at(c, y, x, z - up),
-            device_at(c, y, 1 - x, z),
-            device_at(1 - c, y, x, z),
-            device_at(1 - c, y, x, z),
-        )[kind]
-        part = self.result.at[c, side, rows]
-        return remote(
-            part, part, self.sems.at[2 * kind, chunk], self.sems.at[2 * kind + 1, chunk], target
-        )
-
-    def slot(self, t):
-        for half in range(2):
-            at = self.z if half == 0 else LINE - 1 - self.z
-
-            def event(delay, run):
-                step = t - delay
-                chunk = jnp.clip(step, 0, self.each - 1) + half * self.each
-
-                @pl.when((step >= 0) & (step < self.each))
-                def _():
-                    run(chunk)
-
-            def spread(chunk):
-                @pl.when(at < LINE - 1)
-                def _():
-                    self.move(0, chunk, half).wait_recv()
-
-                @pl.when(at > 0)
-                def _():
-                    self.move(0, chunk, half).start()
-
-                self.move(1, chunk, half).start()
-                self.move(2, chunk, half).start()
-
-            def late(chunk):
-                self.move(1, chunk, half).wait_recv()
-                self.move(3, chunk, half).start()
-
-            event(LINE - 1 - at, spread)
-            event(LINE - at, late)
-
-    def drain(self):
-        for half in range(2):
-            at = self.z if half == 0 else LINE - 1 - self.z
-
-            def finish(step, carry):
-                chunk = step + half * self.each
-
-                @pl.when(at > 0)
-                def _():
-                    self.move(0, chunk, half).wait_send()
-
-                self.move(1, chunk, half).wait_send()
-                self.move(2, chunk, half).wait()
-                self.move(3, chunk, half).wait()
-                return carry
-
-            lax.fori_loop(0, self.each, finish, 0)
-
-
 class LineSum:
-    LAG = 1
     KINDS = 8
 
-    def __init__(self, grad, result, inbox, sems, swap, size, place):
+    def __init__(self, grad, result, inbox, sems, swap, size, lag, place):
         self.grad, self.result, self.inbox, self.sems, self.swap = grad, result, inbox, sems, swap
         self.c, self.y, self.x, self.z = place
         self.size = size
         self.count = grad.shape[0] // size
         self.split = (self.count + 1) // 2
-        self.slots = self.split + 6 * self.LAG
+        self.lag = lag
+        self.slots = self.split + 6 * lag
 
     def rows(self, chunk):
         return pl.ds(pl.multiple_of(chunk * self.size, self.size), self.size)
@@ -1126,7 +977,7 @@
 
     def half_slot(self, t, half):
         size, base, at = self.extent(half)
-        lag = self.LAG
+        lag = self.lag
         swap = self.swap
         owner = at == 1
 
@@ -1237,6 +1088,29 @@
             lax.fori_loop(0, size, finish, 0)
 
 
+def sort_kernel(order, src, dst, *, units, back):
+    for unit in range(units):
+        place = order[0, unit]
+        if back:
+            dst[:, unit] = src[:, place]
+        else:
+            dst[:, place] = src[:, unit]
+
+
+def sort_units(order, array, units, back):
+    shape = array.shape
+    vmem = pl.BlockSpec(memory_space=pltpu.VMEM)
+    view = (shape[0], units, UNIT, shape[-1])
+    return pl.pallas_call(
+        functools.partial(sort_kernel, units=units, back=back),
+        out_shape=jax.ShapeDtypeStruct(view, array.dtype),
+        in_specs=[pl.BlockSpec(memory_space=pltpu.SMEM), vmem],
+        out_specs=vmem,
+        compiler_params=pltpu.CompilerParams(vmem_limit_bytes=16 << 20),
+        name="restore_units" if back else "sort_units",
+    )(order, array.reshape(view))
+
+
 def attention_kernel(
     ints,
     parts,
@@ -1246,7 +1120,7 @@
     row_sin,
     feed_grad,
     out,
-    feed_sum,
+    feed_all,
     masked,
     flat,
     scores,
@@ -1268,7 +1142,8 @@
     greet_line(here)
     load = pltpu.make_async_copy(feed_grad, feed_own, local)
     load.start()
-    line = LineReduce(feed_own, feed_sum, feed_inbox, feed_sems, swap, FEED_CHUNK, here)
+    load.wait()
+    line = LineSum(feed_own, feed_all, feed_inbox, feed_sems, swap, FEED_CHUNK, 2, here)
     length = parts.shape[1]
     scale = 1.0 / math.sqrt(HEAD)
     blocks = length // SPAN
@@ -1276,14 +1151,13 @@
     lower = lanes < HEAD
 
     def arrange(index, carry):
+        @pl.when(lax.rem(index, 4) == 0)
+        def _():
+            line.slot(lax.div(index, 4))
+
         at = pl.ds(pl.multiple_of(index * UNIT, UNIT), UNIT)
         for which in range(4):
-            rows = jnp.zeros((UNIT, 2 * HEAD), jnp.bfloat16)
-            for unit in range(units):
-                rows = jnp.where(
-                    ints[0, unit] == index, parts[which, pl.ds(unit * UNIT, UNIT), :], rows
-                )
-            rows = rows.astype(jnp.float32)
+            rows = parts[which, at, :].astype(jnp.float32)
             if which == 0:
                 rows = rows * scale
             masked[which, 0, at, :] = jnp.where(lower, rows, 0.0).astype(jnp.bfloat16)
@@ -1292,7 +1166,7 @@
         return carry
 
     lax.fori_loop(0, units, arrange, 0)
-    load.wait()
+    early = -(-units // 4)
     key_sum[...] = jnp.zeros_like(key_sum)
     value_sum[...] = jnp.zeros_like(value_sum)
 
@@ -1321,13 +1195,20 @@
         )
 
         def one_head(head, carry):
-            slot = 3 * (2 * block + head)
-            line.slot(slot)
+            start_tick = 3 * block * (block + 1) + head * 3 * (block + 1)
+
+            def tick(index):
+                at = start_tick + index
+
+                @pl.when(lax.rem(at, 2) == 0)
+                def _():
+                    line.slot(early + lax.div(at, 2))
+
             queries = flat[0, :, columns]
             grads = flat[3, :, columns]
             side = pl.ds(pl.multiple_of(head * HEAD, HEAD), HEAD)
 
-            def score_tile(start, size, top, mask):
+            def score_tile(start, size, top, mask=None):
                 rows = pl.ds(start, size)
                 tile = dot(masked[1, head, rows, :], queries)
                 if mask is not None:
@@ -1335,12 +1216,18 @@
                 scores[rows, :] = tile
                 return jnp.maximum(top, jnp.max(tile, axis=0, keepdims=True))
 
+            def tile_step(step, run, j, carry):
+                tick(step * (block + 1) + j)
+                start = pl.multiple_of(j * SPAN, SPAN)
+                return run(start, SPAN, carry)
+
             top = lax.fori_loop(
                 0,
                 block,
-                lambda j, top: score_tile(pl.multiple_of(j * SPAN, SPAN), SPAN, top, None),
+                functools.partial(tile_step, 0, score_tile),
                 jnp.full((1, SPAN), NEGATIVE, jnp.float32),
             )
+            tick(block)
             top = score_tile(begin, last, top, allowed)
 
             def weight_tile(start, size, sums):
@@ -1355,14 +1242,14 @@
                     delta + jnp.sum(weights * slope, axis=0, keepdims=True),
                 )
 
-            line.slot(slot + 1)
             zero = jnp.zeros((1, SPAN), jnp.float32)
             sums = lax.fori_loop(
                 0,
                 block,
-                lambda j, sums: weight_tile(pl.multiple_of(j * SPAN, SPAN), SPAN, sums),
+                functools.partial(tile_step, 1, weight_tile),
                 (zero, zero),
             )
+            tick(2 * block + 1)
             total, delta = weight_tile(begin, last, sums)
             inverse = 1.0 / total
             delta = delta * inverse
@@ -1379,14 +1266,14 @@
                 query = query + dot(flat[1, side, rows], grad)
                 return (mixed, query)
 
-            line.slot(slot + 2)
             none = jnp.zeros((HEAD, SPAN), jnp.float32)
             sums = lax.fori_loop(
                 0,
                 block,
-                lambda j, sums: grad_tile(pl.multiple_of(j * SPAN, SPAN), SPAN, sums),
+                functools.partial(tile_step, 2, grad_tile),
                 (none, none),
             )
+            tick(3 * block + 2)
             mixed, query = grad_tile(begin, last, sums)
             mixed_sum[side, columns] = mixed
             query_sum[side, columns] = query * scale
@@ -1409,32 +1296,20 @@
             down = pltpu.roll(rows, HALF, 1)
             return rows * cosine + up * sine_up - down * sine_down
 
-        masked[0, 0, at, :] = mixed_sum[:, at].T.astype(jnp.bfloat16)
-        masked[1, 0, at, :] = turn_back(query_sum[:, at].T).astype(jnp.bfloat16)
-        masked[2, 0, at, :] = turn_back(key_sum[at, :]).astype(jnp.bfloat16)
-        masked[3, 0, at, :] = value_sum[at, :].astype(jnp.bfloat16)
+        out[0, at, :] = mixed_sum[:, at].T.astype(jnp.bfloat16)
+        out[1, at, :] = turn_back(query_sum[:, at].T).astype(jnp.bfloat16)
+        out[2, at, :] = turn_back(key_sum[at, :]).astype(jnp.bfloat16)
+        out[3, at, :] = value_sum[at, :].astype(jnp.bfloat16)
         return carry
 
     lax.fori_loop(0, units, finish, 0)
-
-    def restore(index, carry):
-        here = pl.ds(pl.multiple_of(index * UNIT, UNIT), UNIT)
-        for which in range(4):
-            rows = jnp.zeros((UNIT, 2 * HEAD), jnp.bfloat16)
-            for unit in range(units):
-                rows = jnp.where(
-                    ints[0, index] == unit, masked[which, 0, pl.ds(unit * UNIT, UNIT), :], rows
-                )
-            out[which, here, :] = rows
-        return carry
-
-    lax.fori_loop(0, units, restore, 0)
 
     def more(slot, carry):
         line.slot(slot)
         return carry
 
-    lax.fori_loop(6 * blocks, max(line.slots, 6 * blocks), more, 0)
+    ticked = early + (3 * blocks * (blocks + 1) + 1) // 2
+    lax.fori_loop(ticked, max(line.slots, ticked), more, 0)
     line.drain()
 
 
@@ -1445,7 +1320,7 @@
         functools.partial(attention_kernel, units=units, pieces=pieces, swap=swap),
         out_shape=(
             jax.ShapeDtypeStruct(parts.shape, parts.dtype),
-            jax.ShapeDtypeStruct(feed_grad.shape, feed_grad.dtype),
+            jax.ShapeDtypeStruct((2, 2) + feed_grad.shape, feed_grad.dtype),
         ),
         in_specs=[pl.BlockSpec(memory_space=pltpu.SMEM)]
         + [vmem] * 5
@@ -1461,8 +1336,8 @@
             pltpu.VMEM((2 * HEAD, length), jnp.float32),
             pltpu.VMEM((2 * HEAD, length), jnp.float32),
             pltpu.VMEM(feed_grad.shape, jnp.bfloat16),
-            pltpu.VMEM(feed_grad.shape, jnp.bfloat16),
-            pltpu.SemaphoreType.DMA((4, feed_grad.shape[0] // FEED_CHUNK)),
+            pltpu.VMEM((2,) + feed_grad.shape, jnp.bfloat16),
+            pltpu.SemaphoreType.DMA((2 * LineSum.KINDS, feed_grad.shape[0] // FEED_CHUNK)),
             pltpu.SemaphoreType.DMA,
         ],
         compiler_params=pltpu.CompilerParams(
@@ -1474,19 +1349,17 @@
 
 def close_kernel(
     done,
-    active,
-    grad_expanded,
-    we,
-    wc,
-    wm,
-    wo,
-    hidden,
-    cots,
+    active_src,
+    grad_expanded_src,
+    we_src,
+    wc_src,
+    wm_src,
+    wo_src,
+    hidden_src,
+    cots_src,
     vectors,
     feed_sums,
-    feed_sum,
     attn_all,
-    feed_all,
     out_sum,
     term_sum,
     parts,
@@ -1497,17 +1370,27 @@
     attn_own,
     attn_inbox,
     near,
-    four,
-    mid,
-    two,
+    pair,
+    beside,
+    single,
     far,
     totals,
+    active,
+    grad_expanded,
+    we,
+    wc,
+    wm,
+    wo,
+    hidden,
+    cots,
     send,
     recv,
     attn_sems,
-    feed_sems,
-    sems,
+    near_sems,
+    beside_sems,
+    far_sems,
     local,
+    loads,
     *,
     swap,
 ):
@@ -1516,6 +1399,27 @@
     core = device_at(1 - c, y, x, z)
     over_x = device_at(c, y, 1 - x, z)
     over_y = device_at(c, 1 - y, x, z)
+    inner = 2 * x + c
+
+    def rows_of(src, dst):
+        count = dst.shape[0]
+        return src.at[pl.ds(pl.multiple_of(inner * count, count), count)]
+
+    sources = (
+        (hidden_src, hidden),
+        (grad_expanded_src, grad_expanded),
+        (we_src, we),
+        (active_src, active),
+        (rows_of(wc_src, wc), wc),
+        (cots_src, cots),
+        (wm_src, wm),
+        (rows_of(wo_src, wo), wo),
+    )
+    fetched = []
+    for index, (src, dst) in enumerate(sources):
+        copy = pltpu.make_async_copy(src, dst, loads.at[index])
+        copy.start()
+        fetched.append(copy)
     barrier = pltpu.get_barrier_semaphore()
     peers = [lax.rem(z + d, LINE) for d in range(1, LINE)]
     partners = [device_at(c, y, x, peer) for peer in peers] + [core, over_x, over_y]
@@ -1544,27 +1448,14 @@
         )
         copy.start()
         owns.append(copy)
-    spread = LineSpread(feed_all, feed_sems, CHUNK, place)
-    own_half = CHUNK * spread.each
-
-    @pl.when((z == 0) | (z == LINE - 1))
-    def _():
-        at = pl.ds(pl.multiple_of(jnp.where(z == 0, own_half, 0), own_half), own_half)
-        copy = pltpu.make_async_copy(feed_sum.at[at], feed_all.at[c, x, at], local.at[4])
-        copy.start()
-        copy.wait()
-
     gain_one, shift_one, gain_two = vectors[0:1, :], vectors[1:2, :], vectors[2:3, :]
     width = hidden.shape[1]
     half = width // 2
-    tokens = outs.shape[1]
     totals[...] = jnp.zeros_like(totals)
-
-    def normed(at, mean, rstd):
-        return (hidden[at, :].astype(jnp.float32) - mean) * rstd
+    for copy in fetched:
+        copy.wait()
 
     def before(index, carry):
-        spread.slot(index)
         at = pl.ds(pl.multiple_of(index * TILE, TILE), TILE)
         raw = hidden[at, :].astype(jnp.float32)
         mean = jnp.mean(raw, axis=1, keepdims=True)
@@ -1582,24 +1473,49 @@
         totals[4:5, :] += jnp.sum(cots[at, :].astype(jnp.float32), axis=0, keepdims=True)
         return carry
 
-    shown = hidden.shape[0] // TILE
-    lax.fori_loop(0, shown, before, 0)
-
-    def spread_rest(t, carry):
-        spread.slot(t)
-        return carry
-
-    lax.fori_loop(shown, spread.slots, spread_rest, 0)
+    lax.fori_loop(0, hidden.shape[0] // TILE, before, 0)
     for copy in owns:
         copy.wait()
     for copy in copies:
         copy.wait()
 
-    def after(index, carry):
+    arrays = (outs, terms)
+
+    def block_at(cc, yy, xx):
+        return (2 * cc + yy) * 2 + xx
+
+    def to_core(a, yy, xx):
+        block = block_at(1 - c, yy, xx)
+        return remote(
+            arrays[a].at[block],
+            near.at[a, yy, xx],
+            near_sems.at[0, a, yy, xx],
+            near_sems.at[1, a, yy, xx],
+            core,
+        )
+
+    ways = ((y, x, over_y, over_x), (x, y, over_x, over_y))
+
+    def hop_one(a, index):
+        near_axis, far_axis, target, beyond = ways[a]
+        return remote(
+            pair.at[a, 1 - near_axis, index],
+            beside.at[a, index],
+            beside_sems.at[0, a, index],
+            beside_sems.at[1, a, index],
+            target,
+        )
+
+    def hop_two(a):
+        return remote(
+            single.at[a], far.at[a], far_sems.at[0, a], far_sems.at[1, a], ways[a][3]
+        )
+
+    def after(index):
         at = pl.ds(pl.multiple_of(index * TILE, TILE), TILE)
         grads = parts[at, pl.ds(lanes, 3 * lanes)]
         grad_first = dot_rows(grads, wm[...])
-        xhat = normed(at, stats[0, at, 0:1], stats[1, at, 0:1])
+        xhat = (hidden[at, :].astype(jnp.float32) - stats[0, at, 0:1]) * stats[1, at, 0:1]
         terms[index] = (terms[index].astype(jnp.float32) + grad_first * gain_one).astype(
             jnp.bfloat16
         )
@@ -1611,21 +1527,34 @@
         totals[5:6, pl.ds(0, 3 * lanes)] += jnp.sum(
             grads.astype(jnp.float32), axis=0, keepdims=True
         )
+
+    def others(step, carry):
+        yy, xx = lax.rem(1 - y + step // 2, 2), lax.rem(step, 2)
+        after(block_at(1 - c, yy, xx))
+        for a in range(2):
+            to_core(a, yy, xx).start()
         return carry
 
-    lax.fori_loop(0, hidden.shape[0] // TILE, after, 0)
-    arrays = (outs, terms)
-    nears = []
-    for a in range(2):
-        copy = remote(
-            arrays[a].at[pl.ds(pl.multiple_of(4 * (1 - c), 4), 4)],
-            near.at[a],
-            sems.at[0, a],
-            sems.at[1, a],
-            core,
-        )
-        copy.start()
-        nears.append(copy)
+    lax.fori_loop(0, 4, others, 0)
+
+    def ours(step, carry):
+        yy, xx = lax.rem(1 - y + step // 2, 2), lax.rem(step, 2)
+        after(block_at(c, yy, xx))
+        for a in range(2):
+            to_core(a, yy, xx).wait_recv()
+            total = arrays[a][block_at(c, yy, xx)].astype(jnp.float32) + near[a, yy, xx].astype(
+                jnp.float32
+            )
+            near_at, far_at = (yy, xx) if a == 0 else (xx, yy)
+            pair[a, near_at, far_at] = total.astype(jnp.bfloat16)
+
+            @pl.when(near_at != ways[a][0])
+            def _():
+                hop_one(a, far_at).start()
+
+        return carry
+
+    lax.fori_loop(0, 4, ours, 0)
     for index in range(width // TILE):
         block = dot_tokens(first[:, pl.ds(index * TILE, TILE)], parts[:, pl.ds(lanes, 3 * lanes)])
         side, row = divmod(index * TILE, half)
@@ -1660,78 +1589,49 @@
     attn_own[tail, pl.ds(swap, swap)] = small
     attn_own[tail, pl.ds(2 * swap, wide)] = jnp.zeros((small.shape[0], wide), jnp.bfloat16)
 
-    attn = LineSum(attn_own, attn_all, attn_inbox, attn_sems, swap, CHUNK, place)
+    attn = LineSum(attn_own, attn_all, attn_inbox, attn_sems, swap, CHUNK, 1, place)
 
     def step(t, carry):
         attn.slot(t)
         return carry
 
-    lax.fori_loop(0, 2, step, 0)
-    mids = []
-    for a in range(2):
-        nears[a].wait()
-        for j in range(4):
-            total = arrays[a][4 * c + j].astype(jnp.float32) + near[a, j].astype(jnp.float32)
-            if a == 0:
-                four[a, j % 2, j // 2] = total.astype(jnp.bfloat16)
-            else:
-                four[a, j // 2, j % 2] = total.astype(jnp.bfloat16)
-        copy = remote(
-            four.at[a, 1 - x if a == 0 else 1 - y],
-            mid.at[a],
-            sems.at[0, 2 + a],
-            sems.at[1, 2 + a],
-            over_x if a == 0 else over_y,
-        )
-        copy.start()
-        mids.append(copy)
-    lax.fori_loop(2, 9, step, 0)
-    fars = []
-    for a in range(2):
-        mids[a].wait()
-        mine_at, away = (x, y) if a == 0 else (y, x)
-        two[a] = (
-            four[a, mine_at, 1 - away].astype(jnp.float32) + mid[a, 1 - away].astype(jnp.float32)
+    def pass_on(a):
+        near_axis, far_axis = ways[a][:2]
+        for index in range(2):
+            hop_one(a, index).wait()
+        single[a] = (
+            pair[a, near_axis, 1 - far_axis].astype(jnp.float32)
+            + beside[a, 1 - far_axis].astype(jnp.float32)
         ).astype(jnp.bfloat16)
-        copy = remote(
-            two.at[a],
-            far.at[a],
-            sems.at[0, 4 + a],
-            sems.at[1, 4 + a],
-            over_y if a == 0 else over_x,
-        )
-        copy.start()
-        fars.append(copy)
-    lax.fori_loop(9, attn.slots, step, 0)
+        hop_two(a).start()
+
+    middle = attn.slots - 6
+    lax.fori_loop(0, middle, step, 0)
+    pass_on(0)
+    pass_on(1)
+    lax.fori_loop(middle, attn.slots, step, 0)
     for a, dst in enumerate((out_sum, term_sum)):
-        fars[a].wait()
-        mine_at, away = (x, y) if a == 0 else (y, x)
+        hop_two(a).wait()
+        near_axis, far_axis = ways[a][:2]
         dst[...] = (
-            four[a, mine_at, away].astype(jnp.float32)
-            + mid[a, away].astype(jnp.float32)
+            pair[a, near_axis, far_axis].astype(jnp.float32)
+            + beside[a, far_axis].astype(jnp.float32)
             + far[a].astype(jnp.float32)
         )
+
+    def sent(step, carry):
+        for a in range(2):
+            to_core(a, step // 2, lax.rem(step, 2)).wait_send()
+        return carry
+
+    lax.fori_loop(0, 4, sent, 0)
     attn.drain()
-    spread.drain()
-
-
-def close(
-    done,
-    active,
-    grad_expanded,
-    we,
-    wc,
-    wm,
-    wo,
-    hidden,
-    cots,
-    vectors,
-    feed_sums,
-    feed_sum,
-    tokens,
-):
+
+
+def close(done, active, grad_expanded, we, wc, wm, wo, hidden, cots, vectors, feed_sums, tokens):
     rows, width = hidden.shape
     lanes = done.shape[3]
+    ff = active.shape[1]
     swap = 3 * lanes
     block = (tokens, width)
     vmem = pl.BlockSpec(memory_space=pltpu.VMEM)
@@ -1745,37 +1645,44 @@
         pltpu.VMEM((GROUP,) + block, jnp.bfloat16),
         pltpu.VMEM(grad_shape, jnp.bfloat16),
         pltpu.VMEM((2,) + grad_shape, jnp.bfloat16),
-        pltpu.VMEM((2, 4) + block, jnp.bfloat16),
+        pltpu.VMEM((2, 2, 2) + block, jnp.bfloat16),
         pltpu.VMEM((2, 2, 2) + block, jnp.bfloat16),
         pltpu.VMEM((2, 2) + block, jnp.bfloat16),
         pltpu.VMEM((2,) + block, jnp.bfloat16),
         pltpu.VMEM((2,) + block, jnp.bfloat16),
         pltpu.VMEM((8, width), jnp.float32),
+        pltpu.VMEM((rows, ff), jnp.bfloat16),
+        pltpu.VMEM((rows, ff), jnp.bfloat16),
+        pltpu.VMEM((width, ff), jnp.bfloat16),
+        pltpu.VMEM((ff, width), jnp.bfloat16),
+        pltpu.VMEM((width, 3 * lanes), jnp.bfloat16),
+        pltpu.VMEM((lanes, width), jnp.bfloat16),
+        pltpu.VMEM((rows, width), jnp.bfloat16),
+        pltpu.VMEM((rows, width), jnp.bfloat16),
         pltpu.SemaphoreType.DMA((LINE - 1, 4)),
         pltpu.SemaphoreType.DMA((LINE - 1, 4)),
         pltpu.SemaphoreType.DMA((2 * LineSum.KINDS, grad_shape[0] // CHUNK)),
-        pltpu.SemaphoreType.DMA((8, feed_sum.shape[0] // CHUNK)),
-        pltpu.SemaphoreType.DMA((2, 6)),
-        pltpu.SemaphoreType.DMA((5,)),
+        pltpu.SemaphoreType.DMA((2, 2, 2, 2)),
+        pltpu.SemaphoreType.DMA((2, 2, 2)),
+        pltpu.SemaphoreType.DMA((2, 2)),
+        pltpu.SemaphoreType.DMA((4,)),
+        pltpu.SemaphoreType.DMA((8,)),
     ]
     return pl.pallas_call(
         functools.partial(close_kernel, swap=swap),
         out_shape=(
             jax.ShapeDtypeStruct((2, 2) + grad_shape, jnp.bfloat16),
-            jax.ShapeDtypeStruct((2, 2) + feed_sum.shape, jnp.bfloat16),
             jax.ShapeDtypeStruct(block, jnp.float32),
             jax.ShapeDtypeStruct(block, jnp.float32),
         ),
-        in_specs=[any_spec] + [vmem] * 10 + [any_spec],
-        out_specs=[vmem, any_spec, vmem, vmem],
+        in_specs=[any_spec] * 9 + [vmem] * 2,
+        out_specs=[vmem] * 3,
         scratch_shapes=scratch,
         compiler_params=pltpu.CompilerParams(
             collective_id=3, has_side_effects=True, vmem_limit_bytes=60 << 20
         ),
         name="close",
-    )(
-        done, active, grad_expanded, we, wc, wm, wo, hidden, cots, vectors, feed_sums, feed_sum
-    )
+    )(done, active, grad_expanded, we, wc, wm, wo, hidden, cots, vectors, feed_sums)
 
 
 def widen_kernel(
@@ -1914,7 +1821,7 @@
         contract_bias,
     )
     sizes = [v.shape[0] for v in vectors]
-    packed = jnp.concatenate(vectors).astype(jnp.float32).reshape(-1, 128)
+    packed = jnp.concatenate([v.astype(jnp.float32).reshape(-1, 128) for v in vectors])
     ints = jnp.concatenate([unit_order[0], piece_starts[0]])
     ints = jnp.broadcast_to(jnp.pad(ints, (0, 128 - ints.shape[0]))[None], (8, 128))
     tables = turn_tables(jnp.arange(units, dtype=jnp.int32) * UNIT, part) + turn_tables(
@@ -1924,16 +1831,14 @@
         hidden_states[0], ints, packed, merged_weight, tables
     )
     inner = 2 * x + c
-    wo = lax.dynamic_slice_in_dim(output_weight, inner * part, part, 0)
-    wc = lax.dynamic_slice_in_dim(contract_weight, inner * ff_part, ff_part, 0)
     own_expand = lax.dynamic_slice_in_dim(expand_bias, inner * ff_part, ff_part, 0)
     got, cot_all, we_all, active, grad_expanded, feed_grad, feed_sums = feed_forward(
         heads,
         second,
         out_cotangent[0],
         expand_weight,
-        wo,
-        wc,
+        output_weight,
+        contract_weight,
         own_expand.astype(jnp.float32)[None],
     )
     vec_all = vec_all.reshape(2, -1)
@@ -1947,9 +1852,10 @@
     we = we_all.reshape(width, ff_part)
     cots = cot_all.reshape(rows, width)
     own_ints = lax.dynamic_index_in_dim(ints_all[:, 0], z, 0, keepdims=True)
-    done, feed_sum = attend(
+    sorted_parts = sort_units(own_ints, got, units, False)
+    done, feed_all = attend(
         own_ints,
-        got.reshape(4, length, part),
+        sorted_parts.reshape(4, length, part),
         tables,
         feed_grad,
         units,
@@ -1958,19 +1864,18 @@
     )
     swap = 3 * part
     lines = CHUNK
-    attn_all, feed_all, out_sum, term_sum = close(
-        done.reshape(4, LINE, 2 * tokens, part),
+    attn_all, out_sum, term_sum = close(
+        sort_units(own_ints, done, units, True).reshape(4, LINE, 2 * tokens, part),
         active,
         grad_expanded,
         we,
-        wc,
+        contract_weight,
         wm,
-        wo,
+        output_weight,
         hid_all.reshape(rows, width),
         cots,
         jnp.stack([gain_one, shift_one, gain_two]),
         feed_sums,
-        feed_sum,
         tokens,
     )
     expand_out, contract_out, merged_out, output_out = widen(

time: 395 us -> 363 us (0.919)
  Pallas kernels: 357 us -> 324 us
    pallas_call x1, Pallas kernels: 188 us -> 125 us  [close(): pl.pallas_call(functools.partial(close_kernel, swap=swap), out_shape=(jax...]
    pallas_call x1, Pallas kernels: 66 us -> 94.2 us  [attend(): pl.pallas_call(functools.partial(attention_kernel, units=units, pieces=pi...]
    unnamed x43 -> x46, local copies, waits for them, and re-layouts: 10.8 us -> 11.9 us
where the time goes in v3:
time: 363 us; the launch traced here: 356 us
  Pallas kernels  324 us (89%)
  local copies, waits for them, and re-layouts  18.9 us (5%)
  other arithmetic  11.3 us (3%)
    pallas_call x1, Pallas kernels, close(): pl.pallas_call(functools.partial(close_kernel, swap=swap), out_shape=(jax...  125 us
    pallas_call x1, Pallas kernels, attend(): pl.pallas_call(functools.partial(attention_kernel, units=units, pieces=pi...  94.2 us
    pallas_call x1, Pallas kernels, feed_forward(): pl.pallas_call(feed_kernel, out_shape=(jax.ShapeDtypeStruct((4, LINE, row...  54.4 us
    pallas_call x1, Pallas kernels, enter(): pl.pallas_call(enter_kernel, out_shape=(jax.ShapeDtypeStruct((GROUP,) + h...  38.6 us
    unnamed x46, local copies, waits for them, and re-layouts  11.9 us
    pallas_call x1, Pallas kernels, widen(): pl.pallas_call(functools.partial(widen_kernel, swap=swap, lanes=lanes, ff...  10.5 us

profile of v3, /device:TPU:0, one launch (start us, length us, event | category | flops | bytes accessed | tf_op | source)
XLA Modules:
  0.0 356.1 jit_solution(14730843218961833187)
XLA Ops:
  0.7 0.7 pad_add_fusion
  1.5 1.2 convert_reduce_fusion
  2.7 1.3 fusion.9
  4.0 1.3 dynamic-slice_convert_fusion
  5.3 4.2 %concatenate.9 = bf16[52,128]{1,0:T(8,128)(2,1)S(1)} concatenate(bf16[4,128]{1,0:T(4,128)(2,1)} %bitcast.108, bf16[4,128]{1,0:T(4,128)(2,1)} %bitcast.109, bf16[4,128]{1,0:T(4,128)(2,1)} %bitcast.110, bf16[4,128]{1,0:T(4,128)(2,1)} %bitcast.111, bf16[12,128]{1,0:T(8,128)(2,1)} %bitcast.103, bf16[4,128]{1,0:T(4,128)(2,1)} %bitcast.112, bf16[16,128]{1,0:T(8,128)(2,1)} %bitcast.102, ...), dimensions={0} | concatenate | bytes 26624 | tf_op jit(solution)/shard_map/concatenate | solution.py:1824
  10.0 1.1 copy-done
  11.1 38.6 %enter.1 = (bf16[8,256,1024]{2,1,0:T(8,128)(2,1)}, s32[4,8,128]{2,1,0:T(8,128)S(1)}, f32[2,52,128]{2,1,0:T(8,128)S(1)}, bf16[2,512,384]{2,1,0:T(8,128)(2,1)S(1)}...) custom-call(bf16[256,1024]{1,0:T(8,128)(2,1)S(1)} %bitcast.77, s32[8,128]{1,0:T(8,128)S(1)} %broadcast_in_dim.75.ints, ...), custom_call_target="tpu_custom_call" | custom-call | tf_op jit(solution)/shard_map/enter/pallas_call | solution.py:689
  49.8 1.1 copy-done.7
  50.9 0.9 copy-done.8
  52.5 54.4 %feed_forward.1 = (bf16[4,4,512,128]{3,2,1,0:T(8,128)(2,1)}, bf16[8,256,1024]{2,1,0:T(8,128)(2,1)}, bf16[2,512,512]{2,1,0:T(8,128)(2,1)}, bf16[2048,512]{1,0:T(8...) custom-call(bf16[3,2048,128]{2,1,0:T(8,128)(2,1)} %copy-done.7, ...), custom_call_target="tpu_custom_call" | custom-call | tf_op jit(solution)/shard_map/feed_forward/pallas_call | solution.py:883
  107.0 1.6 copy-done.5
  108.6 0.7 sort_units.1
  109.3 1.3 copy-done.3
  110.6 94.2 %attend.1 = (bf16[4,2048,128]{2,1,0:T(8,128)(2,1)}, bf16[2,2,512,2048]{3,2,1,0:T(8,128)(2,1)}) custom-call(s32[1,128]{1,0:T(1,128)} %copy-done.13, bf16[4,2048,128]{2,1,0:T(8,128)(2,1)} %bitcast.79, f32[16,128]{1,0:T(8,128)} %copy-done.12, f32[16,128]{1,0:T(8,128)} %copy-done.11, f32[128,128]{1,0:T(8,128)} %copy-done.10, f32[128,128]{1,0:T(8,128)} %copy-done.9, ...), custom_call_target="tpu_custom_call" | custom-call | tf_op jit(solution)/shard_map/attend/pallas_call | solution.py:1319
  204.8 1.6 copy-done.6
  206.4 0.7 restore_units.1
  207.1 1.3 copy-done.2
  208.4 125.2 %close.1 = (bf16[2,2,544,1024]{3,2,1,0:T(8,128)(2,1)}, f32[256,1024]{1,0:T(8,128)}, f32[256,1024]{1,0:T(8,128)}) custom-call(bf16[4,4,512,128]{3,2,1,0:T(8,128)(2,1)} %bitcast.78, bf16[2048,512]{1,0:T(8,128)(2,1)} %get-tuple-element.42.active_src, bf16[2048,512]{1,0:T(8,128)(2,1)} %get-tuple-element.43.grad_expanded_src, bf16[1024,512]{1,0:T(8,128)(2,1)} %bitcast.87, ...), custom_call_target="tpu_custom_call" | custom-call | tf_op jit(solution)/shard_map/close/pallas_call | solution.py:1671
  333.6 1.6 fusion.23
  335.2 3.1 fusion.8
  338.3 1.0 slice_convert_fusion
  339.7 0.7 dynamic_slice.49
  342.2 2.3 copy-done.4
  344.5 10.5 %widen.1 = (f32[512,4096]{1,0:T(8,128)}, f32[2048,1024]{1,0:T(8,128)}, f32[512,3072]{1,0:T(8,128)}, f32[512,1024]{1,0:T(8,128)}) custom-call(bf16[2,2,512,2048]{3,2,1,0:T(8,128)(2,1)} %get-tuple-element.53.feed_all, bf16[2,2,544,1024]{3,2,1,0:T(8,128)(2,1)S(1)} %copy-done.4), custom_call_target="tpu_custom_call" | custom-call | tf_op jit(solution)/shard_map/widen/pallas_call | solution.py:1762
  (67 shorter events, 4.0 us)
Async XLA Ops:
  9.7 97.3 %copy-start.11 = (f32[16,128]{1,0:T(8,128)}, f32[16,128]{1,0:T(8,128)S(1)}, u32[]{:S(2)}) copy-start(f32[16,128]{1,0:T(8,128)S(1)} %get-tuple-element.73.unit_sin) | copy-start | bytes 24580
  9.7 97.3 %copy-start.12 = (f32[16,128]{1,0:T(8,128)}, f32[16,128]{1,0:T(8,128)S(1)}, u32[]{:S(2)}) copy-start(f32[16,128]{1,0:T(8,128)S(1)} %get-tuple-element.74.unit_cos) | copy-start | bytes 24580
  10.0 97.0 %copy-start.9 = (f32[128,128]{1,0:T(8,128)}, f32[128,128]{1,0:T(8,128)S(1)}, u32[]{:S(2)}) copy-start(f32[128,128]{1,0:T(8,128)S(1)} %get-tuple-element.71.row_sin) | copy-start | bytes 196612
  10.0 97.0 %copy-start.10 = (f32[128,128]{1,0:T(8,128)}, f32[128,128]{1,0:T(8,128)S(1)}, u32[]{:S(2)}) copy-start(f32[128,128]{1,0:T(8,128)S(1)} %get-tuple-element.72.row_cos) | copy-start | bytes 196612
  10.0 1.1 copy-start
  49.8 1.1 copy-start.7
  50.9 0.9 copy-start.8
  51.8 55.2 %copy-start.13 = (s32[1,128]{1,0:T(1,128)}, s32[1,128]{1,0:T(1,128)S(1)}, u32[]{:S(2)}) copy-start(s32[1,128]{1,0:T(1,128)S(1)} %fusion.18.order.ints) | copy-start | bytes 1540
  107.0 1.6 copy-start.5
  109.3 1.3 copy-start.3
  110.6 94.2 %copy-start.14 = (s32[1,128]{1,0:T(1,128)S(1)}, s32[1,128]{1,0:T(1,128)}, u32[]{:S(2)}) copy-start(s32[1,128]{1,0:T(1,128)} %copy-done.13) | copy-start | bytes 1540
  204.8 1.6 copy-start.6
  207.1 1.3 copy-start.2
  208.4 125.2 %copy-start.1 = (bf16[1,256,1024]{2,1,0:T(8,128)(2,1)S(1)}, bf16[1,256,1024]{2,1,0:T(8,128)(2,1)}, u32[]{:S(2)}) copy-start(bf16[1,256,1024]{2,1,0:T(8,128)(2,1)} %param.16) | copy-start | bytes 1572868
  208.4 126.8 %copy-start.15 = (bf16[1,256,1024]{2,1,0:T(8,128)(2,1)S(1)}, bf16[1,256,1024]{2,1,0:T(8,128)(2,1)}, u32[]{:S(2)}) copy-start(bf16[1,256,1024]{2,1,0:T(8,128)(2,1)} %param.31) | copy-start | bytes 1572868
  339.6 15.4 %copy-start.16 = (f32[512]{0:T(512)}, f32[512]{0:T(512)S(1)}, u32[]{:S(2)}) copy-start(f32[512]{0:T(512)S(1)} %dynamic_slice.50) | copy-start | bytes 6148
  342.2 2.3 copy-start.4

commit v4 on v3

--- a/solution.py
+++ b/solution.py
@@ -425,6 +425,7 @@
 SPAN = 512
 CHUNK = 32
 FEED_CHUNK = 16
+EVERY = 4
 
 
 def place_here():
@@ -912,7 +913,7 @@
 
 
 class LineSum:
-    KINDS = 8
+    KINDS = 9
 
     def __init__(self, grad, result, inbox, sems, swap, size, lag, place):
         self.grad, self.result, self.inbox, self.sems, self.swap = grad, result, inbox, sems, swap
@@ -965,6 +966,19 @@
 
         return make
 
+    def keeps(self, chunk):
+        rows, swap = self.rows(chunk), self.swap
+        own = pl.ds(pl.multiple_of(self.y * swap, swap), swap)
+        plain = pl.ds(2 * swap, self.grad.shape[1] - 2 * swap)
+        return [
+            pltpu.make_async_copy(
+                self.grad.at[rows, lanes],
+                self.result.at[self.c, self.x, rows, lanes],
+                self.sems.at[2 * self.KINDS - 2 + index, chunk],
+            )
+            for index, lanes in enumerate((own, plain))
+        ]
+
     def slot(self, t):
         for half in range(2):
             self.half_slot(t, half)
@@ -1019,10 +1033,8 @@
                 )
                 self.grad[rows] = total.astype(jnp.bfloat16)
                 moves("swap").start()
-                own = pl.ds(pl.multiple_of(self.y * swap, swap), swap)
-                plain = pl.ds(2 * swap, self.grad.shape[1] - 2 * swap)
-                self.result[self.c, self.x, rows, own] = self.grad[rows, own]
-                self.result[self.c, self.x, rows, plain] = self.grad[rows, plain]
+                for copy in self.keeps(index):
+                    copy.start()
 
         event(jnp.where(owner, 2 * lag, jnp.where(at == 2, lag, 0)), reduce)
 
@@ -1030,6 +1042,8 @@
             @pl.when(owner)
             def _():
                 moves("swap").wait_recv()
+                for copy in self.keeps(index):
+                    copy.wait()
                 moves("down").start()
 
             @pl.when(at == 0)
@@ -1088,267 +1102,33 @@
             lax.fori_loop(0, size, finish, 0)
 
 
-def sort_kernel(order, src, dst, *, units, back):
+def sort_kernel(order, src, dst, *, units):
     for unit in range(units):
-        place = order[0, unit]
-        if back:
-            dst[:, unit] = src[:, place]
-        else:
-            dst[:, place] = src[:, unit]
-
-
-def sort_units(order, array, units, back):
+        dst[:, order[0, unit]] = src[:, unit]
+
+
+def sort_units(order, array, units):
     shape = array.shape
     vmem = pl.BlockSpec(memory_space=pltpu.VMEM)
     view = (shape[0], units, UNIT, shape[-1])
     return pl.pallas_call(
-        functools.partial(sort_kernel, units=units, back=back),
+        functools.partial(sort_kernel, units=units),
         out_shape=jax.ShapeDtypeStruct(view, array.dtype),
         in_specs=[pl.BlockSpec(memory_space=pltpu.SMEM), vmem],
         out_specs=vmem,
         compiler_params=pltpu.CompilerParams(vmem_limit_bytes=16 << 20),
-        name="restore_units" if back else "sort_units",
+        name="sort_units",
     )(order, array.reshape(view))
 
 
-def attention_kernel(
+def middle_kernel(
     ints,
-    parts,
+    sorted_parts,
     unit_cos,
     unit_sin,
     row_cos,
     row_sin,
     feed_grad,
-    out,
-    feed_all,
-    masked,
-    flat,
-    scores,
-    slopes,
-    key_sum,
-    value_sum,
-    mixed_sum,
-    query_sum,
-    feed_own,
-    feed_inbox,
-    feed_sems,
-    local,
-    *,
-    units,
-    pieces,
-    swap,
-):
-    here = place_here()
-    greet_line(here)
-    load = pltpu.make_async_copy(feed_grad, feed_own, local)
-    load.start()
-    load.wait()
-    line = LineSum(feed_own, feed_all, feed_inbox, feed_sems, swap, FEED_CHUNK, 2, here)
-    length = parts.shape[1]
-    scale = 1.0 / math.sqrt(HEAD)
-    blocks = length // SPAN
-    lanes = lax.broadcasted_iota(jnp.int32, (UNIT, 2 * HEAD), 1)
-    lower = lanes < HEAD
-
-    def arrange(index, carry):
-        @pl.when(lax.rem(index, 4) == 0)
-        def _():
-            line.slot(lax.div(index, 4))
-
-        at = pl.ds(pl.multiple_of(index * UNIT, UNIT), UNIT)
-        for which in range(4):
-            rows = parts[which, at, :].astype(jnp.float32)
-            if which == 0:
-                rows = rows * scale
-            masked[which, 0, at, :] = jnp.where(lower, rows, 0.0).astype(jnp.bfloat16)
-            masked[which, 1, at, :] = jnp.where(lower, 0.0, rows).astype(jnp.bfloat16)
-            flat[which, :, at] = rows.T.astype(jnp.bfloat16)
-        return carry
-
-    lax.fori_loop(0, units, arrange, 0)
-    early = -(-units // 4)
-    key_sum[...] = jnp.zeros_like(key_sum)
-    value_sum[...] = jnp.zeros_like(value_sum)
-
-    def labels(positions):
-        found = jnp.full(positions.shape, -1, jnp.int32)
-        for piece in range(pieces):
-            start = ints[0, units + piece]
-            found = jnp.where(
-                (positions >= start) & (positions < start + PIECE), piece, found
-            )
-        return found
-
-    def dot(a, b):
-        return jnp.dot(a, b, preferred_element_type=jnp.float32)
-
-    for block in range(blocks):
-        begin = block * SPAN
-        last = SPAN + (UNIT if block + 1 < blocks else 0)
-        columns = pl.ds(begin, SPAN)
-        row_at = begin + lax.broadcasted_iota(jnp.int32, (1, SPAN), 1)
-        col_at = begin + lax.broadcasted_iota(jnp.int32, (last, 1), 0)
-        row_lab = labels(row_at)
-        col_lab = labels(col_at)
-        allowed = (col_at <= row_at) | (
-            (col_lab == row_lab) & (row_lab >= 0)
-        )
-
-        def one_head(head, carry):
-            start_tick = 3 * block * (block + 1) + head * 3 * (block + 1)
-
-            def tick(index):
-                at = start_tick + index
-
-                @pl.when(lax.rem(at, 2) == 0)
-                def _():
-                    line.slot(early + lax.div(at, 2))
-
-            queries = flat[0, :, columns]
-            grads = flat[3, :, columns]
-            side = pl.ds(pl.multiple_of(head * HEAD, HEAD), HEAD)
-
-            def score_tile(start, size, top, mask=None):
-                rows = pl.ds(start, size)
-                tile = dot(masked[1, head, rows, :], queries)
-                if mask is not None:
-                    tile = jnp.where(mask, tile, NEGATIVE)
-                scores[rows, :] = tile
-                return jnp.maximum(top, jnp.max(tile, axis=0, keepdims=True))
-
-            def tile_step(step, run, j, carry):
-                tick(step * (block + 1) + j)
-                start = pl.multiple_of(j * SPAN, SPAN)
-                return run(start, SPAN, carry)
-
-            top = lax.fori_loop(
-                0,
-                block,
-                functools.partial(tile_step, 0, score_tile),
-                jnp.full((1, SPAN), NEGATIVE, jnp.float32),
-            )
-            tick(block)
-            top = score_tile(begin, last, top, allowed)
-
-            def weight_tile(start, size, sums):
-                total, delta = sums
-                rows = pl.ds(start, size)
-                weights = jnp.exp(scores[rows, :] - top)
-                slope = dot(masked[2, head, rows, :], grads)
-                scores[rows, :] = weights
-                slopes[rows, :] = slope
-                return (
-                    total + jnp.sum(weights, axis=0, keepdims=True),
-                    delta + jnp.sum(weights * slope, axis=0, keepdims=True),
-                )
-
-            zero = jnp.zeros((1, SPAN), jnp.float32)
-            sums = lax.fori_loop(
-                0,
-                block,
-                functools.partial(tile_step, 1, weight_tile),
-                (zero, zero),
-            )
-            tick(2 * block + 1)
-            total, delta = weight_tile(begin, last, sums)
-            inverse = 1.0 / total
-            delta = delta * inverse
-
-            def grad_tile(start, size, sums):
-                mixed, query = sums
-                rows = pl.ds(start, size)
-                probs = scores[rows, :] * inverse
-                grad = (probs * (slopes[rows, :] - delta)).astype(jnp.bfloat16)
-                probs = probs.astype(jnp.bfloat16)
-                value_sum[rows, :] += dot(probs, masked[3, head, columns, :])
-                key_sum[rows, :] += dot(grad, masked[0, head, columns, :])
-                mixed = mixed + dot(flat[2, side, rows], probs)
-                query = query + dot(flat[1, side, rows], grad)
-                return (mixed, query)
-
-            none = jnp.zeros((HEAD, SPAN), jnp.float32)
-            sums = lax.fori_loop(
-                0,
-                block,
-                functools.partial(tile_step, 2, grad_tile),
-                (none, none),
-            )
-            tick(3 * block + 2)
-            mixed, query = grad_tile(begin, last, sums)
-            mixed_sum[side, columns] = mixed
-            query_sum[side, columns] = query * scale
-            return carry
-
-        lax.fori_loop(0, 2, one_head, 0)
-
-    lane = lax.rem(lax.broadcasted_iota(jnp.int32, row_cos.shape, 1), HEAD)
-
-    def finish(index, carry):
-        at = pl.ds(pl.multiple_of(index * UNIT, UNIT), UNIT)
-        base_cos, base_sin = unit_cos[pl.ds(index, 1), :], unit_sin[pl.ds(index, 1), :]
-        cosine = base_cos * row_cos[...] - base_sin * row_sin[...]
-        sine = base_sin * row_cos[...] + base_cos * row_sin[...]
-        sine_up = jnp.where(lane < HALF, sine, 0.0)
-        sine_down = jnp.where(lane < HALF, 0.0, sine)
-
-        def turn_back(rows):
-            up = pltpu.roll(rows, 2 * HEAD - HALF, 1)
-            down = pltpu.roll(rows, HALF, 1)
-            return rows * cosine + up * sine_up - down * sine_down
-
-        out[0, at, :] = mixed_sum[:, at].T.astype(jnp.bfloat16)
-        out[1, at, :] = turn_back(query_sum[:, at].T).astype(jnp.bfloat16)
-        out[2, at, :] = turn_back(key_sum[at, :]).astype(jnp.bfloat16)
-        out[3, at, :] = value_sum[at, :].astype(jnp.bfloat16)
-        return carry
-
-    lax.fori_loop(0, units, finish, 0)
-
-    def more(slot, carry):
-        line.slot(slot)
-        return carry
-
-    ticked = early + (3 * blocks * (blocks + 1) + 1) // 2
-    lax.fori_loop(ticked, max(line.slots, ticked), more, 0)
-    line.drain()
-
-
-def attend(ints, parts, tables, feed_grad, units, pieces, swap):
-    length = parts.shape[1]
-    vmem = pl.BlockSpec(memory_space=pltpu.VMEM)
-    return pl.pallas_call(
-        functools.partial(attention_kernel, units=units, pieces=pieces, swap=swap),
-        out_shape=(
-            jax.ShapeDtypeStruct(parts.shape, parts.dtype),
-            jax.ShapeDtypeStruct((2, 2) + feed_grad.shape, feed_grad.dtype),
-        ),
-        in_specs=[pl.BlockSpec(memory_space=pltpu.SMEM)]
-        + [vmem] * 5
-        + [pl.BlockSpec(memory_space=pl.ANY)],
-        out_specs=[vmem, vmem],
-        scratch_shapes=[
-            pltpu.VMEM((4, 2, length, 2 * HEAD), jnp.bfloat16),
-            pltpu.VMEM((4, 2 * HEAD, length), jnp.bfloat16),
-            pltpu.VMEM((length, SPAN), jnp.float32),
-            pltpu.VMEM((length, SPAN), jnp.float32),
-            pltpu.VMEM((length, 2 * HEAD), jnp.float32),
-            pltpu.VMEM((length, 2 * HEAD), jnp.float32),
-            pltpu.VMEM((2 * HEAD, length), jnp.float32),
-            pltpu.VMEM((2 * HEAD, length), jnp.float32),
-            pltpu.VMEM(feed_grad.shape, jnp.bfloat16),
-            pltpu.VMEM((2,) + feed_grad.shape, jnp.bfloat16),
-            pltpu.SemaphoreType.DMA((2 * LineSum.KINDS, feed_grad.shape[0] // FEED_CHUNK)),
-            pltpu.SemaphoreType.DMA,
-        ],
-        compiler_params=pltpu.CompilerParams(
-            collective_id=2, has_side_effects=True, vmem_limit_bytes=56 << 20
-        ),
-        name="attend",
-    )(ints, parts, *tables, feed_grad)
-
-
-def close_kernel(
-    done,
     active_src,
     grad_expanded_src,
     we_src,
@@ -1359,22 +1139,514 @@
     cots_src,
     vectors,
     feed_sums,
+    feed_all,
     attn_all,
     out_sum,
     term_sum,
+    done,
+    feed_own,
+    feed_inbox,
     parts,
-    first,
-    stats,
-    outs,
-    terms,
     attn_own,
     attn_inbox,
     near,
-    pair,
     beside,
-    single,
     far,
     totals,
+    send,
+    recv,
+    feed_sems,
+    attn_sems,
+    near_sems,
+    beside_sems,
+    far_sems,
+    local,
+    loads,
+    *,
+    units,
+    pieces,
+    feed_swap,
+    swap,
+):
+    place = place_here()
+    c, y, x, z = place
+    core = device_at(1 - c, y, x, z)
+    over_x = device_at(c, y, 1 - x, z)
+    over_y = device_at(c, 1 - y, x, z)
+    inner = 2 * x + c
+
+    def rows_of(src, dst):
+        count = dst.shape[0]
+        return src.at[pl.ds(pl.multiple_of(inner * count, count), count)]
+
+    first_load = pltpu.make_async_copy(feed_grad, feed_own, loads.at[8])
+    first_load.start()
+    peers = [lax.rem(z + d, LINE) for d in range(1, LINE)]
+    greet([device_at(c, y, x, peer) for peer in peers] + [core, over_x, over_y])
+    first_load.wait()
+    line = LineSum(feed_own, feed_all, feed_inbox, feed_sems, feed_swap, FEED_CHUNK, 2, place)
+    lanes = done.shape[2]
+    rows = done.shape[1] // LINE
+    mine = pl.ds(pl.multiple_of(z * rows, rows), rows)
+
+    def gather(index, which):
+        peer = peers[index]
+        return remote(
+            done.at[which, pl.ds(pl.multiple_of(peer * rows, rows), rows)],
+            parts.at[mine, pl.ds(which * lanes, lanes)],
+            send.at[index, which],
+            recv.at[index, which],
+            device_at(c, y, x, peer),
+        )
+
+    def gather_own(which):
+        return pltpu.make_async_copy(
+            done.at[which, mine], parts.at[mine, pl.ds(which * lanes, lanes)], local.at[which]
+        )
+
+    def attention_phase(
+        masked, flat, scores, slopes, key_sum, value_sum, mixed_sum, query_sum
+    ):
+        length = sorted_parts.shape[1]
+        scale = 1.0 / math.sqrt(HEAD)
+        blocks = length // SPAN
+        lanes = lax.broadcasted_iota(jnp.int32, (UNIT, 2 * HEAD), 1)
+        lower = lanes < HEAD
+
+        def arrange(index, carry):
+            @pl.when(lax.rem(index, 8) == 0)
+            def _():
+                line.slot(lax.div(index, 8))
+
+            at = pl.ds(pl.multiple_of(index * UNIT, UNIT), UNIT)
+            for which in range(4):
+                rows = sorted_parts[which, at, :].astype(jnp.float32)
+                if which == 0:
+                    rows = rows * scale
+                masked[which, 0, at, :] = jnp.where(lower, rows, 0.0).astype(jnp.bfloat16)
+                masked[which, 1, at, :] = jnp.where(lower, 0.0, rows).astype(jnp.bfloat16)
+                flat[which, :, at] = rows.T.astype(jnp.bfloat16)
+            return carry
+
+        lax.fori_loop(0, units, arrange, 0)
+        early = -(-units // 8)
+        key_sum[...] = jnp.zeros_like(key_sum)
+        value_sum[...] = jnp.zeros_like(value_sum)
+
+        def labels(positions):
+            found = jnp.full(positions.shape, -1, jnp.int32)
+            for piece in range(pieces):
+                start = ints[0, units + piece]
+                found = jnp.where(
+                    (positions >= start) & (positions < start + PIECE), piece, found
+                )
+            return found
+
+        def dot(a, b):
+            return jnp.dot(a, b, preferred_element_type=jnp.float32)
+
+        for block in range(blocks):
+            begin = block * SPAN
+            last = SPAN + (UNIT if block + 1 < blocks else 0)
+            columns = pl.ds(begin, SPAN)
+            row_at = begin + lax.broadcasted_iota(jnp.int32, (1, SPAN), 1)
+            col_at = begin + lax.broadcasted_iota(jnp.int32, (last, 1), 0)
+            row_lab = labels(row_at)
+            col_lab = labels(col_at)
+            allowed = (col_at <= row_at) | (
+                (col_lab == row_lab) & (row_lab >= 0)
+            )
+
+            def one_head(head, carry):
+                start_tick = 3 * block * (block + 1) + head * 3 * (block + 1)
+
+                def tick(index):
+                    at = start_tick + index
+
+                    @pl.when(lax.rem(at, EVERY) == 0)
+                    def _():
+                        line.slot(early + lax.div(at, EVERY))
+
+                queries = flat[0, :, columns]
+                grads = flat[3, :, columns]
+                side = pl.ds(pl.multiple_of(head * HEAD, HEAD), HEAD)
+
+                def score_tile(start, size, top, mask=None):
+                    rows = pl.ds(start, size)
+                    tile = dot(masked[1, head, rows, :], queries)
+                    if mask is not None:
+                        tile = jnp.where(mask, tile, NEGATIVE)
+                    scores[rows, :] = tile
+                    return jnp.maximum(top, jnp.max(tile, axis=0, keepdims=True))
+
+                def tile_step(step, run, j, carry):
+                    tick(step * (block + 1) + j)
+                    start = pl.multiple_of(j * SPAN, SPAN)
+                    return run(start, SPAN, carry)
+
+                top = lax.fori_loop(
+                    0,
+                    block,
+                    functools.partial(tile_step, 0, score_tile),
+                    jnp.full((1, SPAN), NEGATIVE, jnp.float32),
+                )
+                tick(block)
+                top = score_tile(begin, last, top, allowed)
+
+                def weight_tile(start, size, sums):
+                    total, delta = sums
+                    rows = pl.ds(start, size)
+                    weights = jnp.exp(scores[rows, :] - top)
+                    slope = dot(masked[2, head, rows, :], grads)
+                    scores[rows, :] = weights
+                    slopes[rows, :] = slope
+                    return (
+                        total + jnp.sum(weights, axis=0, keepdims=True),
+                        delta + jnp.sum(weights * slope, axis=0, keepdims=True),
+                    )
+
+                zero = jnp.zeros((1, SPAN), jnp.float32)
+                sums = lax.fori_loop(
+                    0,
+                    block,
+                    functools.partial(tile_step, 1, weight_tile),
+                    (zero, zero),
+                )
+                tick(2 * block + 1)
+                total, delta = weight_tile(begin, last, sums)
+                inverse = 1.0 / total
+                delta = delta * inverse
+
+                def grad_tile(start, size, sums):
+                    mixed, query = sums
+                    rows = pl.ds(start, size)
+                    probs = scores[rows, :] * inverse
+                    grad = (probs * (slopes[rows, :] - delta)).astype(jnp.bfloat16)
+                    probs = probs.astype(jnp.bfloat16)
+                    value_sum[rows, :] += dot(probs, masked[3, head, columns, :])
+                    key_sum[rows, :] += dot(grad, masked[0, head, columns, :])
+                    mixed = mixed + dot(flat[2, side, rows], probs)
+                    query = query + dot(flat[1, side, rows], grad)
+                    return (mixed, query)
+
+                none = jnp.zeros((HEAD, SPAN), jnp.float32)
+                sums = lax.fori_loop(
+                    0,
+                    block,
+                    functools.partial(tile_step, 2, grad_tile),
+                    (none, none),
+                )
+                tick(3 * block + 2)
+                mixed, query = grad_tile(begin, last, sums)
+                mixed_sum[side, columns] = mixed
+                query_sum[side, columns] = query * scale
+                return carry
+
+            lax.fori_loop(0, 2, one_head, 0)
+
+        lane = lax.rem(lax.broadcasted_iota(jnp.int32, row_cos.shape, 1), HEAD)
+        ticked = early - (-3 * blocks * (blocks + 1) // EVERY)
+
+        def finish(index, carry):
+            @pl.when(lax.rem(index, 8) == 0)
+            def _():
+                line.slot(ticked + lax.div(index, 8))
+
+            at = pl.ds(pl.multiple_of(index * UNIT, UNIT), UNIT)
+            base_cos, base_sin = unit_cos[pl.ds(index, 1), :], unit_sin[pl.ds(index, 1), :]
+            cosine = base_cos * row_cos[...] - base_sin * row_sin[...]
+            sine = base_sin * row_cos[...] + base_cos * row_sin[...]
+            sine_up = jnp.where(lane < HALF, sine, 0.0)
+            sine_down = jnp.where(lane < HALF, 0.0, sine)
+
+            def turn_back(rows):
+                up = pltpu.roll(rows, 2 * HEAD - HALF, 1)
+                down = pltpu.roll(rows, HALF, 1)
+                return rows * cosine + up * sine_up - down * sine_down
+
+            masked[0, 0, at, :] = mixed_sum[:, at].T.astype(jnp.bfloat16)
+            masked[1, 0, at, :] = turn_back(query_sum[:, at].T).astype(jnp.bfloat16)
+            masked[2, 0, at, :] = turn_back(key_sum[at, :]).astype(jnp.bfloat16)
+            masked[3, 0, at, :] = value_sum[at, :].astype(jnp.bfloat16)
+            return carry
+
+        lax.fori_loop(0, units, finish, 0)
+        ticked += -(-units // 8)
+
+        def restore(owner):
+            for index in range(units // LINE):
+                unit = owner * (units // LINE) + index
+                here = pl.ds(pl.multiple_of(unit * UNIT, UNIT), UNIT)
+                place = ints[0, unit]
+                for which in range(4):
+                    rows = masked[which, 0, pl.ds(0, UNIT), :]
+                    for other in range(1, units):
+                        rows = jnp.where(
+                            place == other, masked[which, 0, pl.ds(other * UNIT, UNIT), :], rows
+                        )
+                    done[which, here, :] = rows
+
+        for index, peer in enumerate(peers):
+            restore(peer)
+            for which in (1, 2, 3, 0):
+                gather(index, which).start()
+        restore(z)
+        for which in range(4):
+            gather_own(which).start()
+
+
+    length = sorted_parts.shape[1]
+    ticked = (
+        2 * -(-units // 8) - (-3 * (length // SPAN) * (length // SPAN + 1) // EVERY)
+    )
+    pl.run_scoped(
+        attention_phase,
+        pltpu.VMEM((4, 2, length, 2 * HEAD), jnp.bfloat16),
+        pltpu.VMEM((4, 2 * HEAD, length), jnp.bfloat16),
+        pltpu.VMEM((length, SPAN), jnp.float32),
+        pltpu.VMEM((length, SPAN), jnp.float32),
+        pltpu.VMEM((length, 2 * HEAD), jnp.float32),
+        pltpu.VMEM((length, 2 * HEAD), jnp.float32),
+        pltpu.VMEM((2 * HEAD, length), jnp.float32),
+        pltpu.VMEM((2 * HEAD, length), jnp.float32),
+    )
+
+    def close_phase(
+        stats, outs, terms, single, active, grad_expanded, we, wc, wm, wo, hidden, cots
+    ):
+        sources = (
+            (hidden_src, hidden),
+            (grad_expanded_src, grad_expanded),
+            (we_src, we),
+            (active_src, active),
+            (rows_of(wc_src, wc), wc),
+            (cots_src, cots),
+            (wm_src, wm),
+            (rows_of(wo_src, wo), wo),
+        )
+        fetched = []
+        for index, (src, dst) in enumerate(sources):
+            copy = pltpu.make_async_copy(src, dst, loads.at[index])
+            copy.start()
+            fetched.append(copy)
+        gain_one, shift_one, gain_two = vectors[0:1, :], vectors[1:2, :], vectors[2:3, :]
+        width = hidden.shape[1]
+        half = width // 2
+        totals[...] = jnp.zeros_like(totals)
+        for copy in fetched:
+            copy.wait()
+
+        def before(index, carry):
+            at = pl.ds(pl.multiple_of(index * TILE, TILE), TILE)
+            raw = hidden[at, :].astype(jnp.float32)
+            mean = jnp.mean(raw, axis=1, keepdims=True)
+            centred = raw - mean
+            rstd = lax.rsqrt(jnp.mean(centred * centred, axis=1, keepdims=True) + EPS)
+            stats[0, at, :] = jnp.broadcast_to(mean, (TILE, stats.shape[2]))
+            stats[1, at, :] = jnp.broadcast_to(rstd, (TILE, stats.shape[2]))
+            xhat = centred * rstd
+            grad_second = dot_rows(grad_expanded[at, :], we[...])
+            terms[index] = (grad_second * gain_two).astype(jnp.bfloat16)
+            outs[index] = dot_plain(active[at, :], wc[...]).astype(jnp.bfloat16)
+            totals[2:3, :] += jnp.sum(grad_second * xhat, axis=0, keepdims=True)
+            totals[3:4, :] += jnp.sum(grad_second, axis=0, keepdims=True)
+            totals[4:5, :] += jnp.sum(cots[at, :].astype(jnp.float32), axis=0, keepdims=True)
+            return carry
+
+        tiles = hidden.shape[0] // TILE
+        lax.fori_loop(0, tiles, before, 0)
+
+        for which in range(4):
+            gather_own(which).wait()
+        for index in range(len(peers)):
+            for which in range(4):
+                gather(index, which).wait()
+
+        arrays = (outs, terms)
+
+        def block_at(cc, yy, xx):
+            return (2 * cc + yy) * 2 + xx
+
+        def to_core(a, yy, xx):
+            block = block_at(1 - c, yy, xx)
+            return remote(
+                arrays[a].at[block],
+                near.at[a, yy, xx],
+                near_sems.at[0, a, yy, xx],
+                near_sems.at[1, a, yy, xx],
+                core,
+            )
+
+        ways = ((y, x, over_y, over_x), (x, y, over_x, over_y))
+
+        def own_block(a, near_at, far_at):
+            yy, xx = (near_at, far_at) if a == 0 else (far_at, near_at)
+            return block_at(c, yy, xx)
+
+        def hop_one(a, index):
+            near_axis, far_axis, target, beyond = ways[a]
+            return remote(
+                arrays[a].at[own_block(a, 1 - near_axis, index)],
+                beside.at[a, index],
+                beside_sems.at[0, a, index],
+                beside_sems.at[1, a, index],
+                target,
+            )
+
+        def hop_two(a):
+            return remote(
+                single.at[a], far.at[a], far_sems.at[0, a], far_sems.at[1, a], ways[a][3]
+            )
+
+        def after(index):
+            at = pl.ds(pl.multiple_of(index * TILE, TILE), TILE)
+            grads = parts[at, pl.ds(lanes, 3 * lanes)]
+            grad_first = dot_rows(grads, wm[...])
+            xhat = (hidden[at, :].astype(jnp.float32) - stats[0, at, 0:1]) * stats[1, at, 0:1]
+            hidden[at, :] = (xhat * gain_one + shift_one).astype(jnp.bfloat16)
+            terms[index] = (terms[index].astype(jnp.float32) + grad_first * gain_one).astype(
+                jnp.bfloat16
+            )
+            outs[index] = (
+                outs[index].astype(jnp.float32) + dot_plain(parts[at, pl.ds(0, lanes)], wo[...])
+            ).astype(jnp.bfloat16)
+            totals[0:1, :] += jnp.sum(grad_first * xhat, axis=0, keepdims=True)
+            totals[1:2, :] += jnp.sum(grad_first, axis=0, keepdims=True)
+            totals[5:6, pl.ds(0, 3 * lanes)] += jnp.sum(
+                grads.astype(jnp.float32), axis=0, keepdims=True
+            )
+
+        def others(step, carry):
+            line.slot(ticked + step)
+            yy, xx = lax.rem(1 - y + step // 2, 2), lax.rem(step, 2)
+            after(block_at(1 - c, yy, xx))
+            for a in range(2):
+                to_core(a, yy, xx).start()
+            return carry
+
+        lax.fori_loop(0, 4, others, 0)
+
+        def ours(step, carry):
+            line.slot(ticked + 4 + step)
+            yy, xx = lax.rem(1 - y + step // 2, 2), lax.rem(step, 2)
+            after(block_at(c, yy, xx))
+            for a in range(2):
+                to_core(a, yy, xx).wait_recv()
+                block = block_at(c, yy, xx)
+                total = arrays[a][block].astype(jnp.float32) + near[a, yy, xx].astype(jnp.float32)
+                arrays[a][block] = total.astype(jnp.bfloat16)
+                near_at, far_at = (yy, xx) if a == 0 else (xx, yy)
+
+                @pl.when(near_at != ways[a][0])
+                def _():
+                    hop_one(a, far_at).start()
+
+            return carry
+
+        lax.fori_loop(0, 4, ours, 0)
+        later = ticked + 8
+        for index in range(width // TILE):
+            line.slot(later + index)
+            block = dot_tokens(hidden[:, pl.ds(index * TILE, TILE)], parts[:, pl.ds(lanes, 3 * lanes)])
+            side, row = divmod(index * TILE, half)
+            attn_own[pl.ds(row, TILE), pl.ds(side * swap, swap)] = block.astype(jnp.bfloat16)
+        block = dot_tokens(parts[:, pl.ds(0, lanes)], cots[...]).astype(jnp.bfloat16)
+        wide = 2 * lanes
+        for index in range(width // wide):
+            attn_own[pl.ds(index * lanes, lanes), pl.ds(2 * swap, wide)] = block[
+                :, index * wide : (index + 1) * wide
+            ]
+        lines = []
+        fill = jnp.zeros((1, swap), jnp.float32)
+        for index in range(5):
+            for begin in range(0, width, swap):
+                stop = min(begin + swap, width)
+                entry = totals[index : index + 1, begin:stop]
+                if stop - begin < swap:
+                    entry = jnp.concatenate([entry, fill[:, : swap - (stop - begin)]], axis=1)
+                lines.append(entry)
+        lines.append(totals[5:6, 0:swap])
+        ff = feed_sums.shape[1]
+        for begin in range(0, ff, swap):
+            stop = min(begin + swap, ff)
+            entry = feed_sums[:, begin:stop]
+            if stop - begin < swap:
+                entry = jnp.concatenate([entry, fill[:, : swap - (stop - begin)]], axis=1)
+            lines.append(entry)
+        lines += [fill] * (attn_own.shape[0] - half - len(lines))
+        small = jnp.concatenate(lines, axis=0).astype(jnp.bfloat16)
+        tail = pl.ds(half, attn_own.shape[0] - half)
+        attn_own[tail, pl.ds(0, swap)] = small
+        attn_own[tail, pl.ds(swap, swap)] = small
+        attn_own[tail, pl.ds(2 * swap, wide)] = jnp.zeros((small.shape[0], wide), jnp.bfloat16)
+
+        attn = LineSum(attn_own, attn_all, attn_inbox, attn_sems, swap, CHUNK, 1, place)
+
+        later += width // TILE
+
+        def step(t, carry):
+            attn.slot(t)
+            line.slot(later + t)
+            return carry
+
+        def pass_on(a):
+            near_axis, far_axis = ways[a][:2]
+            for index in range(2):
+                hop_one(a, index).wait()
+            single[a] = (
+                arrays[a][own_block(a, near_axis, 1 - far_axis)].astype(jnp.float32)
+                + beside[a, 1 - far_axis].astype(jnp.float32)
+            ).astype(jnp.bfloat16)
+            hop_two(a).start()
+
+        middle = attn.slots - 6
+        lax.fori_loop(0, middle, step, 0)
+        pass_on(0)
+        pass_on(1)
+        lax.fori_loop(middle, attn.slots, step, 0)
+        for a, dst in enumerate((out_sum, term_sum)):
+            hop_two(a).wait()
+            near_axis, far_axis = ways[a][:2]
+            dst[...] = (
+                arrays[a][own_block(a, near_axis, far_axis)].astype(jnp.float32)
+                + beside[a, far_axis].astype(jnp.float32)
+                + far[a].astype(jnp.float32)
+            )
+
+        def sent(step, carry):
+            for a in range(2):
+                to_core(a, step // 2, lax.rem(step, 2)).wait_send()
+            return carry
+
+        lax.fori_loop(0, 4, sent, 0)
+        attn.drain()
+        line.drain()
+
+    token_rows, width = hidden_src.shape
+    ff = active_src.shape[1]
+    block = (token_rows // GROUP, width)
+    pl.run_scoped(
+        close_phase,
+        pltpu.VMEM((2, token_rows, 128), jnp.float32),
+        pltpu.VMEM((GROUP,) + block, jnp.bfloat16),
+        pltpu.VMEM((GROUP,) + block, jnp.bfloat16),
+        pltpu.VMEM((2,) + block, jnp.bfloat16),
+        pltpu.VMEM((token_rows, ff), jnp.bfloat16),
+        pltpu.VMEM((token_rows, ff), jnp.bfloat16),
+        pltpu.VMEM((width, ff), jnp.bfloat16),
+        pltpu.VMEM((ff, width), jnp.bfloat16),
+        pltpu.VMEM((width, 3 * lanes), jnp.bfloat16),
+        pltpu.VMEM((lanes, width), jnp.bfloat16),
+        pltpu.VMEM((token_rows, width), jnp.bfloat16),
+        pltpu.VMEM((token_rows, width), jnp.bfloat16),
+    )
+
+
+def middle(
+    ints,
+    sorted_parts,
+    tables,
+    feed_grad,
     active,
     grad_expanded,
     we,
@@ -1383,306 +1655,77 @@
     wo,
     hidden,
     cots,
-    send,
-    recv,
-    attn_sems,
-    near_sems,
-    beside_sems,
-    far_sems,
-    local,
-    loads,
-    *,
-    swap,
+    vectors,
+    feed_sums,
+    tokens,
+    units,
+    pieces,
+    feed_swap,
 ):
-    place = place_here()
-    c, y, x, z = place
-    core = device_at(1 - c, y, x, z)
-    over_x = device_at(c, y, 1 - x, z)
-    over_y = device_at(c, 1 - y, x, z)
-    inner = 2 * x + c
-
-    def rows_of(src, dst):
-        count = dst.shape[0]
-        return src.at[pl.ds(pl.multiple_of(inner * count, count), count)]
-
-    sources = (
-        (hidden_src, hidden),
-        (grad_expanded_src, grad_expanded),
-        (we_src, we),
-        (active_src, active),
-        (rows_of(wc_src, wc), wc),
-        (cots_src, cots),
-        (wm_src, wm),
-        (rows_of(wo_src, wo), wo),
-    )
-    fetched = []
-    for index, (src, dst) in enumerate(sources):
-        copy = pltpu.make_async_copy(src, dst, loads.at[index])
-        copy.start()
-        fetched.append(copy)
-    barrier = pltpu.get_barrier_semaphore()
-    peers = [lax.rem(z + d, LINE) for d in range(1, LINE)]
-    partners = [device_at(c, y, x, peer) for peer in peers] + [core, over_x, over_y]
-    for partner in partners:
-        pl.semaphore_signal(barrier, inc=1, device_id=partner, device_id_type=MESH)
-    pl.semaphore_wait(barrier, len(partners))
-    rows = done.shape[2]
-    lanes = done.shape[3]
-    mine = pl.ds(pl.multiple_of(z * rows, rows), rows)
-    copies = []
-    for index, peer in enumerate(peers):
-        for which in (1, 2, 3, 0):
-            copy = remote(
-                done.at[which, peer],
-                parts.at[mine, pl.ds(which * lanes, lanes)],
-                send.at[index, which],
-                recv.at[index, which],
-                device_at(c, y, x, peer),
-            )
-            copy.start()
-            copies.append(copy)
-    owns = []
-    for which in range(4):
-        copy = pltpu.make_async_copy(
-            done.at[which, z], parts.at[mine, pl.ds(which * lanes, lanes)], local.at[which]
-        )
-        copy.start()
-        owns.append(copy)
-    gain_one, shift_one, gain_two = vectors[0:1, :], vectors[1:2, :], vectors[2:3, :]
-    width = hidden.shape[1]
-    half = width // 2
-    totals[...] = jnp.zeros_like(totals)
-    for copy in fetched:
-        copy.wait()
-
-    def before(index, carry):
-        at = pl.ds(pl.multiple_of(index * TILE, TILE), TILE)
-        raw = hidden[at, :].astype(jnp.float32)
-        mean = jnp.mean(raw, axis=1, keepdims=True)
-        centred = raw - mean
-        rstd = lax.rsqrt(jnp.mean(centred * centred, axis=1, keepdims=True) + EPS)
-        stats[0, at, :] = jnp.broadcast_to(mean, (TILE, stats.shape[2]))
-        stats[1, at, :] = jnp.broadcast_to(rstd, (TILE, stats.shape[2]))
-        xhat = centred * rstd
-        first[at, :] = (xhat * gain_one + shift_one).astype(jnp.bfloat16)
-        grad_second = dot_rows(grad_expanded[at, :], we[...])
-        terms[index] = (grad_second * gain_two).astype(jnp.bfloat16)
-        outs[index] = dot_plain(active[at, :], wc[...]).astype(jnp.bfloat16)
-        totals[2:3, :] += jnp.sum(grad_second * xhat, axis=0, keepdims=True)
-        totals[3:4, :] += jnp.sum(grad_second, axis=0, keepdims=True)
-        totals[4:5, :] += jnp.sum(cots[at, :].astype(jnp.float32), axis=0, keepdims=True)
-        return carry
-
-    lax.fori_loop(0, hidden.shape[0] // TILE, before, 0)
-    for copy in owns:
-        copy.wait()
-    for copy in copies:
-        copy.wait()
-
-    arrays = (outs, terms)
-
-    def block_at(cc, yy, xx):
-        return (2 * cc + yy) * 2 + xx
-
-    def to_core(a, yy, xx):
-        block = block_at(1 - c, yy, xx)
-        return remote(
-            arrays[a].at[block],
-            near.at[a, yy, xx],
-            near_sems.at[0, a, yy, xx],
-            near_sems.at[1, a, yy, xx],
-            core,
-        )
-
-    ways = ((y, x, over_y, over_x), (x, y, over_x, over_y))
-
-    def hop_one(a, index):
-        near_axis, far_axis, target, beyond = ways[a]
-        return remote(
-            pair.at[a, 1 - near_axis, index],
-            beside.at[a, index],
-            beside_sems.at[0, a, index],
-            beside_sems.at[1, a, index],
-            target,
-        )
-
-    def hop_two(a):
-        return remote(
-            single.at[a], far.at[a], far_sems.at[0, a], far_sems.at[1, a], ways[a][3]
-        )
-
-    def after(index):
-        at = pl.ds(pl.multiple_of(index * TILE, TILE), TILE)
-        grads = parts[at, pl.ds(lanes, 3 * lanes)]
-        grad_first = dot_rows(grads, wm[...])
-        xhat = (hidden[at, :].astype(jnp.float32) - stats[0, at, 0:1]) * stats[1, at, 0:1]
-        terms[index] = (terms[index].astype(jnp.float32) + grad_first * gain_one).astype(
-            jnp.bfloat16
-        )
-        outs[index] = (
-            outs[index].astype(jnp.float32) + dot_plain(parts[at, pl.ds(0, lanes)], wo[...])
-        ).astype(jnp.bfloat16)
-        totals[0:1, :] += jnp.sum(grad_first * xhat, axis=0, keepdims=True)
-        totals[1:2, :] += jnp.sum(grad_first, axis=0, keepdims=True)
-        totals[5:6, pl.ds(0, 3 * lanes)] += jnp.sum(
-            grads.astype(jnp.float32), axis=0, keepdims=True
-        )
-
-    def others(step, carry):
-        yy, xx = lax.rem(1 - y + step // 2, 2), lax.rem(step, 2)
-        after(block_at(1 - c, yy, xx))
-        for a in range(2):
-            to_core(a, yy, xx).start()
-        return carry
-
-    lax.fori_loop(0, 4, others, 0)
-
-    def ours(step, carry):
-        yy, xx = lax.rem(1 - y + step // 2, 2), lax.rem(step, 2)
-        after(block_at(c, yy, xx))
-        for a in range(2):
-            to_core(a, yy, xx).wait_recv()
-            total = arrays[a][block_at(c, yy, xx)].astype(jnp.float32) + near[a, yy, xx].astype(
-                jnp.float32
-            )
-            near_at, far_at = (yy, xx) if a == 0 else (xx, yy)
-            pair[a, near_at, far_at] = total.astype(jnp.bfloat16)
-
-            @pl.when(near_at != ways[a][0])
-            def _():
-                hop_one(a, far_at).start()
-
-        return carry
-
-    lax.fori_loop(0, 4, ours, 0)
-    for index in range(width // TILE):
-        block = dot_tokens(first[:, pl.ds(index * TILE, TILE)], parts[:, pl.ds(lanes, 3 * lanes)])
-        side, row = divmod(index * TILE, half)
-        attn_own[pl.ds(row, TILE), pl.ds(side * swap, swap)] = block.astype(jnp.bfloat16)
-    block = dot_tokens(parts[:, pl.ds(0, lanes)], cots[...]).astype(jnp.bfloat16)
-    wide = 2 * lanes
-    for index in range(width // wide):
-        attn_own[pl.ds(index * lanes, lanes), pl.ds(2 * swap, wide)] = block[
-            :, index * wide : (index + 1) * wide
-        ]
-    lines = []
-    fill = jnp.zeros((1, swap), jnp.float32)
-    for index in range(5):
-        for begin in range(0, width, swap):
-            stop = min(begin + swap, width)
-            line = totals[index : index + 1, begin:stop]
-            if stop - begin < swap:
-                line = jnp.concatenate([line, fill[:, : swap - (stop - begin)]], axis=1)
-            lines.append(line)
-    lines.append(totals[5:6, 0:swap])
-    ff = feed_sums.shape[1]
-    for begin in range(0, ff, swap):
-        stop = min(begin + swap, ff)
-        line = feed_sums[:, begin:stop]
-        if stop - begin < swap:
-            line = jnp.concatenate([line, fill[:, : swap - (stop - begin)]], axis=1)
-        lines.append(line)
-    lines += [fill] * (attn_own.shape[0] - half - len(lines))
-    small = jnp.concatenate(lines, axis=0).astype(jnp.bfloat16)
-    tail = pl.ds(half, attn_own.shape[0] - half)
-    attn_own[tail, pl.ds(0, swap)] = small
-    attn_own[tail, pl.ds(swap, swap)] = small
-    attn_own[tail, pl.ds(2 * swap, wide)] = jnp.zeros((small.shape[0], wide), jnp.bfloat16)
-
-    attn = LineSum(attn_own, attn_all, attn_inbox, attn_sems, swap, CHUNK, 1, place)
-
-    def step(t, carry):
-        attn.slot(t)
-        return carry
-
-    def pass_on(a):
-        near_axis, far_axis = ways[a][:2]
-        for index in range(2):
-            hop_one(a, index).wait()
-        single[a] = (
-            pair[a, near_axis, 1 - far_axis].astype(jnp.float32)
-            + beside[a, 1 - far_axis].astype(jnp.float32)
-        ).astype(jnp.bfloat16)
-        hop_two(a).start()
-
-    middle = attn.slots - 6
-    lax.fori_loop(0, middle, step, 0)
-    pass_on(0)
-    pass_on(1)
-    lax.fori_loop(middle, attn.slots, step, 0)
-    for a, dst in enumerate((out_sum, term_sum)):
-        hop_two(a).wait()
-        near_axis, far_axis = ways[a][:2]
-        dst[...] = (
-            pair[a, near_axis, far_axis].astype(jnp.float32)
-            + beside[a, far_axis].astype(jnp.float32)
-            + far[a].astype(jnp.float32)
-        )
-
-    def sent(step, carry):
-        for a in range(2):
-            to_core(a, step // 2, lax.rem(step, 2)).wait_send()
-        return carry
-
-    lax.fori_loop(0, 4, sent, 0)
-    attn.drain()
-
-
-def close(done, active, grad_expanded, we, wc, wm, wo, hidden, cots, vectors, feed_sums, tokens):
     rows, width = hidden.shape
-    lanes = done.shape[3]
-    ff = active.shape[1]
+    lanes = sorted_parts.shape[2]
     swap = 3 * lanes
     block = (tokens, width)
     vmem = pl.BlockSpec(memory_space=pltpu.VMEM)
     any_spec = pl.BlockSpec(memory_space=pl.ANY)
     grad_shape = (width // 2 + CHUNK, 2 * swap + 2 * lanes)
     scratch = [
+        pltpu.VMEM(sorted_parts.shape, jnp.bfloat16),
+        pltpu.VMEM(feed_grad.shape, jnp.bfloat16),
+        pltpu.VMEM((2,) + feed_grad.shape, jnp.bfloat16),
         pltpu.VMEM((rows, 4 * lanes), jnp.bfloat16),
-        pltpu.VMEM((rows, width), jnp.bfloat16),
-        pltpu.VMEM((2, rows, 128), jnp.float32),
-        pltpu.VMEM((GROUP,) + block, jnp.bfloat16),
-        pltpu.VMEM((GROUP,) + block, jnp.bfloat16),
         pltpu.VMEM(grad_shape, jnp.bfloat16),
         pltpu.VMEM((2,) + grad_shape, jnp.bfloat16),
         pltpu.VMEM((2, 2, 2) + block, jnp.bfloat16),
-        pltpu.VMEM((2, 2, 2) + block, jnp.bfloat16),
         pltpu.VMEM((2, 2) + block, jnp.bfloat16),
         pltpu.VMEM((2,) + block, jnp.bfloat16),
-        pltpu.VMEM((2,) + block, jnp.bfloat16),
         pltpu.VMEM((8, width), jnp.float32),
-        pltpu.VMEM((rows, ff), jnp.bfloat16),
-        pltpu.VMEM((rows, ff), jnp.bfloat16),
-        pltpu.VMEM((width, ff), jnp.bfloat16),
-        pltpu.VMEM((ff, width), jnp.bfloat16),
-        pltpu.VMEM((width, 3 * lanes), jnp.bfloat16),
-        pltpu.VMEM((lanes, width), jnp.bfloat16),
-        pltpu.VMEM((rows, width), jnp.bfloat16),
-        pltpu.VMEM((rows, width), jnp.bfloat16),
         pltpu.SemaphoreType.DMA((LINE - 1, 4)),
         pltpu.SemaphoreType.DMA((LINE - 1, 4)),
+        pltpu.SemaphoreType.DMA((2 * LineSum.KINDS, feed_grad.shape[0] // FEED_CHUNK)),
         pltpu.SemaphoreType.DMA((2 * LineSum.KINDS, grad_shape[0] // CHUNK)),
         pltpu.SemaphoreType.DMA((2, 2, 2, 2)),
         pltpu.SemaphoreType.DMA((2, 2, 2)),
         pltpu.SemaphoreType.DMA((2, 2)),
         pltpu.SemaphoreType.DMA((4,)),
-        pltpu.SemaphoreType.DMA((8,)),
+        pltpu.SemaphoreType.DMA((9,)),
     ]
     return pl.pallas_call(
-        functools.partial(close_kernel, swap=swap),
+        functools.partial(
+            middle_kernel, units=units, pieces=pieces, feed_swap=feed_swap, swap=swap
+        ),
         out_shape=(
+            jax.ShapeDtypeStruct((2, 2) + feed_grad.shape, jnp.bfloat16),
             jax.ShapeDtypeStruct((2, 2) + grad_shape, jnp.bfloat16),
             jax.ShapeDtypeStruct(block, jnp.float32),
             jax.ShapeDtypeStruct(block, jnp.float32),
         ),
-        in_specs=[any_spec] * 9 + [vmem] * 2,
-        out_specs=[vmem] * 3,
+        in_specs=[pl.BlockSpec(memory_space=pltpu.SMEM)]
+        + [vmem] * 5
+        + [any_spec] * 9
+        + [vmem] * 2,
+        out_specs=[any_spec] + [vmem] * 3,
         scratch_shapes=scratch,
         compiler_params=pltpu.CompilerParams(
             collective_id=3, has_side_effects=True, vmem_limit_bytes=60 << 20
         ),
-        name="close",
-    )(done, active, grad_expanded, we, wc, wm, wo, hidden, cots, vectors, feed_sums)
+        name="middle",
+    )(
+        ints,
+        sorted_parts,
+        *tables,
+        feed_grad,
+        active,
+        grad_expanded,
+        we,
+        wc,
+        wm,
+        wo,
+        hidden,
+        cots,
+        vectors,
+        feed_sums,
+    )
 
 
 def widen_kernel(
@@ -1852,20 +1895,14 @@
     we = we_all.reshape(width, ff_part)
     cots = cot_all.reshape(rows, width)
     own_ints = lax.dynamic_index_in_dim(ints_all[:, 0], z, 0, keepdims=True)
-    sorted_parts = sort_units(own_ints, got, units, False)
-    done, feed_all = attend(
+    sorted_parts = sort_units(own_ints, got, units)
+    swap = 3 * part
+    lines = CHUNK
+    feed_all, attn_all, out_sum, term_sum = middle(
         own_ints,
         sorted_parts.reshape(4, length, part),
         tables,
         feed_grad,
-        units,
-        pieces,
-        ff_part,
-    )
-    swap = 3 * part
-    lines = CHUNK
-    attn_all, out_sum, term_sum = close(
-        sort_units(own_ints, done, units, True).reshape(4, LINE, 2 * tokens, part),
         active,
         grad_expanded,
         we,
@@ -1877,6 +1914,9 @@
         jnp.stack([gain_one, shift_one, gain_two]),
         feed_sums,
         tokens,
+        units,
+        pieces,
+        ff_part,
     )
     expand_out, contract_out, merged_out, output_out = widen(
         feed_all, attn_all, swap, part, ff_part

time: 363 us -> 341 us (0.939)
  Pallas kernels: 324 us -> 305 us
    pallas_call x4 -> x2, Pallas kernels: 221 us -> 202 us  [the longest x1 201 us: middle(): pl.pallas_call(functools.partial(middle_kernel, units=units, pieces=piece...]
    unnamed x46 -> x40, local copies, waits for them, and re-layouts: 11.9 us -> 8.96 us
where the time goes in v4:
time: 341 us; the launch traced here: 334 us
  Pallas kernels  305 us (89%)
  local copies, waits for them, and re-layouts  16 us (5%)
  other arithmetic  11.3 us (3%)
    pallas_call x1, Pallas kernels, middle(): pl.pallas_call(functools.partial(middle_kernel, units=units, pieces=piece...  201 us
    pallas_call x1, Pallas kernels, feed_forward(): pl.pallas_call(feed_kernel, out_shape=(jax.ShapeDtypeStruct((4, LINE, row...  54.5 us
    pallas_call x1, Pallas kernels, enter(): pl.pallas_call(enter_kernel, out_shape=(jax.ShapeDtypeStruct((GROUP,) + h...  38.6 us
    pallas_call x1, Pallas kernels, widen(): pl.pallas_call(functools.partial(widen_kernel, swap=swap, lanes=lanes, ff...  10.5 us
    unnamed x40, local copies, waits for them, and re-layouts  8.96 us

profile of v4, /device:TPU:0, one launch (start us, length us, event | category | flops | bytes accessed | tf_op | source)
XLA Modules:
  0.0 333.8 jit_solution(4892000827359136163)
XLA Ops:
  0.7 0.7 pad_add_fusion
  1.5 1.2 convert_reduce_fusion
  2.7 1.3 fusion.9
  4.0 1.3 dynamic-slice_convert_fusion
  5.3 4.2 %concatenate.9 = bf16[52,128]{1,0:T(8,128)(2,1)S(1)} concatenate(bf16[4,128]{1,0:T(4,128)(2,1)} %bitcast.104, bf16[4,128]{1,0:T(4,128)(2,1)} %bitcast.105, bf16[4,128]{1,0:T(4,128)(2,1)} %bitcast.106, bf16[4,128]{1,0:T(4,128)(2,1)} %bitcast.107, bf16[12,128]{1,0:T(8,128)(2,1)} %bitcast.99, bf16[4,128]{1,0:T(4,128)(2,1)} %bitcast.108, bf16[16,128]{1,0:T(8,128)(2,1)} %bitcast.98, ...), dimensions={0} | concatenate | bytes 26624 | tf_op jit(solution)/shard_map/concatenate | solution.py:1867
  10.0 1.1 copy-done
  11.1 38.6 %enter.1 = (bf16[8,256,1024]{2,1,0:T(8,128)(2,1)}, s32[4,8,128]{2,1,0:T(8,128)S(1)}, f32[2,52,128]{2,1,0:T(8,128)S(1)}, bf16[2,512,384]{2,1,0:T(8,128)(2,1)S(1)}...) custom-call(bf16[256,1024]{1,0:T(8,128)(2,1)S(1)} %bitcast.75, s32[8,128]{1,0:T(8,128)S(1)} %broadcast_in_dim.75.ints, ...), custom_call_target="tpu_custom_call" | custom-call | tf_op jit(solution)/shard_map/enter/pallas_call | solution.py:690
  49.8 1.1 copy-done.5
  50.9 0.9 copy-done.6
  51.9 0.6 pad_maximum_fusion.vectors
  52.5 54.5 %feed_forward.1 = (bf16[4,4,512,128]{3,2,1,0:T(8,128)(2,1)}, bf16[8,256,1024]{2,1,0:T(8,128)(2,1)}, bf16[2,512,512]{2,1,0:T(8,128)(2,1)}, bf16[2048,512]{1,0:T(8...) custom-call(bf16[3,2048,128]{2,1,0:T(8,128)(2,1)} %copy-done.5, ...), custom_call_target="tpu_custom_call" | custom-call | tf_op jit(solution)/shard_map/feed_forward/pallas_call | solution.py:884
  107.1 1.6 copy-done.4
  108.7 0.7 sort_units.1
  109.3 1.3 copy-done.2
  110.7 200.9 %middle.1 = (bf16[2,2,512,2048]{3,2,1,0:T(8,128)(2,1)}, bf16[2,2,544,1024]{3,2,1,0:T(8,128)(2,1)}, f32[256,1024]{1,0:T(8,128)}, f32[256,1024]{1,0:T(8,128)}) custom-call(s32[1,128]{1,0:T(1,128)} %copy-done.11, bf16[4,2048,128]{2,1,0:T(8,128)(2,1)} %bitcast.76, f32[16,128]{1,0:T(8,128)} %copy-done.10, f32[16,128]{1,0:T(8,128)} %copy-done.9, ...), custom_call_target="tpu_custom_call" | custom-call | tf_op jit(solution)/shard_map/middle/pallas_call | solution.py:1693
  311.6 1.6 fusion.23
  313.2 3.1 fusion.8
  316.3 1.0 slice_convert_fusion
  317.6 0.7 dynamic_slice.49
  318.4 0.6 constant_dynamic-slice_fusion
  319.0 0.6 constant_dynamic-slice_fusion.2
  319.6 0.6 dynamic_slice.51
  320.2 2.3 copy-done.3
  322.4 10.5 %widen.1 = (f32[512,4096]{1,0:T(8,128)}, f32[2048,1024]{1,0:T(8,128)}, f32[512,3072]{1,0:T(8,128)}, f32[512,1024]{1,0:T(8,128)}) custom-call(bf16[2,2,512,2048]{3,2,1,0:T(8,128)(2,1)} %get-tuple-element.51.feed_all, bf16[2,2,544,1024]{3,2,1,0:T(8,128)(2,1)S(1)} %copy-done.3), custom_call_target="tpu_custom_call" | custom-call | tf_op jit(solution)/shard_map/widen/pallas_call | solution.py:1805
  (59 shorter events, 1.6 us)
Async XLA Ops:
  9.7 97.3 %copy-start.9 = (f32[16,128]{1,0:T(8,128)}, f32[16,128]{1,0:T(8,128)S(1)}, u32[]{:S(2)}) copy-start(f32[16,128]{1,0:T(8,128)S(1)} %get-tuple-element.71.unit_sin) | copy-start | bytes 24580
  9.7 97.3 %copy-start.10 = (f32[16,128]{1,0:T(8,128)}, f32[16,128]{1,0:T(8,128)S(1)}, u32[]{:S(2)}) copy-start(f32[16,128]{1,0:T(8,128)S(1)} %get-tuple-element.72.unit_cos) | copy-start | bytes 24580
  10.0 97.0 %copy-start.7 = (f32[128,128]{1,0:T(8,128)}, f32[128,128]{1,0:T(8,128)S(1)}, u32[]{:S(2)}) copy-start(f32[128,128]{1,0:T(8,128)S(1)} %get-tuple-element.69.row_sin) | copy-start | bytes 196612
  10.0 97.0 %copy-start.8 = (f32[128,128]{1,0:T(8,128)}, f32[128,128]{1,0:T(8,128)S(1)}, u32[]{:S(2)}) copy-start(f32[128,128]{1,0:T(8,128)S(1)} %get-tuple-element.70.row_cos) | copy-start | bytes 196612
  10.0 1.1 copy-start
  49.8 1.1 copy-start.5
  50.9 0.9 copy-start.6
  51.8 55.2 %copy-start.11 = (s32[1,128]{1,0:T(1,128)}, s32[1,128]{1,0:T(1,128)S(1)}, u32[]{:S(2)}) copy-start(s32[1,128]{1,0:T(1,128)S(1)} %fusion.18.order.ints) | copy-start | bytes 1540
  107.1 1.6 copy-start.4
  109.3 1.3 copy-start.2
  110.7 200.9 %copy-start.1 = (bf16[1,256,1024]{2,1,0:T(8,128)(2,1)S(1)}, bf16[1,256,1024]{2,1,0:T(8,128)(2,1)}, u32[]{:S(2)}) copy-start(bf16[1,256,1024]{2,1,0:T(8,128)(2,1)} %param.16) | copy-start | bytes 1572868
  110.7 202.5 %copy-start.12 = (bf16[1,256,1024]{2,1,0:T(8,128)(2,1)S(1)}, bf16[1,256,1024]{2,1,0:T(8,128)(2,1)}, u32[]{:S(2)}) copy-start(bf16[1,256,1024]{2,1,0:T(8,128)(2,1)} %param.31) | copy-start | bytes 1572868
  317.6 15.4 %copy-start.13 = (f32[512]{0:T(512)}, f32[512]{0:T(512)S(1)}, u32[]{:S(2)}) copy-start(f32[512]{0:T(512)S(1)} %dynamic_slice.50) | copy-start | bytes 6148
  320.2 2.3 copy-start.3
